TPU v7x, 128 devices: a whole 4x4x4 slice. The times are simulated.
128 devices in a mesh: ctx: 32 (over y, x, core), dp: 4 (over z).
Axes of the slice: x: 4, y: 4, z: 4, core: 2. Of those that a mesh axis runs over, the one named last changes fastest.
Arguments:
- query: bfloat16 [4, 6144, 4096], P('dp', 'ctx'), may hold values from -6 to 6
- key_value: bfloat16 [4, 6144, 1024], P('dp', 'ctx'), may hold values from -6 to 6
- upstream: bfloat16 [4, 6144, 4096], P('dp', 'ctx'), may hold values from -6 to 6
- log_ratio: float32 [4, 6144], P('dp', 'ctx'), may hold values from -4 to 1
- doc_starts: int32 [4, 64], P('dp'), may hold values from 0 to 6144, as said below
- answer_counts: int32 [4, 64], P('dp'), may hold values from 0 to 768, as said below
Outputs:
- d_query: bfloat16 [4, 6144, 4096], P('dp', 'ctx')
- d_key_value: bfloat16 [4, 6144, 1024], P('dp', 'ctx')
Inputs may be any that keep to these rules, and one draw needn't show every extreme that they name: `doc_starts`: used slots come first; each sequence's documents start at the listed positions in rising order, the first at 0, together covering all 6144 positions; unused slots hold 6144; every document has 96 to 768 positions, and every sequence has a document of exactly 768 positions. A document's answer positions are its last answer_counts positions; a used slot holds half of the document's length (rounded down) up to all of it, an unused slot 0; every sequence has a document of 768 positions that are all answer positions.
All inputs are finite; a program needn't handle non-finite values.
Results may differ from a plain program's by a relative error of at most 0.011.
Values may be sent and summed in bfloat16 or wider, within the bound.
No kernel may reach another device: no remote copies, remote signals or barrier semaphores. Data moves between devices by JAX's collectives and lax.ppermute only.
A program may use at most 64 MiB of HBM per device.

v0:
```python
from functools import partial

import jax
import jax.numpy as jnp
from jax import lax
from jax.sharding import PartitionSpec as P

HQ = 32
HK = 4
DH = 128
SPAN = 4
LOSS_SCALE = 65536


def passed_along(value, axis, steps):
    count = lax.axis_size(axis)
    first, last = (max(0, -steps), min(count, count - steps))
    return lax.ppermute(value, axis, [(source, source + steps) for source in range(first, last)])


def doc_index(starts, positions):
    return jnp.sum((starts[None, :] <= positions[:, None]).astype(jnp.int32), axis=1) - 1


def head_block(visible, blocks):
    query_head, out_grad, key_head, value_head = blocks
    score_scale = DH ** (-0.5)
    scores = (
        jnp.einsum("tgd,kd->gtk", query_head, key_head, preferred_element_type=jnp.float32)
        * score_scale
    )
    scores = jnp.where(visible[None], scores, -1e30)
    row_max = jnp.max(scores, axis=2, keepdims=True)
    row_total = jnp.sum(jnp.exp(scores - row_max), axis=2, keepdims=True)
    prob_full = jnp.exp(scores - (row_max + jnp.log(row_total)))
    prob_low = prob_full.astype(jnp.bfloat16)
    attended = jnp.einsum("gtk,kd->tgd", prob_low, value_head, preferred_element_type=jnp.float32)
    row_delta = jnp.sum(out_grad.astype(jnp.float32) * attended, axis=2)
    d_probs = jnp.einsum("tgd,kd->gtk", out_grad, value_head, preferred_element_type=jnp.float32)
    d_scores = (prob_full * (d_probs - jnp.transpose(row_delta)[:, :, None])).astype(jnp.bfloat16)
    query_grad = (
        jnp.einsum("gtk,kd->tgd", d_scores, key_head, preferred_element_type=jnp.float32)
        * score_scale
    )
    key_grad = (
        jnp.einsum("gtk,tgd->kd", d_scores, query_head, preferred_element_type=jnp.float32)
        * score_scale
    )
    value_grad = jnp.einsum("gtk,tgd->kd", prob_low, out_grad, preferred_element_type=jnp.float32)
    return (query_grad, key_grad, value_grad)


def local(query, key_value, upstream, log_ratio, doc_starts, answer_counts):
    shard_len = query.shape[1]
    kv_width = key_value.shape[2]
    slot_count = doc_starts.shape[1]
    group_size = HQ // HK
    shard_index = lax.axis_index("ctx")
    seq_len = shard_len * lax.axis_size("ctx")
    starts = doc_starts[0]
    counts = answer_counts[0]
    doc_ends = jnp.concatenate([starts[1:], jnp.full((1,), seq_len, jnp.int32)])
    positions = shard_index * shard_len + jnp.arange(shard_len, dtype=jnp.int32)
    doc_here = doc_index(starts, positions)
    in_doc = doc_here[:, None] == jnp.arange(slot_count, dtype=jnp.int32)[None, :]
    end_here = jnp.sum(jnp.where(in_doc, doc_ends[None, :], 0), axis=1)
    count_here = jnp.sum(jnp.where(in_doc, counts[None, :], 0), axis=1)
    answer = positions >= end_here - count_here
    picked = in_doc & answer[:, None]
    partial_sum = jnp.sum(jnp.where(picked, log_ratio[0][:, None], 0.0), axis=0)
    doc_sum = lax.psum(partial_sum, "ctx")
    total_docs = lax.psum(jnp.sum((counts > 0).astype(jnp.float32)), "dp")
    floored = jnp.maximum(counts, 1).astype(jnp.float32)
    doc_coef = LOSS_SCALE * 2.0 * jax.nn.sigmoid(doc_sum / floored) / (floored * total_docs)
    weight = jnp.sum(jnp.where(picked, doc_coef[None, :], 0.0), axis=1)
    out_grad = (weight[:, None] * upstream[0].astype(jnp.float32)).astype(jnp.bfloat16)
    local_kv = key_value[0]
    earlier = [passed_along(local_kv, "ctx", distance) for distance in range(SPAN, 0, -1)]
    keys_all = jnp.concatenate(earlier + [local_kv], axis=0)
    key_pos = (shard_index - SPAN) * shard_len + jnp.arange((SPAN + 1) * shard_len, dtype=jnp.int32)
    doc_keys = doc_index(starts, key_pos)
    visible = (doc_here[:, None] == doc_keys[None, :]) & (key_pos[None, :] <= positions[:, None])
    query_heads = query[0].reshape(shard_len, HK, group_size, DH).transpose(1, 0, 2, 3)
    grad_heads = out_grad.reshape(shard_len, HK, group_size, DH).transpose(1, 0, 2, 3)
    key_heads = keys_all[:, : HK * DH].reshape(-1, HK, DH).transpose(1, 0, 2)
    value_heads = keys_all[:, HK * DH :].reshape(-1, HK, DH).transpose(1, 0, 2)
    query_grad, key_grad, value_grad = lax.map(
        partial(head_block, visible), (query_heads, grad_heads, key_heads, value_heads)
    )
    d_query = query_grad.transpose(1, 0, 2, 3).reshape(shard_len, HQ * DH).astype(jnp.bfloat16)
    kv_grad = jnp.concatenate(
        [
            key_grad.transpose(1, 0, 2).reshape(-1, HK * DH),
            value_grad.transpose(1, 0, 2).reshape(-1, HK * DH),
        ],
        axis=1,
    )
    key_pieces = kv_grad.reshape(SPAN + 1, shard_len, kv_width)
    summed = key_pieces[SPAN]
    for distance in range(1, SPAN + 1):
        summed = summed + passed_along(key_pieces[SPAN - distance], "ctx", -distance)
    return (d_query[None], summed.astype(jnp.bfloat16)[None])


def solution(mesh):
    return jax.shard_map(
        local,
        mesh=mesh,
        in_specs=(
            P("dp", "ctx", None),
            P("dp", "ctx", None),
            P("dp", "ctx", None),
            P("dp", "ctx"),
            P("dp", None),
            P("dp", None),
        ),
        out_specs=(P("dp", "ctx", None), P("dp", "ctx", None)),
        check_vma=False,
    )
```

profile of v0, /device:TPU:17, one launch (start us, length us, event | category | flops | bytes accessed | tf_op | source)
XLA Modules:
  0.0 243.0 jit_solution(8716191067880232477)
XLA Ops:
  0.6 4.7 %collective-permute-start = (bf16[192,1024]{1,0:T(8,128)(2,1)}, bf16[192,1024]{1,0:T(8,128)(2,1)}, u32[]{:S(2)}, u32[]{:S(2)}) collective-permute-start(bf16[192,1024]{1,0:T(8,128)(2,1)} %bitcast.170), channel_id=1, source_target_pairs={{0,16},{4,20},{8,24},{12,28},{16,32},{20,36},{24,40},{28,44},{32,4... | collective-permute-start | bytes 1179656 | tf_op jit(solution)/shard_map/ppermute | solution.py:18
  5.3 3.7 %collective-permute-start.1 = (bf16[192,1024]{1,0:T(8,128)(2,1)}, bf16[192,1024]{1,0:T(8,128)(2,1)}, u32[]{:S(2)}, u32[]{:S(2)}) collective-permute-start(bf16[192,1024]{1,0:T(8,128)(2,1)} %bitcast.171), channel_id=1, source_target_pairs={{0,12},{4,16},{8,20},{12,24},{16,28},{20,32},{24,36},{28,40},{32,4... | collective-permute-start | bytes 1179656 | tf_op jit(solution)/shard_map/ppermute | solution.py:18
  9.0 3.1 %collective-permute-start.2 = (bf16[192,1024]{1,0:T(8,128)(2,1)}, bf16[192,1024]{1,0:T(8,128)(2,1)}, u32[]{:S(2)}, u32[]{:S(2)}) collective-permute-start(bf16[192,1024]{1,0:T(8,128)(2,1)} %bitcast.172), channel_id=1, source_target_pairs={{0,8},{4,12},{8,16},{12,20},{16,24},{20,28},{24,32},{28,36},{32,40... | collective-permute-start | bytes 1179656 | tf_op jit(solution)/shard_map/ppermute | solution.py:18
  12.1 1.9 collective-permute-start.3
  18.5 65.2 %psum.14 = f32[64]{0:T(128)S(1)} all-reduce(f32[64]{0:T(128)S(1)} %select_reduce_fusion.1), channel_id=1, replica_groups=mesh['ctx'=32,'dp'=4] {'ctx'}, use_global_device_ids=true, to_apply=%region_4.5 | all-reduce | flops 64 | bytes 512 | tf_op jit(solution)/shard_map/psum | solution.py:71
  83.7 10.4 %psum.15 = f32[]{:T(128)} all-reduce(f32[]{:T(128)} %fusion.36), channel_id=1, replica_groups=mesh['ctx'=32,'dp'=4] {'dp'}, use_global_device_ids=true, to_apply=%region_6.7 | all-reduce | flops 1 | bytes 8 | tf_op jit(solution)/shard_map/psum | solution.py:72
  106.6 1.9 reshape.91
  109.6 60.3 %while.15 = (s32[]{:T(128)}, bf16[4,192,8,128]{3,1,2,0:T(8,128)(2,1)}, f32[4,960,128]{2,1,0:T(8,128)}, f32[4,960,128]{2,1,0:T(8,128)}, bf16[4,960,128]{2,1,0:T(8...) while((s32[]{:T(128)}, ...), condition=%wide.region_13.14_spmd.clone, body=%wide.region_9.13_spmd.clone.sunk | while | flops 2297349120 | bytes 50773160 | solution.py:87
  112.3 1.8 exponential_reduce_fusion.2
  114.1 2.7 %fusion.68 = f32[4,960,128]{2,1,0:T(8,128)} fusion(f32[4,960,128]{2,1,0:T(8,128)} %get-tuple-element.241, s32[]{:T(128)} %get-tuple-element.238, bf16[1,192,8,128]{3,2,0,1:T(8,128)(2,1)S(1)} %get-tuple-element.223, f32[960,192,8]{0,1,2:T(8,128)S(1)} %get-tuple-element.222, f32[8,192]{1,0:T(8,128)S(1)} %log_add_fusion.2, ...), kind=kOutput, calls=%fused_computation.15.clone.1 | convolution fusion | flops 383385600 | bytes 6973952 | tf_op jit(solution)/shard_map/while/body/eval_jaxpr/gtk,tgd->kd/dot_general | solution.py:49
  116.8 1.9 fusion.64
  118.7 2.4 fusion.65
  127.3 1.8 exponential_reduce_fusion.2
  129.2 2.7 %fusion.68 = f32[4,960,128]{2,1,0:T(8,128)} fusion(f32[4,960,128]{2,1,0:T(8,128)} %get-tuple-element.241, s32[]{:T(128)} %get-tuple-element.238, bf16[1,192,8,128]{3,2,0,1:T(8,128)(2,1)S(1)} %get-tuple-element.223, f32[960,192,8]{0,1,2:T(8,128)S(1)} %get-tuple-element.222, f32[8,192]{1,0:T(8,128)S(1)} %log_add_fusion.2, ...), kind=kOutput, calls=%fused_computation.15.clone.1 | convolution fusion | flops 383385600 | bytes 6973952 | tf_op jit(solution)/shard_map/while/body/eval_jaxpr/gtk,tgd->kd/dot_general | solution.py:49
  131.9 1.9 fusion.64
  133.8 2.4 fusion.65
  144.3 2.7 %fusion.68 = f32[4,960,128]{2,1,0:T(8,128)} fusion(f32[4,960,128]{2,1,0:T(8,128)} %get-tuple-element.241, s32[]{:T(128)} %get-tuple-element.238, bf16[1,192,8,128]{3,2,0,1:T(8,128)(2,1)S(1)} %get-tuple-element.223, f32[960,192,8]{0,1,2:T(8,128)S(1)} %get-tuple-element.222, f32[8,192]{1,0:T(8,128)S(1)} %log_add_fusion.2, ...), kind=kOutput, calls=%fused_computation.15.clone.1 | convolution fusion | flops 383385600 | bytes 6973952 | tf_op jit(solution)/shard_map/while/body/eval_jaxpr/gtk,tgd->kd/dot_general | solution.py:49
  147.0 1.9 fusion.64
  148.9 2.4 fusion.65
  159.4 2.7 %fusion.68 = f32[4,960,128]{2,1,0:T(8,128)} fusion(f32[4,960,128]{2,1,0:T(8,128)} %get-tuple-element.241, s32[]{:T(128)} %get-tuple-element.238, bf16[1,192,8,128]{3,2,0,1:T(8,128)(2,1)S(1)} %get-tuple-element.223, f32[960,192,8]{0,1,2:T(8,128)S(1)} %get-tuple-element.222, f32[8,192]{1,0:T(8,128)S(1)} %log_add_fusion.2, ...), kind=kOutput, calls=%fused_computation.15.clone.1 | convolution fusion | flops 383385600 | bytes 6973952 | tf_op jit(solution)/shard_map/while/body/eval_jaxpr/gtk,tgd->kd/dot_general | solution.py:49
  162.1 1.9 fusion.64
  164.0 2.4 fusion.65
  171.7 1.8 bitcast_dynamic-update-slice_fusion
  175.9 4.1 %collective-permute-start.4 = (f32[192,1024]{1,0:T(8,128)}, f32[192,1024]{1,0:T(8,128)}, u32[]{:S(2)}, u32[]{:S(2)}) collective-permute-start(f32[192,1024]{1,0:T(8,128)} %get-tuple-element.138), channel_id=1, source_target_pairs={{4,0},{8,4},{12,8},{16,12},{20,16},{24,20},{28,24},{32,28},{36,32}... | collective-permute-start | bytes 2359304 | tf_op jit(solution)/shard_map/ppermute | solution.py:18
  180.0 1.9 collective-permute-start.5
  181.9 1.9 collective-permute-start.6
  183.9 5.2 %collective-permute-start.7 = (f32[192,1024]{1,0:T(8,128)S(1)}, f32[192,1024]{1,0:T(8,128)}, u32[]{:S(2)}, u32[]{:S(2)}) collective-permute-start(f32[192,1024]{1,0:T(8,128)S(1)} %get-tuple-element.139), channel_id=1, source_target_pairs={{16,0},{20,4},{24,8},{28,12},{32,16},{36,20},{40,24},{44,28},{48,3... | collective-permute-start | bytes 2359304 | tf_op jit(solution)/shard_map/ppermute | solution.py:18
  189.1 2.4 copy.22
  191.5 2.1 convert_element_type.60
  194.4 7.4 %collective-permute-done.5 = f32[192,1024]{1,0:T(8,128)} collective-permute-done((f32[192,1024]{1,0:T(8,128)}, f32[192,1024]{1,0:T(8,128)}, u32[]{:S(2)}, u32[]{:S(2)}) %collective-permute-start.5) | collective-permute-done | bytes 786464 | tf_op jit(solution)/shard_map/ppermute | solution.py:18
  201.8 38.1 %collective-permute-done.6 = f32[192,1024]{1,0:T(8,128)} collective-permute-done((f32[192,1024]{1,0:T(8,128)S(1)}, f32[192,1024]{1,0:T(8,128)}, u32[]{:S(2)}, u32[]{:S(2)}) %collective-permute-start.6) | collective-permute-done | bytes 786464 | tf_op jit(solution)/shard_map/ppermute | solution.py:18
  239.9 3.1 %fusion.34 = bf16[1,192,1024]{2,1,0:T(8,128)(2,1)} fusion(f32[192,1024]{1,0:T(8,128)} %collective-permute-done.7, f32[192,1024]{1,0:T(8,128)} %collective-permute-done.6, f32[192,1024]{1,0:T(8,128)} %collective-permute-done.5, f32[192,1024]{1,0:T(8,128)} %collective-permute-done.4, f32[960,1024]{1,0:T(8,128)} %copy-done), kind=kLoop, calls=%fused_computation.51 | loop fusion | flops 983040 | bytes 4325376 | tf_op jit(solution)/shard_map/broadcast_in_dim | solution.py:102
  (76 shorter events, 51.4 us)
Async XLA Ops:
  0.6 101.2 %collective-permute-start = (bf16[192,1024]{1,0:T(8,128)(2,1)}, bf16[192,1024]{1,0:T(8,128)(2,1)}, u32[]{:S(2)}, u32[]{:S(2)}) collective-permute-start(bf16[192,1024]{1,0:T(8,128)(2,1)} %bitcast.170), channel_id=1, source_target_pairs={{0,16},{4,20},{8,24},{12,28},{16,32},{20,36},{24,40},{28,44},{32,4... | collective-permute-start | bytes 1179656 | tf_op jit(solution)/shard_map/ppermute | solution.py:18
  5.3 97.6 %collective-permute-start.1 = (bf16[192,1024]{1,0:T(8,128)(2,1)}, bf16[192,1024]{1,0:T(8,128)(2,1)}, u32[]{:S(2)}, u32[]{:S(2)}) collective-permute-start(bf16[192,1024]{1,0:T(8,128)(2,1)} %bitcast.171), channel_id=1, source_target_pairs={{0,12},{4,16},{8,20},{12,24},{16,28},{20,32},{24,36},{28,40},{32,4... | collective-permute-start | bytes 1179656 | tf_op jit(solution)/shard_map/ppermute | solution.py:18
  9.0 95.0 %collective-permute-start.2 = (bf16[192,1024]{1,0:T(8,128)(2,1)}, bf16[192,1024]{1,0:T(8,128)(2,1)}, u32[]{:S(2)}, u32[]{:S(2)}) collective-permute-start(bf16[192,1024]{1,0:T(8,128)(2,1)} %bitcast.172), channel_id=1, source_target_pairs={{0,8},{4,12},{8,16},{12,20},{16,24},{20,28},{24,32},{28,36},{32,40... | collective-permute-start | bytes 1179656 | tf_op jit(solution)/shard_map/ppermute | solution.py:18
  12.1 92.9 %collective-permute-start.3 = (bf16[192,1024]{1,0:T(8,128)(2,1)}, bf16[192,1024]{1,0:T(8,128)(2,1)S(1)}, u32[]{:S(2)}, u32[]{:S(2)}) collective-permute-start(bf16[192,1024]{1,0:T(8,128)(2,1)} %bitcast.173), channel_id=1, source_target_pairs={{0,4},{4,8},{8,12},{12,16},{16,20},{20,24},{24,28},{28,32},{32,36}... | collective-permute-start | bytes 1179656 | tf_op jit(solution)/shard_map/ppermute | solution.py:18
  100.1 5.0 %copy-start.2 = (bf16[1,192,1024]{2,1,0:T(8,128)(2,1)S(1)}, bf16[1,192,1024]{2,1,0:T(8,128)(2,1)}, u32[]{:S(2)}) copy-start(bf16[1,192,1024]{2,1,0:T(8,128)(2,1)} %param.9) | copy-start | bytes 1179652
  114.1 2.7 %copy-start.1 = (bf16[4,960,128]{2,1,0:T(8,128)(2,1)S(1)}, bf16[4,960,128]{2,1,0:T(8,128)(2,1)}, u32[]{:S(2)}) copy-start(bf16[4,960,128]{2,1,0:T(8,128)(2,1)} %get-tuple-element.257) | copy-start | bytes 2949124 | tf_op jit(solution)/shard_map/while
  129.2 2.7 %copy-start.1 = (bf16[4,960,128]{2,1,0:T(8,128)(2,1)S(1)}, bf16[4,960,128]{2,1,0:T(8,128)(2,1)}, u32[]{:S(2)}) copy-start(bf16[4,960,128]{2,1,0:T(8,128)(2,1)} %get-tuple-element.257) | copy-start | bytes 2949124 | tf_op jit(solution)/shard_map/while
  144.3 2.7 %copy-start.1 = (bf16[4,960,128]{2,1,0:T(8,128)(2,1)S(1)}, bf16[4,960,128]{2,1,0:T(8,128)(2,1)}, u32[]{:S(2)}) copy-start(bf16[4,960,128]{2,1,0:T(8,128)(2,1)} %get-tuple-element.257) | copy-start | bytes 2949124 | tf_op jit(solution)/shard_map/while
  159.4 2.7 %copy-start.1 = (bf16[4,960,128]{2,1,0:T(8,128)(2,1)S(1)}, bf16[4,960,128]{2,1,0:T(8,128)(2,1)}, u32[]{:S(2)}) copy-start(bf16[4,960,128]{2,1,0:T(8,128)(2,1)} %get-tuple-element.257) | copy-start | bytes 2949124 | tf_op jit(solution)/shard_map/while
  173.5 2.4 copy-start
  175.9 18.5 %collective-permute-start.4 = (f32[192,1024]{1,0:T(8,128)}, f32[192,1024]{1,0:T(8,128)}, u32[]{:S(2)}, u32[]{:S(2)}) collective-permute-start(f32[192,1024]{1,0:T(8,128)} %get-tuple-element.138), channel_id=1, source_target_pairs={{4,0},{8,4},{12,8},{16,12},{20,16},{24,20},{28,24},{32,28},{36,32}... | collective-permute-start | bytes 2359304 | tf_op jit(solution)/shard_map/ppermute | solution.py:18
  180.0 21.8 %collective-permute-start.5 = (f32[192,1024]{1,0:T(8,128)}, f32[192,1024]{1,0:T(8,128)}, u32[]{:S(2)}, u32[]{:S(2)}) collective-permute-start(f32[192,1024]{1,0:T(8,128)} %get-tuple-element.141), channel_id=1, source_target_pairs={{8,0},{12,4},{16,8},{20,12},{24,16},{28,20},{32,24},{36,28},{40,32... | collective-permute-start | bytes 2359304 | tf_op jit(solution)/shard_map/ppermute | solution.py:18
  181.9 57.9 %collective-permute-start.6 = (f32[192,1024]{1,0:T(8,128)S(1)}, f32[192,1024]{1,0:T(8,128)}, u32[]{:S(2)}, u32[]{:S(2)}) collective-permute-start(f32[192,1024]{1,0:T(8,128)S(1)} %get-tuple-element.140), channel_id=1, source_target_pairs={{12,0},{16,4},{20,8},{24,12},{28,16},{32,20},{36,24},{40,28},{44,3... | collective-permute-start | bytes 2359304 | tf_op jit(solution)/shard_map/ppermute | solution.py:18
  183.9 56.0 %collective-permute-start.7 = (f32[192,1024]{1,0:T(8,128)S(1)}, f32[192,1024]{1,0:T(8,128)}, u32[]{:S(2)}, u32[]{:S(2)}) collective-permute-start(f32[192,1024]{1,0:T(8,128)S(1)} %get-tuple-element.139), channel_id=1, source_target_pairs={{16,0},{20,4},{24,8},{28,12},{32,16},{36,20},{40,24},{44,28},{48,3... | collective-permute-start | bytes 2359304 | tf_op jit(solution)/shard_map/ppermute | solution.py:18
where the time goes:
time: 246 us; the launch traced here: 243 us
  blocking collectives  75.6 us (31%)
  matrix products  47.7 us (19%)
  waiting for transfers between devices  46.3 us (19%)
  starting transfers between devices  26.5 us (11%)
  local copies, waits for them, and re-layouts  25.5 us (10%)
  other arithmetic  20.4 us (8%)
    psum x1, blocking collectives, local(): doc_sum = lax.psum(partial_sum, 'ctx')  65.2 us
    ppermute x8, waiting for transfers between devices, passed_along(): lax.ppermute(value, axis, [(source, source + steps) for source in range(f...  46.3 us
    ppermute x8, starting transfers between devices, passed_along(): lax.ppermute(value, axis, [(source, source + steps) for source in range(f...  26.5 us
    dot_general x4, matrix products, head_block(): jnp.einsum('gtk,tgd->kd', prob_low, out_grad, preferred_element_type=jnp....  10.8 us
    psum x1, blocking collectives, local(): total_docs = lax.psum(jnp.sum((counts > 0).astype(jnp.float32)), 'dp')  10.4 us
    dot_general x4, matrix products, head_block(): jnp.einsum('tgd,kd->gtk', out_grad, value_head, preferred_element_type=jn...  9.58 us
    unnamed x13, local copies, waits for them, and re-layouts  9.31 us
    dot_general x4, matrix products, head_block(): jnp.einsum('gtk,kd->tgd', prob_low, value_head, preferred_element_type=jn...  7.65 us
  transfers between devices with their start and end apart: 8, of which 3 were waited for; matrix products, arithmetic and copies ran while one was open for 8% of the time, Pallas kernels for 0%

commit v1 on v0

v1 whole, which is shorter than its diff:
```python
from functools import partial

import jax
import jax.numpy as jnp
from jax import lax
from jax.experimental import pallas as pl
from jax.experimental.pallas import tpu as pltpu
from jax.sharding import PartitionSpec as P

HQ = 32
HK = 4
DH = 128
LOSS_SCALE = 65536
ROWS = 192
CHIP = 2 * ROWS
WIN = 3 * CHIP
GROUP = HQ // HK
SUB = 96
LANES = SUB * GROUP
SPANS = (256, 512, 640, 784, 896)
CHUNKS = 2
TAIL = 16
PACK = CHIP + 2 * TAIL
MASKED = -1e30
SCALE = DH ** (-0.5)
LOG2E = 1.4426950408889634
F32 = jnp.float32
BF16 = jnp.bfloat16


def to_column(row, shift=0):
    n = row.shape[1]
    r = lax.broadcasted_iota(jnp.int32, (n, n), 0)
    c = lax.broadcasted_iota(jnp.int32, (n, n), 1)
    return jnp.sum(jnp.where(c == r + shift, row, 0), axis=1, keepdims=True)


def end_row(starts, seq_len):
    n = starts.shape[1]
    r = lax.broadcasted_iota(jnp.int32, (n, n), 0)
    c = lax.broadcasted_iota(jnp.int32, (n, n), 1)
    col = to_column(starts)
    row = jnp.sum(jnp.where(r == c + 1, col, 0), axis=0, keepdims=True)
    lane = lax.broadcasted_iota(jnp.int32, (1, n), 1)
    return jnp.where(lane == n - 1, seq_len, row)


def prep_kernel(seq_len, idx_ref, kv_ref, lr_ref, st_ref, ct_ref, snd_ref, mine_ref):
    index = idx_ref[0]
    core = index % 2

    def put(dst, half):
        for j in range(CHUNKS):
            lo = half * CHUNKS * DH + j * DH
            dst[0:ROWS, 2 * j * DH : (2 * j + 1) * DH] = kv_ref[:, lo : lo + DH]
            dst[0:ROWS, (2 * j + 1) * DH : (2 * j + 2) * DH] = kv_ref[:, HK * DH + lo : HK * DH + lo + DH]

    for half in range(2):

        @pl.when(core == half)
        def _():
            put(mine_ref, half)
            put(snd_ref, 1 - half)

    starts = st_ref[...]
    n = starts.shape[1]
    row_i = lax.broadcasted_iota(jnp.int32, (n, 1), 0)
    st = to_column(starts)
    en = jnp.where(row_i == n - 1, seq_len, to_column(starts, 1))
    first = jnp.maximum(st, en - to_column(ct_ref[...]))
    pos = index * ROWS + lax.broadcasted_iota(jnp.int32, (n, ROWS), 1)
    part = jnp.sum(jnp.where((pos >= first) & (pos < en), lr_ref[...], 0.0), axis=1, keepdims=True)
    r = lax.broadcasted_iota(jnp.int32, (n, n), 0)
    c = lax.broadcasted_iota(jnp.int32, (n, n), 1)
    part = jnp.sum(jnp.where(r == c, part, 0.0), axis=0, keepdims=True)
    high = part.astype(BF16).astype(F32)
    rest = part - high
    mid = rest.astype(BF16).astype(F32)
    low = rest - mid
    k = lax.broadcasted_iota(jnp.int32, (TAIL, n), 0)
    tail = jnp.where(k == 0, high, jnp.where(k == 1, mid, jnp.where(k == 2, low, 0.0))).astype(BF16)
    for dst in (snd_ref, mine_ref):
        dst[ROWS : ROWS + TAIL, :] = jnp.zeros((TAIL, 2 * CHUNKS * DH), BF16)
        dst[ROWS : ROWS + TAIL, 0:n] = tail


def scalar_kernel(idx_ref, st_ref, ct_ref, sc_ref, cnt_ref):
    index = idx_ref[0]
    first = index // 2 * CHIP
    base = first - (WIN - CHIP)
    sc_ref[0] = index % 2
    sc_ref[1] = base
    n = st_ref.shape[0]

    def each(j, carry):
        lows = list(carry[:-1])
        start = st_ref[j]
        for s in range(CHIP // SUB):
            lows[s] = jnp.where(start <= first + s * SUB, start, lows[s])
        return (*lows, carry[-1] + (ct_ref[j] > 0).astype(jnp.int32))

    out = lax.fori_loop(0, n, each, (jnp.int32(0),) * (CHIP // SUB + 1))
    for s in range(CHIP // SUB):
        low = jnp.maximum(out[s] - base, 0) // 16 * 16
        need = (WIN - CHIP) + (s + 1) * SUB - low
        pick = jnp.int32(0)
        span = jnp.int32(SPANS[0])
        for v in range(1, len(SPANS)):
            more = need > SPANS[v - 1]
            pick = jnp.where(more, v, pick)
            span = jnp.where(more, SPANS[v], span)
        sc_ref[2 + 2 * s] = jnp.minimum(low, WIN - span)
        sc_ref[3 + 2 * s] = pick
    cnt_ref[...] = jnp.full(cnt_ref.shape, out[-1].astype(F32))


def nt(a, b):
    return lax.dot_general(a, b, (((1,), (1,)), ((), ())), preferred_element_type=F32)


def nn(a, b):
    return lax.dot_general(a, b, (((1,), (0,)), ((), ())), preferred_element_type=F32)


def tn(a, b):
    return lax.dot_general(a, b, (((0,), (0,)), ((), ())), preferred_element_type=F32)


def fold(x, op):
    out = x[0:8]
    for i in range(8, x.shape[0], 8):
        out = op(out, x[i : i + 8])
    return out


def attention_kernel(
    seq_len,
    sc_ref,
    q_ref,
    g_ref,
    qg_ref,
    own_ref,
    a_ref,
    b_ref,
    st_ref,
    ct_ref,
    dq_own_ref,
    dq_other_ref,
    d_own_ref,
    d_a_ref,
    d_b_ref,
    q_all,
    g_all,
    k_all,
    v_all,
    q_now,
    g_now,
    s_buf,
    d_buf,
    k_acc,
    v_acc,
    dq_all,
):
    core = sc_ref[0]
    base = sc_ref[1]
    mine = pl.multiple_of(core * ROWS, ROWS)
    other = pl.multiple_of((1 - core) * ROWS, ROWS)
    starts = st_ref[...]
    n = starts.shape[1]
    ends = end_row(starts, seq_len)
    first_answer = jnp.maximum(starts, ends - ct_ref[...])

    def answers(offset):
        pos = base + (WIN - CHIP) + offset + lax.broadcasted_iota(jnp.int32, (ROWS, n), 0)
        hit = jnp.where((pos >= first_answer) & (pos < ends), 1.0, 0.0)
        return jnp.sum(hit, axis=1, keepdims=True) > 0.5

    q_all[pl.ds(mine, ROWS), :] = q_ref[...]
    q_all[pl.ds(other, ROWS), :] = qg_ref[0]
    g_all[pl.ds(mine, ROWS), :] = jnp.where(answers(mine), g_ref[...], jnp.zeros((), BF16))
    g_all[pl.ds(other, ROWS), :] = jnp.where(answers(other), qg_ref[1], jnp.zeros((), BF16))
    for i, src in enumerate((b_ref, a_ref, own_ref)):
        for at, lo in ((mine, 0), (other, ROWS)):
            rows = pl.ds(i * CHIP + at, ROWS)
            k_all[rows, :] = src[lo : lo + ROWS, 0:DH]
            v_all[rows, :] = src[lo : lo + ROWS, DH : 2 * DH]
    k_acc[...] = jnp.zeros(k_acc.shape, F32)
    v_acc[...] = jnp.zeros(v_acc.shape, F32)
    st_col = to_column(starts)

    def span_step(span, key_first, row_first, low, pos):
        pieces = [(o, min(256, span - o)) for o in range(0, span, 256)]
        queries = q_now[...]
        grads = g_now[...]
        top = jnp.full((8, LANES), MASKED, F32)
        for o, size in pieces:
            at = pl.multiple_of(key_first + o, 16)
            scores = nt(k_all[pl.ds(at, size), :], queries)
            key_pos = base + at + lax.broadcasted_iota(jnp.int32, (size, LANES // 2), 0)
            seen = (key_pos >= low) & (key_pos <= pos)
            scores = jnp.where(jnp.concatenate([seen, seen], axis=1), scores, MASKED)
            s_buf[o : o + size, :] = scores
            top = jnp.maximum(top, fold(scores, jnp.maximum))
        peak = jnp.max(top, axis=0, keepdims=True) * (SCALE * LOG2E)
        total = jnp.zeros((8, LANES), F32)
        delta = jnp.zeros((8, LANES), F32)
        for o, size in pieces:
            at = pl.multiple_of(key_first + o, 16)
            d_probs = nt(v_all[pl.ds(at, size), :], grads)
            weight = jnp.exp2(s_buf[o : o + size, :] * (SCALE * LOG2E) - peak)
            s_buf[o : o + size, :] = weight
            d_buf[o : o + size, :] = d_probs
            total = total + fold(weight, jnp.add)
            delta = delta + fold(weight * d_probs, jnp.add)
        inverse = 1.0 / jnp.sum(total, axis=0, keepdims=True)
        delta = jnp.sum(delta, axis=0, keepdims=True) * inverse
        dq = None
        for o, size in pieces:
            at = pl.multiple_of(key_first + o, 16)
            rows = pl.ds(at, size)
            probs = s_buf[o : o + size, :] * inverse
            d_scores = (probs * (d_buf[o : o + size, :] - delta)).astype(BF16)
            v_acc[rows, :] += nn(probs.astype(BF16), grads)
            k_acc[rows, :] += nn(d_scores, queries)
            more = tn(d_scores, k_all[rows, :])
            dq = more if dq is None else dq + more
        dq = (dq * SCALE).astype(BF16)
        for h in range(GROUP):
            dq_all[pl.ds(row_first, SUB), h * DH : (h + 1) * DH] = dq[h * SUB : (h + 1) * SUB]

    def step(s, carry):
        key_first = pl.multiple_of(sc_ref[2 + 2 * s], 16)
        pick = sc_ref[3 + 2 * s]
        row_first = pl.multiple_of(s * SUB, SUB)
        for h in range(GROUP):
            q_now[h * SUB : (h + 1) * SUB, :] = q_all[pl.ds(row_first, SUB), h * DH : (h + 1) * DH]
            g_now[h * SUB : (h + 1) * SUB, :] = g_all[pl.ds(row_first, SUB), h * DH : (h + 1) * DH]
        lane = lax.broadcasted_iota(jnp.int32, (1, LANES // 2), 1)
        pos = base + (WIN - CHIP) + row_first + lane % SUB
        low = jnp.max(jnp.where(st_col <= pos, st_col, 0), axis=0, keepdims=True)
        for v, span in enumerate(SPANS):
            pl.when(pick == v)(partial(span_step, span, key_first, row_first, low, pos))
        return carry

    lax.fori_loop(0, CHIP // SUB, step, 0)
    dq_own_ref[...] = dq_all[pl.ds(mine, ROWS), :]
    dq_other_ref[...] = dq_all[pl.ds(other, ROWS), :]
    for i, dst in enumerate((d_b_ref, d_a_ref, d_own_ref)):
        for at, lo in ((mine, 0), (other, ROWS)):
            rows = pl.ds(i * CHIP + at, ROWS)
            dst[lo : lo + ROWS, 0:DH] = (k_acc[rows, :] * SCALE).astype(dst.dtype)
            dst[lo : lo + ROWS, DH : 2 * DH] = v_acc[rows, :].astype(dst.dtype)
    for dst in (d_b_ref, d_a_ref):
        dst[CHIP:PACK, :] = own_ref[CHIP:PACK, :]


def doc_coefs(seq_len, st_ref, ct_ref, cnt_refs, tail_refs):
    starts = st_ref[...]
    n = starts.shape[1]
    sums = jnp.zeros((1, n), F32)
    for ref in tail_refs:
        sums = sums + jnp.sum(ref[CHIP:PACK, 0:n].astype(F32), axis=0, keepdims=True)
    docs = cnt_refs[0][0:1, 0:n]
    for ref in cnt_refs[1:]:
        docs = docs + ref[0:1, 0:n]
    size = jnp.maximum(ct_ref[...], 1).astype(F32)
    coef = LOSS_SCALE * 2.0 / (1.0 + jnp.exp(-sums / size)) / (size * docs)
    return starts, end_row(starts, seq_len), coef


def row_coefs(starts, ends, coef, first):
    n = starts.shape[1]
    pos = first + lax.broadcasted_iota(jnp.int32, (ROWS, n), 0)
    return jnp.sum(jnp.where((pos >= starts) & (pos < ends), coef, 0.0), axis=1, keepdims=True)


def key_value_kernel(seq_len, idx_ref, st_ref, ct_ref, *refs):
    cnt_refs, fwd_refs = refs[0:4], refs[4:7]
    own_refs, a_refs, b_refs = refs[7:9], refs[9:11], refs[11:13]
    mine_ref, snd_ref = refs[13:15]
    index = idx_ref[0]
    starts, ends, coef = doc_coefs(seq_len, st_ref, ct_ref, cnt_refs, (*fwd_refs, a_refs[0], b_refs[0]))
    for dst, lo, where in ((mine_ref, 0, index), (snd_ref, ROWS, index // 2 * 2 + 1 - index % 2)):
        scale = row_coefs(starts, ends, coef, where * ROWS)
        for j in range(CHUNKS):
            rows = slice(lo, lo + ROWS)
            out = own_refs[j][rows, :] + a_refs[j][rows, :].astype(F32) + b_refs[j][rows, :].astype(F32)
            out = (out * scale).astype(BF16)
            dst[:, j * DH : (j + 1) * DH] = out[:, 0:DH]
            dst[:, (CHUNKS + j) * DH : (CHUNKS + j + 1) * DH] = out[:, DH : 2 * DH]


def query_kernel(seq_len, idx_ref, st_ref, ct_ref, *refs):
    cnt_refs, tail_refs = refs[0:4], refs[4:9]
    mine_refs, got_refs = refs[9:11], refs[11:13]
    out_ref = refs[13]
    index = idx_ref[0]
    starts, ends, coef = doc_coefs(seq_len, st_ref, ct_ref, cnt_refs, tail_refs)
    scale = row_coefs(starts, ends, coef, index * ROWS)
    width = GROUP * DH
    for half in range(2):

        @pl.when(index % 2 == half)
        def _():
            for k, srcs in ((half, mine_refs), (1 - half, got_refs)):
                for j in range(CHUNKS):
                    lo = (k * CHUNKS + j) * width
                    out_ref[:, lo : lo + width] = (srcs[j][...].astype(F32) * scale).astype(BF16)


def local(query, key_value, upstream, log_ratio, doc_starts, answer_counts):
    count = lax.axis_size("ctx")
    seq_len = ROWS * count
    index = lax.axis_index("ctx").astype(jnp.int32)
    core = index % 2
    where = index.reshape(1)
    smem = pl.BlockSpec(memory_space=pltpu.SMEM)
    vmem = pl.BlockSpec(memory_space=pltpu.VMEM)
    params = pltpu.CompilerParams(vmem_limit_bytes=56 << 20)

    def moved(value, steps):
        first, last = (max(0, -steps), min(count, count - steps))
        return lax.ppermute(value, "ctx", [(i, i + steps) for i in range(first, last)])

    def swapped(value):
        return lax.ppermute(value, "ctx", [(i, i ^ 1) for i in range(count)])

    def pallas(body, out_shape, in_specs, out_specs, name):
        return pl.pallas_call(
            body, out_shape=out_shape, in_specs=in_specs, out_specs=out_specs, compiler_params=params, name=name
        )

    shape = jax.ShapeDtypeStruct
    half_cols = CHUNKS * GROUP * DH
    packed = shape((ROWS + TAIL, 2 * CHUNKS * DH), BF16)
    snd, mine = pallas(
        partial(prep_kernel, seq_len), (packed, packed), [smem] + [vmem] * 4, (vmem, vmem), "prep"
    )(where, key_value[0], log_ratio, doc_starts, answer_counts)
    got = swapped(snd)
    own = []
    for j in range(CHUNKS):
        cols = slice(2 * j * DH, 2 * (j + 1) * DH)
        own.append(
            jnp.concatenate([mine[:ROWS, cols], got[:ROWS, cols], mine[ROWS:, cols], got[ROWS:, cols]], axis=0)
        )
    back1 = [moved(x, 2) for x in own]
    back2 = [moved(x, 4) for x in own]
    theirs = (1 - core) * half_cols
    to_send = jnp.stack(
        [
            lax.dynamic_slice_in_dim(query[0], theirs, half_cols, 1),
            lax.dynamic_slice_in_dim(upstream[0], theirs, half_cols, 1),
        ]
    )
    swapped_rows = swapped(to_send)
    scalars, docs = pallas(
        scalar_kernel,
        (shape((2 + 2 * (CHIP // SUB),), jnp.int32), shape((8, 128), F32)),
        [smem] * 3,
        (smem, vmem),
        "scalars",
    )(where, doc_starts[0], answer_counts[0])
    size = lax.axis_size("dp")
    docs_all = [docs] + [
        lax.ppermute(docs, "dp", [(i, (i + k) % size) for i in range(size)]) for k in range(1, size)
    ]

    width = GROUP * DH
    dq_mine, dq_other, d_own, d_a, d_b = [], [], [], [], []
    for j in range(CHUNKS):
        full = lambda i, sc: (0, 0)
        picked = lambda i, sc, j=j: (0, sc[0] * CHUNKS + j)
        pack_spec = pl.BlockSpec((PACK, 2 * DH), full)
        row_spec = pl.BlockSpec((1, doc_starts.shape[1]), full)
        outs = pl.pallas_call(
            partial(attention_kernel, seq_len),
            grid_spec=pltpu.PrefetchScalarGridSpec(
                num_scalar_prefetch=1,
                grid=(1,),
                in_specs=[
                    pl.BlockSpec((ROWS, width), picked),
                    pl.BlockSpec((ROWS, width), picked),
                    pl.BlockSpec((2, ROWS, width), lambda i, sc, j=j: (0, 0, j)),
                    pack_spec,
                    pack_spec,
                    pack_spec,
                    row_spec,
                    row_spec,
                ],
                out_specs=[
                    pl.BlockSpec((ROWS, width), full),
                    pl.BlockSpec((ROWS, width), full),
                    pl.BlockSpec((CHIP, 2 * DH), full),
                    pack_spec,
                    pack_spec,
                ],
                scratch_shapes=[
                    pltpu.VMEM((CHIP, width), BF16),
                    pltpu.VMEM((CHIP, width), BF16),
                    pltpu.VMEM((WIN, DH), BF16),
                    pltpu.VMEM((WIN, DH), BF16),
                    pltpu.VMEM((LANES, DH), BF16),
                    pltpu.VMEM((LANES, DH), BF16),
                    pltpu.VMEM((SPANS[-1], LANES), F32),
                    pltpu.VMEM((SPANS[-1], LANES), F32),
                    pltpu.VMEM((WIN, DH), F32),
                    pltpu.VMEM((WIN, DH), F32),
                    pltpu.VMEM((CHIP, width), BF16),
                ],
            ),
            out_shape=[
                shape((ROWS, width), BF16),
                shape((ROWS, width), BF16),
                shape((CHIP, 2 * DH), F32),
                shape((PACK, 2 * DH), BF16),
                shape((PACK, 2 * DH), BF16),
            ],
            compiler_params=params,
            name="attention",
        )(scalars, query[0], upstream[0], swapped_rows, own[j], back1[j], back2[j], doc_starts, answer_counts)
        for kept, out in zip((dq_mine, dq_other, d_own, d_a, d_b), outs):
            kept.append(out)

    got_a = [moved(x, -2) for x in d_a]
    got_b = [moved(x, -4) for x in d_b]
    dq_got = [swapped(x) for x in dq_other]
    half = shape((ROWS, 2 * CHUNKS * DH), BF16)
    kv_mine, kv_send = pallas(
        partial(key_value_kernel, seq_len), (half, half), [smem] + [vmem] * 15, (vmem, vmem), "kv_out"
    )(where, doc_starts, answer_counts, *docs_all, own[0], back1[0], back2[0], *d_own, *got_a, *got_b)
    kv_got = swapped(kv_send)
    d_query = pallas(
        partial(query_kernel, seq_len),
        shape((ROWS, HQ * DH), BF16),
        [smem] + [vmem] * 15,
        vmem,
        "q_out",
    )(where, doc_starts, answer_counts, *docs_all, own[0], back1[0], back2[0], got_a[0], got_b[0], *dq_mine, *dq_got)
    cut = CHUNKS * DH
    lower, upper = (jnp.where(core == 0, kv_mine, kv_got), jnp.where(core == 0, kv_got, kv_mine))
    d_key_value = jnp.concatenate([lower[:, :cut], upper[:, :cut], lower[:, cut:], upper[:, cut:]], axis=1)
    return (d_query[None], d_key_value[None])


def solution(mesh):
    return jax.shard_map(
        local,
        mesh=mesh,
        in_specs=(
            P("dp", "ctx", None),
            P("dp", "ctx", None),
            P("dp", "ctx", None),
            P("dp", "ctx"),
            P("dp", None),
            P("dp", None),
        ),
        out_specs=(P("dp", "ctx", None), P("dp", "ctx", None)),
        check_vma=False,
    )
```

time: 246 us -> 90.4 us (0.37)
  blocking collectives: 75.6 us -> 0 us
  matrix products: 47.7 us -> 0 us
  waiting for transfers between devices: 46.3 us -> 8.48 us
  Pallas kernels: 0 us -> 29.2 us
  other arithmetic: 20.4 us -> 1.01 us
  local copies, waits for them, and re-layouts: 25.5 us -> 7.5 us
  starting transfers between devices: 26.5 us -> 42.2 us
    psum x2 -> x0, blocking collectives: 75.6 us -> none  [the longest x1 65.2 us: local(): doc_sum = lax.psum(partial_sum, 'ctx')]
    dot_general x24 -> x0, matrix products: 47.7 us -> none  [the longest x4 10.8 us: head_block(): jnp.einsum('gtk,tgd->kd', prob_low, out_grad, preferred_element_type=jnp....]
    ppermute x8 -> x16, waiting for transfers between devices: 46.3 us -> 8.48 us  [the longest x3 8.44 us: local(): lax.ppermute(docs, 'dp', [(i, (i + k) % size) for i in range(size)])]
    pallas_call x0 -> x6, Pallas kernels: none -> 29.2 us  [the longest x2 19 us: local(): pl.pallas_call(partial(attention_kernel, seq_len), grid_spec=pltpu.Prefet...]
    ppermute x8 -> x16, starting transfers between devices: 26.5 us -> 42.2 us  [the longest x8 29.1 us: moved(): lax.ppermute(value, 'ctx', [(i, i + steps) for i in range(first, last)])]
    reduce_sum x10 -> x0, other arithmetic: 11.6 us -> none  [the longest x4 7.23 us: head_block(): row_total = jnp.sum(jnp.exp(scores - row_max), axis=2, keepdims=True)]
    unnamed x13 -> x38, local copies, waits for them, and re-layouts: 9.31 us -> 4.3 us
    convert_element_type x2 -> x0, local copies, waits for them, and re-layouts: 4.48 us -> none  [local(): query_grad.transpose(1, 0, 2, 3).reshape(shard_len, HQ * DH)]
  transfers between devices with their start and end apart: 8 -> 16, of which waited for: 3 -> 3; matrix products, arithmetic and copies ran while one was open for 8% -> 2% of each run, Pallas kernels for 0% -> 33%
where the time goes in v1:
time: 90.4 us; the launch traced here: 89.4 us
  starting transfers between devices  42.2 us (47%)
  Pallas kernels  29.2 us (32%)
  waiting for transfers between devices  8.48 us (9%)
  local copies, waits for them, and re-layouts  7.5 us (8%)
  other arithmetic  1.01 us (1%)
  between operations  0.99 us (1%)
    ppermute x8, starting transfers between devices, moved(): lax.ppermute(value, 'ctx', [(i, i + steps) for i in range(first, last)])  29.1 us
    pallas_call x2, Pallas kernels, local(): pl.pallas_call(partial(attention_kernel, seq_len), grid_spec=pltpu.Prefet...  19 us
    ppermute x3, waiting for transfers between devices, local(): lax.ppermute(docs, 'dp', [(i, (i + k) % size) for i in range(size)])  8.44 us
    ppermute x5, starting transfers between devices, swapped(): return lax.ppermute(value, 'ctx', [(i, i ^ 1) for i in range(count)])  6.9 us
    ppermute x3, starting transfers between devices, local(): lax.ppermute(docs, 'dp', [(i, (i + k) % size) for i in range(size)])  6.23 us
    unnamed x38, local copies, waits for them, and re-layouts  4.3 us
    pallas_call x1, Pallas kernels, local(): pallas(partial(query_kernel, seq_len), shape((ROWS, HQ * DH), BF16), [sme...  3.43 us
    pallas_call x1, Pallas kernels, local(): pallas(partial(key_value_kernel, seq_len), (half, half), [smem] + [vmem]...  2.62 us
  transfers between devices with their start and end apart: 16, of which 3 were waited for; matrix products, arithmetic and copies ran while one was open for 2% of the time, Pallas kernels for 33%

profile of v1, /device:TPU:17, one launch (start us, length us, event | category | flops | bytes accessed | tf_op | source)
XLA Modules:
  0.0 89.4 jit_solution(7500881822436493206)
XLA Ops:
  0.6 1.5 %constant_dynamic-slice_fusion = (bf16[1,192,2048]{2,1,0:T(8,128)(2,1)S(1)}, bf16[1,192,2048]{2,1,0:T(8,128)(2,1)S(1)}) fusion(bf16[1,192,4096]{2,1,0:T(8,128)(2,1)} %param.8, s32[]{:T(128)S(6)} %select_n.24, bf16[1,192,4096]{2,1,0:T(8,128)(2,1)} %param.6), kind=kLoop, calls=%fused_computation.6 | loop fusion | bytes 3145732 | tf_op jit(solution)/shard_map/dynamic_slice | solution.py:352
  2.3 0.8 collective-permute-start.6
  3.0 2.1 %prep.1 = (bf16[208,512]{1,0:T(8,128)(2,1)}, bf16[208,512]{1,0:T(8,128)(2,1)}) custom-call(s32[1]{0:T(128)} %bitcast.idx_ref, bf16[192,1024]{1,0:T(8,128)(2,1)} %bitcast.14, f32[1,192]{1,0:T(1,128)} %lr_ref.1, s32[1,64]{1,0:T(1,128)} %st_ref.9, s32[1,64]{1,0:T(1,128)} %ct_ref.9), custom_call_target="tpu_custom_call" | custom-call | tf_op jit(solution)/shard_map/prep/pallas_call | solution.py:336
  5.1 1.0 %fusion = (bf16[192,256]{1,0:T(8,128)(2,1)S(1)}, bf16[192,256]{1,0:T(8,128)(2,1)S(1)}) fusion(bf16[208,512]{1,0:T(8,128)(2,1)} %get-tuple-element.19), kind=kLoop, calls=%fused_computation.8 | loop fusion | bytes 393216 | tf_op jit(solution)/shard_map/slice | solution.py:344
  6.1 0.7 fusion.2
  6.9 4.7 %collective-permute-start.10 = (bf16[416,256]{1,0:T(8,128)(2,1)S(1)}, bf16[416,256]{1,0:T(8,128)(2,1)S(1)}, u32[]{:S(2)}, u32[]{:S(2)}) collective-permute-start(bf16[416,256]{1,0:T(8,128)(2,1)S(1)} %pad_maximum_fusion.2.own_ref), channel_id=1, source_target_pairs={{0,16},{4,20},{8,24},{12,28},{16,32},{20,36},{24,40},{28,44},{32,4... | collective-permute-start | bytes 638984 | tf_op jit(solution)/shard_map/ppermute | solution.py:323
  11.5 2.2 %collective-permute-start.9 = (bf16[416,256]{1,0:T(8,128)(2,1)S(1)}, bf16[416,256]{1,0:T(8,128)(2,1)S(1)}, u32[]{:S(2)}, u32[]{:S(2)}) collective-permute-start(bf16[416,256]{1,0:T(8,128)(2,1)S(1)} %pad_maximum_fusion.2.own_ref), channel_id=1, source_target_pairs={{0,8},{4,12},{8,16},{12,20},{16,24},{20,28},{24,32},{28,36},{32,40... | collective-permute-start | bytes 638984 | tf_op jit(solution)/shard_map/ppermute | solution.py:323
  13.8 2.2 %collective-permute-start.4 = (bf16[416,256]{1,0:T(8,128)(2,1)S(1)}, bf16[416,256]{1,0:T(8,128)(2,1)S(1)}, u32[]{:S(2)}, u32[]{:S(2)}) collective-permute-start(bf16[416,256]{1,0:T(8,128)(2,1)S(1)} %pad_maximum_fusion.1.own_ref.refs_4_), channel_id=1, source_target_pairs={{0,8},{4,12},{8,16},{12,20},{16,24},{20,28},{24,32},{28,36},{32,40... | collective-permute-start | bytes 638984 | tf_op jit(solution)/shard_map/ppermute | solution.py:323
  16.0 5.9 %collective-permute-start.5 = (bf16[416,256]{1,0:T(8,128)(2,1)S(1)}, bf16[416,256]{1,0:T(8,128)(2,1)S(1)}, u32[]{:S(2)}, u32[]{:S(2)}) collective-permute-start(bf16[416,256]{1,0:T(8,128)(2,1)S(1)} %pad_maximum_fusion.1.own_ref.refs_4_), channel_id=1, source_target_pairs={{0,16},{4,20},{8,24},{12,28},{16,32},{20,36},{24,40},{28,44},{32,4... | collective-permute-start | bytes 638984 | tf_op jit(solution)/shard_map/ppermute | solution.py:323
  21.9 2.1 %scalars.1 = (s32[10]{0:T(128)}, f32[8,128]{1,0:T(8,128)}) custom-call(s32[1]{0:T(128)} %bitcast.idx_ref, s32[64]{0:T(128)} %bitcast.15, s32[64]{0:T(128)} %bitcast.16), custom_call_target="tpu_custom_call" | custom-call | tf_op jit(solution)/shard_map/scalars/pallas_call | solution.py:356
  24.0 0.6 copy-done.11
  24.7 0.5 copy-done
  25.2 9.5 %attention.3 = (bf16[192,1024]{1,0:T(8,128)(2,1)}, bf16[192,1024]{1,0:T(8,128)(2,1)}, f32[384,256]{1,0:T(8,128)}, bf16[416,256]{1,0:T(8,128)(2,1)}, bf16[416,256]{1,0:T(8,128)(2,1)}) custom-call(s32[10]{0:T(128)} %get-tuple-element.21.sc_ref, bf16[192,4096]{1,0:T(8,128)(2,1)} %bitcast.9, bf16[192,4096]{1,0:T(8,128)(2,1)} %bitcast.11, ...), custom_call_target="tpu_custom_call" | custom-call | tf_op jit(solution)/shard_map/attention/pallas_call | solution.py:375
  34.8 2.3 %collective-permute-start.13 = (bf16[416,256]{1,0:T(8,128)(2,1)}, bf16[416,256]{1,0:T(8,128)(2,1)S(1)}, u32[]{:S(2)}, u32[]{:S(2)}) collective-permute-start(bf16[416,256]{1,0:T(8,128)(2,1)} %get-tuple-element.30), channel_id=1, source_target_pairs={{8,0},{12,4},{16,8},{20,12},{24,16},{28,20},{32,24},{36,28},{40,32... | collective-permute-start | bytes 638984 | tf_op jit(solution)/shard_map/ppermute | solution.py:323
  37.1 3.6 %collective-permute-start.14 = (bf16[416,256]{1,0:T(8,128)(2,1)}, bf16[416,256]{1,0:T(8,128)(2,1)S(1)}, u32[]{:S(2)}, u32[]{:S(2)}) collective-permute-start(bf16[416,256]{1,0:T(8,128)(2,1)} %get-tuple-element.31), channel_id=1, source_target_pairs={{16,0},{20,4},{24,8},{28,12},{32,16},{36,20},{40,24},{44,28},{48,3... | collective-permute-start | bytes 638984 | tf_op jit(solution)/shard_map/ppermute | solution.py:323
  40.7 0.7 copy-done.2
  41.4 0.7 copy-done.3
  42.1 9.5 %attention.2 = (bf16[192,1024]{1,0:T(8,128)(2,1)}, bf16[192,1024]{1,0:T(8,128)(2,1)}, f32[384,256]{1,0:T(8,128)}, bf16[416,256]{1,0:T(8,128)(2,1)}, bf16[416,256]{1,0:T(8,128)(2,1)}) custom-call(s32[10]{0:T(128)} %get-tuple-element.21.sc_ref, bf16[192,4096]{1,0:T(8,128)(2,1)} %bitcast.10, bf16[192,4096]{1,0:T(8,128)(2,1)} %bitcast.12, ...), custom_call_target="tpu_custom_call" | custom-call | tf_op jit(solution)/shard_map/attention/pallas_call | solution.py:375
  51.6 4.2 %collective-permute-start.7 = (bf16[416,256]{1,0:T(8,128)(2,1)}, bf16[416,256]{1,0:T(8,128)(2,1)S(1)}, u32[]{:S(2)}, u32[]{:S(2)}) collective-permute-start(bf16[416,256]{1,0:T(8,128)(2,1)} %get-tuple-element.22), channel_id=1, source_target_pairs={{8,0},{12,4},{16,8},{20,12},{24,16},{28,20},{32,24},{36,28},{40,32... | collective-permute-start | bytes 638984 | tf_op jit(solution)/shard_map/ppermute | solution.py:323
  55.8 4.1 %collective-permute-start.8 = (bf16[416,256]{1,0:T(8,128)(2,1)}, bf16[416,256]{1,0:T(8,128)(2,1)S(1)}, u32[]{:S(2)}, u32[]{:S(2)}) collective-permute-start(bf16[416,256]{1,0:T(8,128)(2,1)} %get-tuple-element.23), channel_id=1, source_target_pairs={{16,0},{20,4},{24,8},{28,12},{32,16},{36,20},{40,24},{44,28},{48,3... | collective-permute-start | bytes 638984 | tf_op jit(solution)/shard_map/ppermute | solution.py:323
  59.9 3.8 %collective-permute-start = (f32[8,128]{1,0:T(8,128)S(1)}, f32[8,128]{1,0:T(8,128)S(1)}, u32[]{:S(2)}, u32[]{:S(2)}) collective-permute-start(f32[8,128]{1,0:T(8,128)S(1)} %copy-done.14), channel_id=1, source_target_pairs={{0,1},{1,2},{2,3},{3,0},{4,5},{5,6},{6,7},{7,4},{8,9},{9,10},{10,1... | collective-permute-start | bytes 12296 | tf_op jit(solution)/shard_map/ppermute | solution.py:365
  63.7 4.4 %collective-permute-done.refs_1_ = f32[8,128]{1,0:T(8,128)S(1)} collective-permute-done((f32[8,128]{1,0:T(8,128)S(1)}, f32[8,128]{1,0:T(8,128)S(1)}, u32[]{:S(2)}, u32[]{:S(2)}) %collective-permute-start) | collective-permute-done | bytes 4128 | tf_op jit(solution)/shard_map/ppermute | solution.py:365
  68.1 0.9 %collective-permute-start.1 = (f32[8,128]{1,0:T(8,128)S(1)}, f32[8,128]{1,0:T(8,128)S(1)}, u32[]{:S(2)}, u32[]{:S(2)}) collective-permute-start(f32[8,128]{1,0:T(8,128)S(1)} %copy-done.14), channel_id=1, source_target_pairs={{0,2},{1,3},{2,0},{3,1},{4,6},{5,7},{6,4},{7,5},{8,10},{9,11},{10,... | collective-permute-start | bytes 12296 | tf_op jit(solution)/shard_map/ppermute | solution.py:365
  69.1 3.0 %collective-permute-done.1.refs_2_ = f32[8,128]{1,0:T(8,128)S(1)} collective-permute-done((f32[8,128]{1,0:T(8,128)S(1)}, f32[8,128]{1,0:T(8,128)S(1)}, u32[]{:S(2)}, u32[]{:S(2)}) %collective-permute-start.1) | collective-permute-done | bytes 4128 | tf_op jit(solution)/shard_map/ppermute | solution.py:365
  72.1 1.5 %collective-permute-start.2 = (f32[8,128]{1,0:T(8,128)S(1)}, f32[8,128]{1,0:T(8,128)S(1)}, u32[]{:S(2)}, u32[]{:S(2)}) collective-permute-start(f32[8,128]{1,0:T(8,128)S(1)} %copy-done.14), channel_id=1, source_target_pairs={{0,3},{1,0},{2,1},{3,2},{4,7},{5,4},{6,5},{7,6},{8,11},{9,8},{10,9... | collective-permute-start | bytes 12296 | tf_op jit(solution)/shard_map/ppermute | solution.py:365
  73.6 1.0 %collective-permute-done.2.refs_3_ = f32[8,128]{1,0:T(8,128)S(1)} collective-permute-done((f32[8,128]{1,0:T(8,128)S(1)}, f32[8,128]{1,0:T(8,128)S(1)}, u32[]{:S(2)}, u32[]{:S(2)}) %collective-permute-start.2) | collective-permute-done | bytes 4128 | tf_op jit(solution)/shard_map/ppermute | solution.py:365
  74.6 5.6 %collective-permute-start.12 = (bf16[192,1024]{1,0:T(8,128)(2,1)S(1)}, bf16[192,1024]{1,0:T(8,128)(2,1)S(1)}, u32[]{:S(2)}, u32[]{:S(2)}) collective-permute-start(bf16[192,1024]{1,0:T(8,128)(2,1)S(1)} %copy-done.18), channel_id=1, source_target_pairs={{0,4},{4,0},{8,12},{12,8},{16,20},{20,16},{24,28},{28,24},{32,36},... | collective-permute-start | bytes 1179656 | tf_op jit(solution)/shard_map/ppermute | solution.py:326
  80.4 0.5 copy-done.9
  81.1 2.6 %kv_out.1 = (bf16[192,512]{1,0:T(8,128)(2,1)}, bf16[192,512]{1,0:T(8,128)(2,1)}) custom-call(s32[1]{0:T(128)} %bitcast.idx_ref, s32[1,64]{1,0:T(1,128)} %st_ref.9, s32[1,64]{1,0:T(1,128)} %ct_ref.9, f32[8,128]{1,0:T(8,128)} %get-tuple-element.18.refs_0_, f32[8,128]{1,0:T(8,128)} %copy-done.15, f32[8,128]{1,0:T(8,128)} %copy-done.16, f32[8,128]{1,0:T(8,128)} %copy-done.17, ...), custom_call_target="tpu_custom_call" | custom-call | tf_op jit(solution)/shard_map/kv_out/pallas_call | solution.py:428
  84.2 0.8 copy-done.7
  85.1 3.4 %q_out.1 = bf16[192,4096]{1,0:T(8,128)(2,1)} custom-call(s32[1]{0:T(128)} %bitcast.idx_ref, s32[1,64]{1,0:T(1,128)} %st_ref.9, s32[1,64]{1,0:T(1,128)} %ct_ref.9, f32[8,128]{1,0:T(8,128)} %get-tuple-element.18.refs_0_, f32[8,128]{1,0:T(8,128)} %copy-done.15, f32[8,128]{1,0:T(8,128)} %copy-done.16, f32[8,128]{1,0:T(8,128)} %copy-done.17, ...), custom_call_target="tpu_custom_call" | custom-call | tf_op jit(solution)/shard_map/q_out/pallas_call | solution.py:432
  88.6 0.8 maximum_bitcast_fusion
  (56 shorter events, 1.4 us)
Async XLA Ops:
  2.3 21.7 %collective-permute-start.6 = (bf16[2,192,2048]{2,1,0:T(8,128)(2,1)S(1)}, bf16[2,192,2048]{2,1,0:T(8,128)(2,1)S(1)}, u32[]{:S(2)}, u32[]{:S(2)}) collective-permute-start(bf16[2,192,2048]{2,1,0:T(8,128)(2,1)S(1)} %pad_maximum_fusion), channel_id=1, source_target_pairs={{0,4},{4,0},{8,12},{12,8},{16,20},{20,16},{24,28},{28,24},{32,36},... | collective-permute-start | bytes 4718600 | tf_op jit(solution)/shard_map/ppermute | solution.py:326
  5.1 1.7 %collective-permute-start.3 = (bf16[208,512]{1,0:T(8,128)(2,1)}, bf16[208,512]{1,0:T(8,128)(2,1)S(1)}, u32[]{:S(2)}, u32[]{:S(2)}) collective-permute-start(bf16[208,512]{1,0:T(8,128)(2,1)} %get-tuple-element.20), channel_id=1, source_target_pairs={{0,4},{4,0},{8,12},{12,8},{16,20},{20,16},{24,28},{28,24},{32,36},... | collective-permute-start | bytes 638984 | tf_op jit(solution)/shard_map/ppermute | solution.py:326
  6.9 17.2 %copy-start.6 = (bf16[416,256]{1,0:T(8,128)(2,1)}, bf16[416,256]{1,0:T(8,128)(2,1)S(1)}, u32[]{:S(2)}) copy-start(bf16[416,256]{1,0:T(8,128)(2,1)S(1)} %pad_maximum_fusion.2.own_ref) | copy-start | bytes 638980
  6.9 17.1 %collective-permute-start.10 = (bf16[416,256]{1,0:T(8,128)(2,1)S(1)}, bf16[416,256]{1,0:T(8,128)(2,1)S(1)}, u32[]{:S(2)}, u32[]{:S(2)}) collective-permute-start(bf16[416,256]{1,0:T(8,128)(2,1)S(1)} %pad_maximum_fusion.2.own_ref), channel_id=1, source_target_pairs={{0,16},{4,20},{8,24},{12,28},{16,32},{20,36},{24,40},{28,44},{32,4... | collective-permute-start | bytes 638984 | tf_op jit(solution)/shard_map/ppermute | solution.py:323
  11.5 12.4 %collective-permute-start.9 = (bf16[416,256]{1,0:T(8,128)(2,1)S(1)}, bf16[416,256]{1,0:T(8,128)(2,1)S(1)}, u32[]{:S(2)}, u32[]{:S(2)}) collective-permute-start(bf16[416,256]{1,0:T(8,128)(2,1)S(1)} %pad_maximum_fusion.2.own_ref), channel_id=1, source_target_pairs={{0,8},{4,12},{8,16},{12,20},{16,24},{20,28},{24,32},{28,36},{32,40... | collective-permute-start | bytes 638984 | tf_op jit(solution)/shard_map/ppermute | solution.py:323
  13.8 26.9 %copy-start.1 = (bf16[416,256]{1,0:T(8,128)(2,1)}, bf16[416,256]{1,0:T(8,128)(2,1)S(1)}, u32[]{:S(2)}) copy-start(bf16[416,256]{1,0:T(8,128)(2,1)S(1)} %pad_maximum_fusion.1.own_ref.refs_4_) | copy-start | bytes 638980
  13.8 26.9 %collective-permute-start.4 = (bf16[416,256]{1,0:T(8,128)(2,1)S(1)}, bf16[416,256]{1,0:T(8,128)(2,1)S(1)}, u32[]{:S(2)}, u32[]{:S(2)}) collective-permute-start(bf16[416,256]{1,0:T(8,128)(2,1)S(1)} %pad_maximum_fusion.1.own_ref.refs_4_), channel_id=1, source_target_pairs={{0,8},{4,12},{8,16},{12,20},{16,24},{20,28},{24,32},{28,36},{32,40... | collective-permute-start | bytes 638984 | tf_op jit(solution)/shard_map/ppermute | solution.py:323
  16.0 24.7 %collective-permute-start.5 = (bf16[416,256]{1,0:T(8,128)(2,1)S(1)}, bf16[416,256]{1,0:T(8,128)(2,1)S(1)}, u32[]{:S(2)}, u32[]{:S(2)}) collective-permute-start(bf16[416,256]{1,0:T(8,128)(2,1)S(1)} %pad_maximum_fusion.1.own_ref.refs_4_), channel_id=1, source_target_pairs={{0,16},{4,20},{8,24},{12,28},{16,32},{20,36},{24,40},{28,44},{32,4... | collective-permute-start | bytes 638984 | tf_op jit(solution)/shard_map/ppermute | solution.py:323
  24.0 0.7 copy-start.12
  24.0 1.2 %copy-start = (bf16[2,192,2048]{2,1,0:T(8,128)(2,1)}, bf16[2,192,2048]{2,1,0:T(8,128)(2,1)S(1)}, u32[]{:S(2)}) copy-start(bf16[2,192,2048]{2,1,0:T(8,128)(2,1)S(1)} %collective-permute-done.6.qg_ref) | copy-start | bytes 4718596
  34.8 45.4 %collective-permute-start.13 = (bf16[416,256]{1,0:T(8,128)(2,1)}, bf16[416,256]{1,0:T(8,128)(2,1)S(1)}, u32[]{:S(2)}, u32[]{:S(2)}) collective-permute-start(bf16[416,256]{1,0:T(8,128)(2,1)} %get-tuple-element.30), channel_id=1, source_target_pairs={{8,0},{12,4},{16,8},{20,12},{24,16},{28,20},{32,24},{36,28},{40,32... | collective-permute-start | bytes 638984 | tf_op jit(solution)/shard_map/ppermute | solution.py:323
  37.0 22.8 %copy-start.14 = (f32[8,128]{1,0:T(8,128)S(1)}, f32[8,128]{1,0:T(8,128)}, u32[]{:S(2)}) copy-start(f32[8,128]{1,0:T(8,128)} %get-tuple-element.18.refs_0_) | copy-start | bytes 12292
  37.0 37.5 %copy-start.18 = (bf16[192,1024]{1,0:T(8,128)(2,1)S(1)}, bf16[192,1024]{1,0:T(8,128)(2,1)}, u32[]{:S(2)}) copy-start(bf16[192,1024]{1,0:T(8,128)(2,1)} %get-tuple-element.27) | copy-start | bytes 1179652
  37.1 43.2 %collective-permute-start.14 = (bf16[416,256]{1,0:T(8,128)(2,1)}, bf16[416,256]{1,0:T(8,128)(2,1)S(1)}, u32[]{:S(2)}, u32[]{:S(2)}) collective-permute-start(bf16[416,256]{1,0:T(8,128)(2,1)} %get-tuple-element.31), channel_id=1, source_target_pairs={{16,0},{20,4},{24,8},{28,12},{32,16},{36,20},{40,24},{44,28},{48,3... | collective-permute-start | bytes 638984 | tf_op jit(solution)/shard_map/ppermute | solution.py:323
  40.7 0.7 copy-start.2
  51.6 28.7 %collective-permute-start.7 = (bf16[416,256]{1,0:T(8,128)(2,1)}, bf16[416,256]{1,0:T(8,128)(2,1)S(1)}, u32[]{:S(2)}, u32[]{:S(2)}) collective-permute-start(bf16[416,256]{1,0:T(8,128)(2,1)} %get-tuple-element.22), channel_id=1, source_target_pairs={{8,0},{12,4},{16,8},{20,12},{24,16},{28,20},{32,24},{36,28},{40,32... | collective-permute-start | bytes 638984 | tf_op jit(solution)/shard_map/ppermute | solution.py:323
  55.8 24.5 %collective-permute-start.8 = (bf16[416,256]{1,0:T(8,128)(2,1)}, bf16[416,256]{1,0:T(8,128)(2,1)S(1)}, u32[]{:S(2)}, u32[]{:S(2)}) collective-permute-start(bf16[416,256]{1,0:T(8,128)(2,1)} %get-tuple-element.23), channel_id=1, source_target_pairs={{16,0},{20,4},{24,8},{28,12},{32,16},{36,20},{40,24},{44,28},{48,3... | collective-permute-start | bytes 638984 | tf_op jit(solution)/shard_map/ppermute | solution.py:323
  59.9 8.3 %collective-permute-start = (f32[8,128]{1,0:T(8,128)S(1)}, f32[8,128]{1,0:T(8,128)S(1)}, u32[]{:S(2)}, u32[]{:S(2)}) collective-permute-start(f32[8,128]{1,0:T(8,128)S(1)} %copy-done.14), channel_id=1, source_target_pairs={{0,1},{1,2},{2,3},{3,0},{4,5},{5,6},{6,7},{7,4},{8,9},{9,10},{10,1... | collective-permute-start | bytes 12296 | tf_op jit(solution)/shard_map/ppermute | solution.py:365
  68.1 12.2 %copy-start.15 = (f32[8,128]{1,0:T(8,128)}, f32[8,128]{1,0:T(8,128)S(1)}, u32[]{:S(2)}) copy-start(f32[8,128]{1,0:T(8,128)S(1)} %collective-permute-done.refs_1_) | copy-start | bytes 12292
  68.1 4.0 %collective-permute-start.1 = (f32[8,128]{1,0:T(8,128)S(1)}, f32[8,128]{1,0:T(8,128)S(1)}, u32[]{:S(2)}, u32[]{:S(2)}) collective-permute-start(f32[8,128]{1,0:T(8,128)S(1)} %copy-done.14), channel_id=1, source_target_pairs={{0,2},{1,3},{2,0},{3,1},{4,6},{5,7},{6,4},{7,5},{8,10},{9,11},{10,... | collective-permute-start | bytes 12296 | tf_op jit(solution)/shard_map/ppermute | solution.py:365
  72.1 8.2 %copy-start.16 = (f32[8,128]{1,0:T(8,128)}, f32[8,128]{1,0:T(8,128)S(1)}, u32[]{:S(2)}) copy-start(f32[8,128]{1,0:T(8,128)S(1)} %collective-permute-done.1.refs_2_) | copy-start | bytes 12292
  72.1 2.5 %collective-permute-start.2 = (f32[8,128]{1,0:T(8,128)S(1)}, f32[8,128]{1,0:T(8,128)S(1)}, u32[]{:S(2)}, u32[]{:S(2)}) collective-permute-start(f32[8,128]{1,0:T(8,128)S(1)} %copy-done.14), channel_id=1, source_target_pairs={{0,3},{1,0},{2,1},{3,2},{4,7},{5,4},{6,5},{7,6},{8,11},{9,8},{10,9... | collective-permute-start | bytes 12296 | tf_op jit(solution)/shard_map/ppermute | solution.py:365
  74.6 5.8 %copy-start.17 = (f32[8,128]{1,0:T(8,128)}, f32[8,128]{1,0:T(8,128)S(1)}, u32[]{:S(2)}) copy-start(f32[8,128]{1,0:T(8,128)S(1)} %collective-permute-done.2.refs_3_) | copy-start | bytes 12292
  74.6 9.6 %collective-permute-start.12 = (bf16[192,1024]{1,0:T(8,128)(2,1)S(1)}, bf16[192,1024]{1,0:T(8,128)(2,1)S(1)}, u32[]{:S(2)}, u32[]{:S(2)}) collective-permute-start(bf16[192,1024]{1,0:T(8,128)(2,1)S(1)} %copy-done.18), channel_id=1, source_target_pairs={{0,4},{4,0},{8,12},{12,8},{16,20},{20,16},{24,28},{28,24},{32,36},... | collective-permute-start | bytes 1179656 | tf_op jit(solution)/shard_map/ppermute | solution.py:326
  80.2 4.0 %collective-permute-start.11 = (bf16[192,1024]{1,0:T(8,128)(2,1)}, bf16[192,1024]{1,0:T(8,128)(2,1)S(1)}, u32[]{:S(2)}, u32[]{:S(2)}) collective-permute-start(bf16[192,1024]{1,0:T(8,128)(2,1)} %get-tuple-element.26), channel_id=1, source_target_pairs={{0,4},{4,0},{8,12},{12,8},{16,20},{20,16},{24,28},{28,24},{32,36},... | collective-permute-start | bytes 1179656 | tf_op jit(solution)/shard_map/ppermute | solution.py:326
  80.3 0.7 copy-start.10
  80.3 0.7 copy-start.4
  80.3 0.8 copy-start.5
  83.7 4.8 %collective-permute-start.15 = (bf16[192,512]{1,0:T(8,128)(2,1)}, bf16[192,512]{1,0:T(8,128)(2,1)S(1)}, u32[]{:S(2)}, u32[]{:S(2)}) collective-permute-start(bf16[192,512]{1,0:T(8,128)(2,1)} %get-tuple-element.33), channel_id=1, source_target_pairs={{0,4},{4,0},{8,12},{12,8},{16,20},{20,16},{24,28},{28,24},{32,36},... | collective-permute-start | bytes 589832 | tf_op jit(solution)/shard_map/ppermute | solution.py:326
  84.2 0.8 copy-start.7
  84.2 0.9 %copy-start.8 = (bf16[192,1024]{1,0:T(8,128)(2,1)}, bf16[192,1024]{1,0:T(8,128)(2,1)S(1)}, u32[]{:S(2)}) copy-start(bf16[192,1024]{1,0:T(8,128)(2,1)S(1)} %collective-permute-done.11.refs_11_) | copy-start | bytes 1179652
  85.1 3.4 %copy-start.13 = (bf16[192,512]{1,0:T(8,128)(2,1)S(1)}, bf16[192,512]{1,0:T(8,128)(2,1)}, u32[]{:S(2)}) copy-start(bf16[192,512]{1,0:T(8,128)(2,1)} %get-tuple-element.32) | copy-start | bytes 589828
  (3 other events, 2.0 us)

commit v2 on v1

v2 whole, which is shorter than its diff:
```python
from functools import partial

import jax
import jax.numpy as jnp
from jax import lax
from jax.experimental import pallas as pl
from jax.experimental.pallas import tpu as pltpu
from jax.sharding import PartitionSpec as P


HQ = 32
HK = 4
DH = 128
LOSS_SCALE = 65536
ROWS = 192
CHIP = 2 * ROWS
WIN = 3 * CHIP
GROUP = HQ // HK
SUB = 96
LANES = SUB * GROUP
SPANS = (256, 512, 640, 784, 896)
CHUNKS = 2
TAIL = 16
PACK = CHIP + TAIL
MASKED = -1e30
SCALE = DH ** (-0.5)
LOG2E = 1.4426950408889634
DQ_T = True
KV_T = False
F32 = jnp.float32
BF16 = jnp.bfloat16


def to_column(row, shift=0):
    n = row.shape[1]
    r = lax.broadcasted_iota(jnp.int32, (n, n), 0)
    c = lax.broadcasted_iota(jnp.int32, (n, n), 1)
    return jnp.sum(jnp.where(c == r + shift, row, 0), axis=1, keepdims=True)


def end_row(starts, seq_len):
    n = starts.shape[1]
    r = lax.broadcasted_iota(jnp.int32, (n, n), 0)
    c = lax.broadcasted_iota(jnp.int32, (n, n), 1)
    col = to_column(starts)
    row = jnp.sum(jnp.where(r == c + 1, col, 0), axis=0, keepdims=True)
    lane = lax.broadcasted_iota(jnp.int32, (1, n), 1)
    return jnp.where(lane == n - 1, seq_len, row)


def pack_kernel(seq_len, idx_ref, kv_ref, got_ref, lr_ref, got_lr_ref, st_ref, ct_ref, *own_refs):
    index = idx_ref[0]
    core = index % 2
    for half in range(2):

        @pl.when(core == half)
        def _():
            for j in range(CHUNKS):
                for k in range(2):
                    lo = k * HK * DH + (half * CHUNKS + j) * DH
                    own_refs[j][0:ROWS, k * DH : (k + 1) * DH] = kv_ref[:, lo : lo + DH]
                    own_refs[j][ROWS:CHIP, k * DH : (k + 1) * DH] = got_ref[:, lo : lo + DH]

    starts = st_ref[...]
    n = starts.shape[1]
    row_i = lax.broadcasted_iota(jnp.int32, (n, 1), 0)
    st = to_column(starts)
    en = jnp.where(row_i == n - 1, seq_len, to_column(starts, 1))
    first = jnp.maximum(st, en - to_column(ct_ref[...]))
    lane = lax.broadcasted_iota(jnp.int32, (n, ROWS), 1)
    part = jnp.zeros((n, 1), F32)
    for ref, where in ((lr_ref, index), (got_lr_ref, index + 1 - 2 * core)):
        pos = where * ROWS + lane
        part = part + jnp.sum(jnp.where((pos >= first) & (pos < en), ref[...], 0.0), axis=1, keepdims=True)
    r = lax.broadcasted_iota(jnp.int32, (n, n), 0)
    c = lax.broadcasted_iota(jnp.int32, (n, n), 1)
    part = jnp.sum(jnp.where(r == c, part, 0.0), axis=0, keepdims=True)
    high = part.astype(BF16).astype(F32)
    rest = part - high
    mid = rest.astype(BF16).astype(F32)
    low = rest - mid
    k = lax.broadcasted_iota(jnp.int32, (TAIL, n), 0)
    tail = jnp.where(k == 0, high, jnp.where(k == 1, mid, jnp.where(k == 2, low, 0.0))).astype(BF16)
    for ref in own_refs:
        ref[CHIP:PACK, :] = jnp.zeros((TAIL, 2 * DH), BF16)
    own_refs[0][CHIP:PACK, 0:n] = tail


def early_kernel(idx_ref, q_hbm, g_hbm, kv_hbm, lr_ref, st_ref, ct_ref, sc_ref, cnt_ref, q_ref, g_ref, kv_ref, lr_out, st_out, ct_out, sems):
    cols = pl.ds(pl.multiple_of(idx_ref[0] % 2 * q_ref.shape[1], q_ref.shape[1]), q_ref.shape[1])
    copies = [
        pltpu.make_async_copy(kv_hbm, kv_ref, sems.at[0]),
        pltpu.make_async_copy(q_hbm.at[:, cols], q_ref, sems.at[1]),
        pltpu.make_async_copy(g_hbm.at[:, cols], g_ref, sems.at[2]),
    ]
    for copy in copies:
        copy.start()
    lr_out[...] = lr_ref[...]
    st_out[...] = st_ref[...]
    ct_out[...] = ct_ref[...]
    index = idx_ref[0]
    first = index // 2 * CHIP
    base = first - (WIN - CHIP)
    sc_ref[0] = index % 2
    sc_ref[1] = base
    starts = st_ref[...].astype(F32)
    for s in range(CHIP // SUB):
        at = (first + s * SUB).astype(F32)
        start = jnp.max(jnp.where(starts <= at, starts, 0.0)).astype(jnp.int32)
        low = jnp.maximum(start - base, 0) // 16 * 16
        need = (WIN - CHIP) + (s + 1) * SUB - low
        pick = jnp.int32(0)
        span = jnp.int32(SPANS[0])
        for v in range(1, len(SPANS)):
            more = need > SPANS[v - 1]
            pick = jnp.where(more, v, pick)
            span = jnp.where(more, SPANS[v], span)
        sc_ref[2 + 2 * s] = jnp.minimum(low, WIN - span)
        sc_ref[3 + 2 * s] = pick
    used = jnp.sum(jnp.where(ct_ref[...] > 0, 1.0, 0.0), axis=1, keepdims=True)
    cnt_ref[...] = jnp.broadcast_to(used, cnt_ref.shape)
    for copy in copies:
        copy.wait()


def nt(a, b):
    return lax.dot_general(a, b, (((1,), (1,)), ((), ())), preferred_element_type=F32)


def nn(a, b):
    return lax.dot_general(a, b, (((1,), (0,)), ((), ())), preferred_element_type=F32)


def tn(a, b):
    return lax.dot_general(a, b, (((0,), (0,)), ((), ())), preferred_element_type=F32)


def fold(x, op):
    out = x[0:8]
    for i in range(8, x.shape[0], 8):
        out = op(out, x[i : i + 8])
    return out


def attention_kernel(
    seq_len,
    chunk,
    sc_ref,
    q_ref,
    g_ref,
    got_q_ref,
    got_g_ref,
    own_ref,
    a_ref,
    b_ref,
    st_ref,
    ct_ref,
    dq_own_ref,
    dq_other_ref,
    d_own_ref,
    d_a_ref,
    d_b_ref,
    q_all,
    g_all,
    k_all,
    v_all,
    q_now,
    g_now,
    s_buf,
    d_buf,
    k_acc,
    v_acc,
    dq_all,
):
    core = sc_ref[0]
    base = sc_ref[1]
    mine = pl.multiple_of(core * ROWS, ROWS)
    other = pl.multiple_of((1 - core) * ROWS, ROWS)
    starts = st_ref[...]
    n = starts.shape[1]
    ends = end_row(starts, seq_len)
    first_answer = jnp.maximum(starts, ends - ct_ref[...])

    def answers(offset):
        pos = base + (WIN - CHIP) + offset + lax.broadcasted_iota(jnp.int32, (ROWS, n), 0)
        hit = jnp.where((pos >= first_answer) & (pos < ends), 1.0, 0.0)
        return jnp.sum(hit, axis=1, keepdims=True) > 0.5

    width = GROUP * DH
    cols = slice(chunk * width, (chunk + 1) * width)
    got_cols = pl.ds(pl.multiple_of((core * CHUNKS + chunk) * width, width), width)
    q_all[pl.ds(mine, ROWS), :] = q_ref[:, cols]
    q_all[pl.ds(other, ROWS), :] = got_q_ref[:, got_cols]
    g_all[pl.ds(mine, ROWS), :] = jnp.where(answers(mine), g_ref[:, cols], jnp.zeros((), BF16))
    g_all[pl.ds(other, ROWS), :] = jnp.where(answers(other), got_g_ref[:, got_cols], jnp.zeros((), BF16))
    for i, src in enumerate((b_ref, a_ref, own_ref)):
        for at, lo in ((mine, 0), (other, ROWS)):
            rows = pl.ds(i * CHIP + at, ROWS)
            k_all[rows, :] = src[lo : lo + ROWS, 0:DH]
            v_all[rows, :] = src[lo : lo + ROWS, DH : 2 * DH]
    k_acc[...] = jnp.zeros(k_acc.shape, F32)
    v_acc[...] = jnp.zeros(v_acc.shape, F32)
    st_col = to_column(starts)

    def span_step(span, key_first, row_first, low, pos):
        pieces = [(o, min(256, span - o)) for o in range(0, span, 256)]
        queries = q_now[...]
        grads = g_now[...]
        top = jnp.full((8, LANES), MASKED, F32)
        for o, size in pieces:
            at = pl.multiple_of(key_first + o, 16)
            scores = nt(k_all[pl.ds(at, size), :], queries)
            key_pos = base + at + lax.broadcasted_iota(jnp.int32, (size, LANES // 2), 0)
            seen = (key_pos >= low) & (key_pos <= pos)
            scores = jnp.where(jnp.concatenate([seen, seen], axis=1), scores, MASKED)
            s_buf[o : o + size, :] = scores
            top = jnp.maximum(top, fold(scores, jnp.maximum))
        peak = jnp.max(top, axis=0, keepdims=True) * (SCALE * LOG2E)
        total = jnp.zeros((8, LANES), F32)
        delta = jnp.zeros((8, LANES), F32)
        for o, size in pieces:
            at = pl.multiple_of(key_first + o, 16)
            d_probs = nt(v_all[pl.ds(at, size), :], grads)
            weight = jnp.exp2(s_buf[o : o + size, :] * (SCALE * LOG2E) - peak)
            s_buf[o : o + size, :] = weight
            d_buf[o : o + size, :] = d_probs
            total = total + fold(weight, jnp.add)
            delta = delta + fold(weight * d_probs, jnp.add)
        inverse = 1.0 / jnp.sum(total, axis=0, keepdims=True)
        delta = jnp.sum(delta, axis=0, keepdims=True) * inverse
        dq = None
        grads_t = grads.T if KV_T else None
        queries_t = queries.T if KV_T else None
        for o, size in pieces:
            at = pl.multiple_of(key_first + o, 16)
            rows = pl.ds(at, size)
            probs = s_buf[o : o + size, :] * inverse
            d_scores = (probs * (d_buf[o : o + size, :] - delta)).astype(BF16)
            if KV_T:
                v_acc[rows, :] += nt(grads_t, probs.astype(BF16)).T
                k_acc[rows, :] += nt(queries_t, d_scores).T
            else:
                v_acc[rows, :] += nn(probs.astype(BF16), grads)
                k_acc[rows, :] += nn(d_scores, queries)
            more = tn(k_all[rows, :], d_scores) if DQ_T else tn(d_scores, k_all[rows, :])
            dq = more if dq is None else dq + more
        if DQ_T:
            dq = dq.T
        dq = (dq * SCALE).astype(BF16)
        for h in range(GROUP):
            dq_all[pl.ds(row_first, SUB), h * DH : (h + 1) * DH] = dq[h * SUB : (h + 1) * SUB]

    def step(s, carry):
        key_first = pl.multiple_of(sc_ref[2 + 2 * s], 16)
        pick = sc_ref[3 + 2 * s]
        row_first = pl.multiple_of(s * SUB, SUB)
        for h in range(GROUP):
            q_now[h * SUB : (h + 1) * SUB, :] = q_all[pl.ds(row_first, SUB), h * DH : (h + 1) * DH]
            g_now[h * SUB : (h + 1) * SUB, :] = g_all[pl.ds(row_first, SUB), h * DH : (h + 1) * DH]
        lane = lax.broadcasted_iota(jnp.int32, (1, LANES // 2), 1)
        pos = base + (WIN - CHIP) + row_first + lane % SUB
        low = jnp.max(jnp.where(st_col <= pos, st_col, 0), axis=0, keepdims=True)
        for v, span in enumerate(SPANS):
            pl.when(pick == v)(partial(span_step, span, key_first, row_first, low, pos))
        return carry

    lax.fori_loop(0, CHIP // SUB, step, 0)
    dq_own_ref[...] = dq_all[pl.ds(mine, ROWS), :]
    dq_other_ref[...] = dq_all[pl.ds(other, ROWS), :]
    for i, dst in enumerate((d_b_ref, d_a_ref, d_own_ref)):
        for at, lo in ((mine, 0), (other, ROWS)):
            rows = pl.ds(i * CHIP + at, ROWS)
            dst[lo : lo + ROWS, 0:DH] = (k_acc[rows, :] * SCALE).astype(dst.dtype)
            dst[lo : lo + ROWS, DH : 2 * DH] = v_acc[rows, :].astype(dst.dtype)
    for dst in (d_b_ref, d_a_ref):
        dst[CHIP:PACK, :] = own_ref[CHIP:PACK, :]


def row_coefs(starts, ends, coef, first):
    n = starts.shape[1]
    pos = first + lax.broadcasted_iota(jnp.int32, (ROWS, n), 0)
    return jnp.sum(jnp.where((pos >= starts) & (pos < ends), coef, 0.0), axis=1, keepdims=True)


def query_kernel(seq_len, idx_ref, st_ref, ct_ref, docs_ref, more_ref, *refs):
    tail_refs, mine_refs, got_refs = refs[0:5], refs[5:7], refs[7:9]
    out_ref, scale_ref, other_ref = refs[9:12]
    index = idx_ref[0]
    step = pl.program_id(0)

    @pl.when(step == 0)
    def _():
        starts = st_ref[...]
        n = starts.shape[1]
        sums = jnp.zeros((1, n), F32)
        for ref in tail_refs:
            sums = sums + jnp.sum(ref[CHIP:PACK, 0:n].astype(F32), axis=0, keepdims=True)
        size = jnp.maximum(ct_ref[...], 1).astype(F32)
        coef = LOSS_SCALE * 2.0 / (1.0 + jnp.exp(-sums / size)) / (size * (docs_ref[0:1, 0:n] + more_ref[0:1, 0:n]))
        ends = end_row(starts, seq_len)
        for dst, where in ((scale_ref, index), (other_ref, index // 2 * 2 + 1 - index % 2)):
            dst[...] = jnp.broadcast_to(row_coefs(starts, ends, coef, where * ROWS), dst.shape)

    scale = scale_ref[:, 0:1]
    for k, srcs in ((0, mine_refs), (1, got_refs)):
        for j in range(CHUNKS):

            @pl.when(step == (index % 2 + k) % 2 * CHUNKS + j)
            def _():
                out_ref[...] = (srcs[j][...].astype(F32) * scale).astype(BF16)


def key_value_kernel(*refs):
    scale_refs, own_refs, a_refs, b_refs, outs = refs[0:2], refs[2:4], refs[4:6], refs[6:8], refs[8:10]
    for i in range(2):
        rows = slice(i * ROWS, (i + 1) * ROWS)
        scale = scale_refs[i][...]
        for j in range(CHUNKS):
            for k in range(2):
                cols = slice(k * DH, (k + 1) * DH)
                out = own_refs[j][rows, cols] + a_refs[j][rows, cols].astype(F32) + b_refs[j][rows, cols].astype(F32)
                at = (k * CHUNKS + j) * DH
                outs[i][:, at : at + DH] = (out * scale).astype(BF16)


def in_vmem(x):
    return pltpu.with_memory_space_constraint(x, pltpu.VMEM)


def in_hbm(x):
    return pltpu.with_memory_space_constraint(x, pltpu.HBM)


def local(query, key_value, upstream, log_ratio, doc_starts, answer_counts):
    count = lax.axis_size("ctx")
    seq_len = ROWS * count
    index = lax.axis_index("ctx").astype(jnp.int32)
    core = index % 2
    where = index.reshape(1)
    smem = pl.BlockSpec(memory_space=pltpu.SMEM)
    vmem = pl.BlockSpec(memory_space=pltpu.VMEM)

    def moved(value, steps):
        first, last = (max(0, -steps), min(count, count - steps))
        return lax.ppermute(value, "ctx", [(i, i + steps) for i in range(first, last)])

    def swapped(value):
        return lax.ppermute(value, "ctx", [(i, i ^ 1) for i in range(count)])

    def exchanged(value, bit):
        return lax.ppermute(value, "dp", [(i, i ^ bit) for i in range(lax.axis_size("dp"))])

    width = GROUP * DH
    got_lr = swapped(log_ratio)
    got_kv = swapped(key_value[0])
    hbm = pl.BlockSpec(memory_space=pl.ANY)
    half_cols = CHUNKS * width
    slots = doc_starts.shape[1]
    scalars, docs, own_q, own_g, own_kv, ratios, starts, counts = pl.pallas_call(
        early_kernel,
        out_shape=(
            jax.ShapeDtypeStruct((2 + 2 * (CHIP // SUB),), jnp.int32),
            pltpu.VMEM((8, 128), F32),
            pltpu.VMEM((ROWS, half_cols), BF16),
            pltpu.VMEM((ROWS, half_cols), BF16),
            pltpu.VMEM((ROWS, 2 * HK * DH), BF16),
            pltpu.VMEM((1, ROWS), F32),
            pltpu.VMEM((1, slots), jnp.int32),
            pltpu.VMEM((1, slots), jnp.int32),
        ),
        in_specs=[smem] + [hbm] * 3 + [vmem] * 3,
        out_specs=(smem,) + (vmem,) * 7,
        scratch_shapes=[pltpu.SemaphoreType.DMA((3,))],
        compiler_params=pltpu.CompilerParams(vmem_limit_bytes=4 << 20),
        name="early",
    )(where, *[in_hbm(x) for x in (query[0], upstream[0], key_value[0], log_ratio, doc_starts, answer_counts)])
    packed = pltpu.VMEM((PACK, 2 * DH), BF16)
    own = pl.pallas_call(
        partial(pack_kernel, seq_len),
        out_shape=(packed,) * CHUNKS,
        in_specs=[smem] + [vmem] * 6,
        out_specs=(vmem,) * CHUNKS,
        compiler_params=pltpu.CompilerParams(vmem_limit_bytes=4 << 20),
        name="pack",
    )(where, *[in_vmem(x) for x in (own_kv, got_kv, ratios, got_lr, starts, counts)])
    back1, back2 = [], []
    for j in range(CHUNKS):
        back1.append(moved(own[j], 2))
        back2.append(moved(own[j], 4))
    got_q = swapped(query[0])
    got_g = swapped(upstream[0])
    more_docs = exchanged(docs, 1)

    dq_mine, dq_other, d_own, d_a, d_b = [], [], [], [], []
    for j in range(CHUNKS):
        operands = (own_q, own_g, got_q, got_g, own[j], back1[j], back2[j], starts, counts)
        outs = pl.pallas_call(
            partial(attention_kernel, seq_len, j),
            in_specs=[smem] + [vmem] * 9,
            out_specs=[vmem] * 5,
            scratch_shapes=[
                pltpu.VMEM((CHIP, width), BF16),
                pltpu.VMEM((CHIP, width), BF16),
                pltpu.VMEM((WIN, DH), BF16),
                pltpu.VMEM((WIN, DH), BF16),
                pltpu.VMEM((LANES, DH), BF16),
                pltpu.VMEM((LANES, DH), BF16),
                pltpu.VMEM((SPANS[-1], LANES), F32),
                pltpu.VMEM((SPANS[-1], LANES), F32),
                pltpu.VMEM((WIN, DH), F32),
                pltpu.VMEM((WIN, DH), F32),
                pltpu.VMEM((CHIP, width), BF16),
            ],
            out_shape=[
                pltpu.VMEM((ROWS, width), BF16),
                pltpu.VMEM((ROWS, width), BF16),
                pltpu.VMEM((CHIP, 2 * DH), F32),
                pltpu.VMEM((PACK, 2 * DH), BF16),
                pltpu.VMEM((PACK, 2 * DH), BF16),
            ],
            compiler_params=pltpu.CompilerParams(vmem_limit_bytes=24 << 20),
        )(scalars, *[in_vmem(x) for x in operands])
        for kept, out in zip((dq_mine, dq_other, d_own, d_a, d_b), outs):
            kept.append(out)

    got_a, got_b, dq_got = [], [], []
    for j in range(CHUNKS):
        got_a.append(moved(d_a[j], -2))
        got_b.append(moved(d_b[j], -4))
        dq_got.append(swapped(dq_other[j]))
    docs = docs + more_docs
    more_docs = exchanged(docs, 2)
    tails = (own[0], back1[0], back2[0], got_a[0], got_b[0])
    d_query, scale_mine, scale_other = pl.pallas_call(
        partial(query_kernel, seq_len),
        grid=(2 * CHUNKS,),
        out_shape=(
            jax.ShapeDtypeStruct((ROWS, HQ * DH), BF16),
            pltpu.VMEM((ROWS, DH), F32),
            pltpu.VMEM((ROWS, DH), F32),
        ),
        in_specs=[smem] + [vmem] * 13,
        out_specs=(pl.BlockSpec((ROWS, width), lambda i: (0, i)), vmem, vmem),
        compiler_params=pltpu.CompilerParams(vmem_limit_bytes=8 << 20),
        name="q_out",
    )(where, *[in_vmem(x) for x in (starts, counts, docs, more_docs, *tails, *dq_mine, *dq_got)])
    half = pltpu.VMEM((ROWS, 2 * CHUNKS * DH), BF16)
    kv_mine, kv_send = pl.pallas_call(
        key_value_kernel,
        out_shape=(half, half),
        in_specs=[vmem] * 8,
        out_specs=(vmem, vmem),
        compiler_params=pltpu.CompilerParams(vmem_limit_bytes=4 << 20),
        name="kv_out",
    )(*[in_vmem(x) for x in (scale_mine, scale_other, *d_own, *got_a, *got_b)])
    kv_got = swapped(kv_send)
    cut = CHUNKS * DH
    lower, upper = (jnp.where(core == 0, kv_mine, kv_got), jnp.where(core == 0, kv_got, kv_mine))
    d_key_value = jnp.concatenate([lower[:, :cut], upper[:, :cut], lower[:, cut:], upper[:, cut:]], axis=1)
    return (d_query[None], d_key_value[None])


def solution(mesh):
    return jax.shard_map(
        local,
        mesh=mesh,
        in_specs=(
            P("dp", "ctx", None),
            P("dp", "ctx", None),
            P("dp", "ctx", None),
            P("dp", "ctx"),
            P("dp", None),
            P("dp", None),
        ),
        out_specs=(P("dp", "ctx", None), P("dp", "ctx", None)),
        check_vma=False,
    )
```

time: 90.4 us -> 73.6 us (0.81)
  the two profiles are of different devices: /device:TPU:17 before, /device:TPU:27 now
where the time goes in v2:
time: 73.6 us; the launch traced here: 73.2 us
  starting transfers between devices  36.8 us (50%)
  Pallas kernels  20.3 us (28%)
  waiting for transfers between devices  14.5 us (20%)
  other arithmetic  0.83 us (1%)
  between operations  0.78 us (1%)
    ppermute x8, starting transfers between devices, moved(): lax.ppermute(value, 'ctx', [(i, i + steps) for i in range(first, last)])  21.1 us
    pallas_call x2, Pallas kernels, local(): pl.pallas_call(partial(attention_kernel, seq_len, j), in_specs=[smem] + [...  14.8 us
    ppermute x8, waiting for transfers between devices, moved(): lax.ppermute(value, 'ctx', [(i, i + steps) for i in range(first, last)])  9.82 us
    ppermute x2, starting transfers between devices, exchanged(): lax.ppermute(value, 'dp', [(i, i ^ bit) for i in range(lax.axis_size('dp'...  8.97 us
    ppermute x7, starting transfers between devices, swapped(): return lax.ppermute(value, 'ctx', [(i, i ^ 1) for i in range(count)])  6.71 us
    ppermute x7, waiting for transfers between devices, swapped(): return lax.ppermute(value, 'ctx', [(i, i ^ 1) for i in range(count)])  3.72 us
    pallas_call x1, Pallas kernels, local(): pl.pallas_call(early_kernel, out_shape=(jax.ShapeDtypeStruct((2 + 2 * (CH...  2.81 us
    pallas_call x1, Pallas kernels, local(): pl.pallas_call(partial(query_kernel, seq_len), grid=(2 * CHUNKS,), out_sh...  2.24 us
  transfers between devices with their start and end apart: 17, of which 8 were waited for; matrix products, arithmetic and copies ran while one was open for 0% of the time, Pallas kernels for 27%

profile of v2, /device:TPU:27, one launch (start us, length us, event | category | flops | bytes accessed | tf_op | source)
XLA Modules:
  0.0 73.2 jit_solution(1988868986119318050)
XLA Ops:
  0.6 0.8 %collective-permute-start.6 = (bf16[192,4096]{1,0:T(8,128)(2,1)}, bf16[192,4096]{1,0:T(8,128)(2,1)S(1)}, u32[]{:S(2)}, u32[]{:S(2)}) collective-permute-start(bf16[192,4096]{1,0:T(8,128)(2,1)} %bitcast.7), channel_id=1, source_target_pairs={{0,4},{4,0},{8,12},{12,8},{16,20},{20,16},{24,28},{28,24},{32,36},... | collective-permute-start | bytes 4718600 | tf_op jit(solution)/shard_map/ppermute | solution.py:348
  1.4 0.1 collective-permute-start.7
  1.5 0.4 collective-permute-start.2
  1.9 0.1 collective-permute-start.3
  2.0 2.8 %early.1 = (s32[10]{0:T(128)S(1)}, f32[8,128]{1,0:T(8,128)S(1)}, bf16[192,2048]{1,0:T(8,128)(2,1)S(1)}, bf16[192,2048]{1,0:T(8,128)(2,1)S(1)}, bf16[192,1024]{1,...) custom-call(s32[1]{0:T(128)} %bitcast.idx_ref, bf16[192,4096]{1,0:T(8,128)(2,1)} %bitcast.8, ...), custom_call_target="tpu_custom_call" | custom-call | tf_op jit(solution)/shard_map/early/pallas_call | solution.py:359
  4.8 2.6 %collective-permute-done.3.got_lr_ref = f32[1,192]{1,0:T(1,128)S(1)} collective-permute-done((f32[1,192]{1,0:T(1,128)}, f32[1,192]{1,0:T(1,128)S(1)}, u32[]{:S(2)}, u32[]{:S(2)}) %collective-permute-start.3) | collective-permute-done | bytes 800 | tf_op jit(solution)/shard_map/ppermute | solution.py:348
  7.5 0.3 pack.1
  7.8 3.1 %collective-permute-start.4 = (bf16[400,256]{1,0:T(8,128)(2,1)S(1)}, bf16[400,256]{1,0:T(8,128)(2,1)S(1)}, u32[]{:S(2)}, u32[]{:S(2)}) collective-permute-start(bf16[400,256]{1,0:T(8,128)(2,1)S(1)} %get-tuple-element.32.own_ref.refs_0_), channel_id=1, source_target_pairs={{0,8},{4,12},{8,16},{12,20},{16,24},{20,28},{24,32},{28,36},{32,40... | collective-permute-start | bytes 614408 | tf_op jit(solution)/shard_map/ppermute | solution.py:345
  10.9 1.9 %collective-permute-start.5 = (bf16[400,256]{1,0:T(8,128)(2,1)S(1)}, bf16[400,256]{1,0:T(8,128)(2,1)S(1)}, u32[]{:S(2)}, u32[]{:S(2)}) collective-permute-start(bf16[400,256]{1,0:T(8,128)(2,1)S(1)} %get-tuple-element.32.own_ref.refs_0_), channel_id=1, source_target_pairs={{0,16},{4,20},{8,24},{12,28},{16,32},{20,36},{24,40},{28,44},{32,4... | collective-permute-start | bytes 614408 | tf_op jit(solution)/shard_map/ppermute | solution.py:345
  12.8 2.2 %collective-permute-start.10 = (bf16[400,256]{1,0:T(8,128)(2,1)S(1)}, bf16[400,256]{1,0:T(8,128)(2,1)S(1)}, u32[]{:S(2)}, u32[]{:S(2)}) collective-permute-start(bf16[400,256]{1,0:T(8,128)(2,1)S(1)} %get-tuple-element.39.own_ref), channel_id=1, source_target_pairs={{0,8},{4,12},{8,16},{12,20},{16,24},{20,28},{24,32},{28,36},{32,40... | collective-permute-start | bytes 614408 | tf_op jit(solution)/shard_map/ppermute | solution.py:345
  15.0 0.9 %collective-permute-done.4.a_ref.refs_1_ = bf16[400,256]{1,0:T(8,128)(2,1)S(1)} collective-permute-done((bf16[400,256]{1,0:T(8,128)(2,1)S(1)}, bf16[400,256]{1,0:T(8,128)(2,1)S(1)}, u32[]{:S(2)}, u32[]{:S(2)}) %collective-permute-start.4) | collective-permute-done | bytes 204832 | tf_op jit(solution)/shard_map/ppermute | solution.py:345
  15.9 3.7 %collective-permute-start.11 = (bf16[400,256]{1,0:T(8,128)(2,1)S(1)}, bf16[400,256]{1,0:T(8,128)(2,1)S(1)}, u32[]{:S(2)}, u32[]{:S(2)}) collective-permute-start(bf16[400,256]{1,0:T(8,128)(2,1)S(1)} %get-tuple-element.39.own_ref), channel_id=1, source_target_pairs={{0,16},{4,20},{8,24},{12,28},{16,32},{20,36},{24,40},{28,44},{32,4... | collective-permute-start | bytes 614408 | tf_op jit(solution)/shard_map/ppermute | solution.py:345
  19.7 1.5 %collective-permute-done.5.b_ref.refs_2_ = bf16[400,256]{1,0:T(8,128)(2,1)S(1)} collective-permute-done((bf16[400,256]{1,0:T(8,128)(2,1)S(1)}, bf16[400,256]{1,0:T(8,128)(2,1)S(1)}, u32[]{:S(2)}, u32[]{:S(2)}) %collective-permute-start.5) | collective-permute-done | bytes 204832 | tf_op jit(solution)/shard_map/ppermute | solution.py:345
  21.2 7.4 %shard_map.77 = (bf16[192,1024]{1,0:T(8,128)(2,1)S(1)}, bf16[192,1024]{1,0:T(8,128)(2,1)S(1)}, f32[384,256]{1,0:T(8,128)S(1)}, bf16[400,256]{1,0:T(8,128)(2,1)S(1)}, bf16[400,256]{1,0:T(8,128)(2,1)S(1)}) custom-call(s32[10]{0:T(128)S(1)} %get-tuple-element.33.sc_ref, bf16[192,2048]{1,0:T(8,128)(2,1)S(1)} %get-tuple-element.34.q_ref, ...), custom_call_target="tpu_custom_call" | custom-call | tf_op jit(solution)/shard_map/pallas_call | solution.py:397
  28.5 2.1 %collective-permute-start.8 = (bf16[400,256]{1,0:T(8,128)(2,1)S(1)}, bf16[400,256]{1,0:T(8,128)(2,1)S(1)}, u32[]{:S(2)}, u32[]{:S(2)}) collective-permute-start(bf16[400,256]{1,0:T(8,128)(2,1)S(1)} %get-tuple-element.36), channel_id=1, source_target_pairs={{8,0},{12,4},{16,8},{20,12},{24,16},{28,20},{32,24},{36,28},{40,32... | collective-permute-start | bytes 614408 | tf_op jit(solution)/shard_map/ppermute | solution.py:345
  30.7 7.4 %shard_map.78 = (bf16[192,1024]{1,0:T(8,128)(2,1)S(1)}, bf16[192,1024]{1,0:T(8,128)(2,1)S(1)}, f32[384,256]{1,0:T(8,128)S(1)}, bf16[400,256]{1,0:T(8,128)(2,1)S(1)}, bf16[400,256]{1,0:T(8,128)(2,1)S(1)}) custom-call(s32[10]{0:T(128)S(1)} %get-tuple-element.33.sc_ref, bf16[192,2048]{1,0:T(8,128)(2,1)S(1)} %get-tuple-element.34.q_ref, ...), custom_call_target="tpu_custom_call" | custom-call | tf_op jit(solution)/shard_map/pallas_call | solution.py:397
  38.1 3.3 %collective-permute-start.13 = (bf16[192,1024]{1,0:T(8,128)(2,1)S(1)}, bf16[192,1024]{1,0:T(8,128)(2,1)S(1)}, u32[]{:S(2)}, u32[]{:S(2)}) collective-permute-start(bf16[192,1024]{1,0:T(8,128)(2,1)S(1)} %get-tuple-element.42), channel_id=1, source_target_pairs={{0,4},{4,0},{8,12},{12,8},{16,20},{20,16},{24,28},{28,24},{32,36},... | collective-permute-start | bytes 1179656 | tf_op jit(solution)/shard_map/ppermute | solution.py:348
  41.3 0.1 collective-permute-start.12
  41.4 2.6 %collective-permute-start = (f32[8,128]{1,0:T(8,128)S(1)}, f32[8,128]{1,0:T(8,128)S(1)}, u32[]{:S(2)}, u32[]{:S(2)}) collective-permute-start(f32[8,128]{1,0:T(8,128)S(1)} %get-tuple-element.29), channel_id=1, source_target_pairs={{0,1},{1,0},{2,3},{3,2},{4,5},{5,4},{6,7},{7,6},{8,9},{9,8},{10,11... | collective-permute-start | bytes 12296 | tf_op jit(solution)/shard_map/ppermute | solution.py:351
  44.0 1.0 %collective-permute-done = f32[8,128]{1,0:T(8,128)S(1)} collective-permute-done((f32[8,128]{1,0:T(8,128)S(1)}, f32[8,128]{1,0:T(8,128)S(1)}, u32[]{:S(2)}, u32[]{:S(2)}) %collective-permute-start) | collective-permute-done | bytes 4128 | tf_op jit(solution)/shard_map/ppermute | solution.py:351
  45.0 6.4 %collective-permute-start.1 = (f32[8,128]{1,0:T(8,128)S(1)}, f32[8,128]{1,0:T(8,128)S(1)}, u32[]{:S(2)}, u32[]{:S(2)}) collective-permute-start(f32[8,128]{1,0:T(8,128)S(1)} %add.7.docs_ref), channel_id=1, source_target_pairs={{0,2},{1,3},{2,0},{3,1},{4,6},{5,7},{6,4},{7,5},{8,10},{9,11},{10,... | collective-permute-start | bytes 12296 | tf_op jit(solution)/shard_map/ppermute | solution.py:351
  51.4 1.9 %collective-permute-start.9 = (bf16[400,256]{1,0:T(8,128)(2,1)S(1)}, bf16[400,256]{1,0:T(8,128)(2,1)S(1)}, u32[]{:S(2)}, u32[]{:S(2)}) collective-permute-start(bf16[400,256]{1,0:T(8,128)(2,1)S(1)} %get-tuple-element.37), channel_id=1, source_target_pairs={{16,0},{20,4},{24,8},{28,12},{32,16},{36,20},{40,24},{44,28},{48,3... | collective-permute-start | bytes 614408 | tf_op jit(solution)/shard_map/ppermute | solution.py:345
  53.3 4.2 %collective-permute-start.14 = (bf16[400,256]{1,0:T(8,128)(2,1)S(1)}, bf16[400,256]{1,0:T(8,128)(2,1)S(1)}, u32[]{:S(2)}, u32[]{:S(2)}) collective-permute-start(bf16[400,256]{1,0:T(8,128)(2,1)S(1)} %get-tuple-element.48), channel_id=1, source_target_pairs={{8,0},{12,4},{16,8},{20,12},{24,16},{28,20},{32,24},{36,28},{40,32... | collective-permute-start | bytes 614408 | tf_op jit(solution)/shard_map/ppermute | solution.py:345
  57.5 1.9 %collective-permute-start.15 = (bf16[400,256]{1,0:T(8,128)(2,1)S(1)}, bf16[400,256]{1,0:T(8,128)(2,1)S(1)}, u32[]{:S(2)}, u32[]{:S(2)}) collective-permute-start(bf16[400,256]{1,0:T(8,128)(2,1)S(1)} %get-tuple-element.49), channel_id=1, source_target_pairs={{16,0},{20,4},{24,8},{28,12},{32,16},{36,20},{40,24},{44,28},{48,3... | collective-permute-start | bytes 614408 | tf_op jit(solution)/shard_map/ppermute | solution.py:345
  59.4 0.4 collective-permute-done.9.refs_4_.refs_6_
  59.8 2.2 %q_out.1 = (bf16[192,4096]{1,0:T(8,128)(2,1)}, f32[192,128]{1,0:T(8,128)S(1)}, f32[192,128]{1,0:T(8,128)S(1)}) custom-call(s32[1]{0:T(128)} %bitcast.idx_ref, s32[1,64]{1,0:T(1,128)S(1)} %get-tuple-element.27.st_ref, s32[1,64]{1,0:T(1,128)S(1)} %get-tuple-element.28.ct_ref, f32[8,128]{1,0:T(8,128)S(1)} %add.7.docs_ref, ...), custom_call_target="tpu_custom_call" | custom-call | tf_op jit(solution)/shard_map/q_out/pallas_call | solution.py:434
  62.1 4.8 %collective-permute-done.14.refs_5_ = bf16[400,256]{1,0:T(8,128)(2,1)S(1)} collective-permute-done((bf16[400,256]{1,0:T(8,128)(2,1)S(1)}, bf16[400,256]{1,0:T(8,128)(2,1)S(1)}, u32[]{:S(2)}, u32[]{:S(2)}) %collective-permute-start.14) | collective-permute-done | bytes 204832 | tf_op jit(solution)/shard_map/ppermute | solution.py:345
  66.9 2.2 %collective-permute-done.15.refs_7_ = bf16[400,256]{1,0:T(8,128)(2,1)S(1)} collective-permute-done((bf16[400,256]{1,0:T(8,128)(2,1)S(1)}, bf16[400,256]{1,0:T(8,128)(2,1)S(1)}, u32[]{:S(2)}, u32[]{:S(2)}) %collective-permute-start.15) | collective-permute-done | bytes 204832 | tf_op jit(solution)/shard_map/ppermute | solution.py:345
  69.1 0.2 kv_out.1
  69.3 2.0 %collective-permute-start.16 = (bf16[192,512]{1,0:T(8,128)(2,1)S(1)}, bf16[192,512]{1,0:T(8,128)(2,1)S(1)}, u32[]{:S(2)}, u32[]{:S(2)}) collective-permute-start(bf16[192,512]{1,0:T(8,128)(2,1)S(1)} %get-tuple-element.51), channel_id=1, source_target_pairs={{0,4},{4,0},{8,12},{12,8},{16,20},{20,16},{24,28},{28,24},{32,36},... | collective-permute-start | bytes 589832 | tf_op jit(solution)/shard_map/ppermute | solution.py:348
  71.3 1.1 %collective-permute-done.16 = bf16[192,512]{1,0:T(8,128)(2,1)S(1)} collective-permute-done((bf16[192,512]{1,0:T(8,128)(2,1)S(1)}, bf16[192,512]{1,0:T(8,128)(2,1)S(1)}, u32[]{:S(2)}, u32[]{:S(2)}) %collective-permute-start.16) | collective-permute-done | bytes 196640 | tf_op jit(solution)/shard_map/ppermute | solution.py:348
  72.4 0.8 %maximum_bitcast_fusion = bf16[1,192,1024]{2,1,0:T(8,128)(2,1)} fusion(bf16[192,256]{1,0:T(8,128)(2,1)S(1)} %get-tuple-element.58, bf16[192,256]{1,0:T(8,128)(2,1)S(1)} %get-tuple-element.55, bf16[192,256]{1,0:T(8,128)(2,1)S(1)} %get-tuple-element.59, bf16[192,256]{1,0:T(8,128)(2,1)S(1)} %get-tuple-element.54), kind=kLoop, calls=%fused_computation | loop fusion | flops 1572864 | bytes 786432 | tf_op jit(solution)/shard_map/broadcast_in_dim | solution.py:460
  (12 shorter events, 0.1 us)
Async XLA Ops:
  0.6 20.5 %collective-permute-start.6 = (bf16[192,4096]{1,0:T(8,128)(2,1)}, bf16[192,4096]{1,0:T(8,128)(2,1)S(1)}, u32[]{:S(2)}, u32[]{:S(2)}) collective-permute-start(bf16[192,4096]{1,0:T(8,128)(2,1)} %bitcast.7), channel_id=1, source_target_pairs={{0,4},{4,0},{8,12},{12,8},{16,20},{20,16},{24,28},{28,24},{32,36},... | collective-permute-start | bytes 4718600 | tf_op jit(solution)/shard_map/ppermute | solution.py:348
  1.4 19.8 %collective-permute-start.7 = (bf16[192,4096]{1,0:T(8,128)(2,1)}, bf16[192,4096]{1,0:T(8,128)(2,1)S(1)}, u32[]{:S(2)}, u32[]{:S(2)}) collective-permute-start(bf16[192,4096]{1,0:T(8,128)(2,1)} %bitcast.9), channel_id=1, source_target_pairs={{0,4},{4,0},{8,12},{12,8},{16,20},{20,16},{24,28},{28,24},{32,36},... | collective-permute-start | bytes 4718600 | tf_op jit(solution)/shard_map/ppermute | solution.py:348
  1.5 6.0 %collective-permute-start.2 = (bf16[192,1024]{1,0:T(8,128)(2,1)}, bf16[192,1024]{1,0:T(8,128)(2,1)S(1)}, u32[]{:S(2)}, u32[]{:S(2)}) collective-permute-start(bf16[192,1024]{1,0:T(8,128)(2,1)} %bitcast.11), channel_id=1, source_target_pairs={{0,4},{4,0},{8,12},{12,8},{16,20},{20,16},{24,28},{28,24},{32,36},... | collective-permute-start | bytes 1179656 | tf_op jit(solution)/shard_map/ppermute | solution.py:348
  1.9 5.5 %collective-permute-start.3 = (f32[1,192]{1,0:T(1,128)}, f32[1,192]{1,0:T(1,128)S(1)}, u32[]{:S(2)}, u32[]{:S(2)}) collective-permute-start(f32[1,192]{1,0:T(1,128)} %lr_ref.1), channel_id=1, source_target_pairs={{0,4},{4,0},{8,12},{12,8},{16,20},{20,16},{24,28},{28,24},{32,36},... | collective-permute-start | bytes 2312 | tf_op jit(solution)/shard_map/ppermute | solution.py:348
  7.8 8.2 %collective-permute-start.4 = (bf16[400,256]{1,0:T(8,128)(2,1)S(1)}, bf16[400,256]{1,0:T(8,128)(2,1)S(1)}, u32[]{:S(2)}, u32[]{:S(2)}) collective-permute-start(bf16[400,256]{1,0:T(8,128)(2,1)S(1)} %get-tuple-element.32.own_ref.refs_0_), channel_id=1, source_target_pairs={{0,8},{4,12},{8,16},{12,20},{16,24},{20,28},{24,32},{28,36},{32,40... | collective-permute-start | bytes 614408 | tf_op jit(solution)/shard_map/ppermute | solution.py:345
  10.9 10.3 %collective-permute-start.5 = (bf16[400,256]{1,0:T(8,128)(2,1)S(1)}, bf16[400,256]{1,0:T(8,128)(2,1)S(1)}, u32[]{:S(2)}, u32[]{:S(2)}) collective-permute-start(bf16[400,256]{1,0:T(8,128)(2,1)S(1)} %get-tuple-element.32.own_ref.refs_0_), channel_id=1, source_target_pairs={{0,16},{4,20},{8,24},{12,28},{16,32},{20,36},{24,40},{28,44},{32,4... | collective-permute-start | bytes 614408 | tf_op jit(solution)/shard_map/ppermute | solution.py:345
  12.8 17.8 %collective-permute-start.10 = (bf16[400,256]{1,0:T(8,128)(2,1)S(1)}, bf16[400,256]{1,0:T(8,128)(2,1)S(1)}, u32[]{:S(2)}, u32[]{:S(2)}) collective-permute-start(bf16[400,256]{1,0:T(8,128)(2,1)S(1)} %get-tuple-element.39.own_ref), channel_id=1, source_target_pairs={{0,8},{4,12},{8,16},{12,20},{16,24},{20,28},{24,32},{28,36},{32,40... | collective-permute-start | bytes 614408 | tf_op jit(solution)/shard_map/ppermute | solution.py:345
  15.9 14.8 %collective-permute-start.11 = (bf16[400,256]{1,0:T(8,128)(2,1)S(1)}, bf16[400,256]{1,0:T(8,128)(2,1)S(1)}, u32[]{:S(2)}, u32[]{:S(2)}) collective-permute-start(bf16[400,256]{1,0:T(8,128)(2,1)S(1)} %get-tuple-element.39.own_ref), channel_id=1, source_target_pairs={{0,16},{4,20},{8,24},{12,28},{16,32},{20,36},{24,40},{28,44},{32,4... | collective-permute-start | bytes 614408 | tf_op jit(solution)/shard_map/ppermute | solution.py:345
  28.5 29.0 %collective-permute-start.8 = (bf16[400,256]{1,0:T(8,128)(2,1)S(1)}, bf16[400,256]{1,0:T(8,128)(2,1)S(1)}, u32[]{:S(2)}, u32[]{:S(2)}) collective-permute-start(bf16[400,256]{1,0:T(8,128)(2,1)S(1)} %get-tuple-element.36), channel_id=1, source_target_pairs={{8,0},{12,4},{16,8},{20,12},{24,16},{28,20},{32,24},{36,28},{40,32... | collective-permute-start | bytes 614408 | tf_op jit(solution)/shard_map/ppermute | solution.py:345
  38.1 21.8 %collective-permute-start.13 = (bf16[192,1024]{1,0:T(8,128)(2,1)S(1)}, bf16[192,1024]{1,0:T(8,128)(2,1)S(1)}, u32[]{:S(2)}, u32[]{:S(2)}) collective-permute-start(bf16[192,1024]{1,0:T(8,128)(2,1)S(1)} %get-tuple-element.42), channel_id=1, source_target_pairs={{0,4},{4,0},{8,12},{12,8},{16,20},{20,16},{24,28},{28,24},{32,36},... | collective-permute-start | bytes 1179656 | tf_op jit(solution)/shard_map/ppermute | solution.py:348
  41.3 18.5 %collective-permute-start.12 = (bf16[192,1024]{1,0:T(8,128)(2,1)S(1)}, bf16[192,1024]{1,0:T(8,128)(2,1)S(1)}, u32[]{:S(2)}, u32[]{:S(2)}) collective-permute-start(bf16[192,1024]{1,0:T(8,128)(2,1)S(1)} %get-tuple-element.41), channel_id=1, source_target_pairs={{0,4},{4,0},{8,12},{12,8},{16,20},{20,16},{24,28},{28,24},{32,36},... | collective-permute-start | bytes 1179656 | tf_op jit(solution)/shard_map/ppermute | solution.py:348
  41.4 3.6 %collective-permute-start = (f32[8,128]{1,0:T(8,128)S(1)}, f32[8,128]{1,0:T(8,128)S(1)}, u32[]{:S(2)}, u32[]{:S(2)}) collective-permute-start(f32[8,128]{1,0:T(8,128)S(1)} %get-tuple-element.29), channel_id=1, source_target_pairs={{0,1},{1,0},{2,3},{3,2},{4,5},{5,4},{6,7},{7,6},{8,9},{9,8},{10,11... | collective-permute-start | bytes 12296 | tf_op jit(solution)/shard_map/ppermute | solution.py:351
  45.0 8.3 %collective-permute-start.1 = (f32[8,128]{1,0:T(8,128)S(1)}, f32[8,128]{1,0:T(8,128)S(1)}, u32[]{:S(2)}, u32[]{:S(2)}) collective-permute-start(f32[8,128]{1,0:T(8,128)S(1)} %add.7.docs_ref), channel_id=1, source_target_pairs={{0,2},{1,3},{2,0},{3,1},{4,6},{5,7},{6,4},{7,5},{8,10},{9,11},{10,... | collective-permute-start | bytes 12296 | tf_op jit(solution)/shard_map/ppermute | solution.py:351
  51.4 8.5 %collective-permute-start.9 = (bf16[400,256]{1,0:T(8,128)(2,1)S(1)}, bf16[400,256]{1,0:T(8,128)(2,1)S(1)}, u32[]{:S(2)}, u32[]{:S(2)}) collective-permute-start(bf16[400,256]{1,0:T(8,128)(2,1)S(1)} %get-tuple-element.37), channel_id=1, source_target_pairs={{16,0},{20,4},{24,8},{28,12},{32,16},{36,20},{40,24},{44,28},{48,3... | collective-permute-start | bytes 614408 | tf_op jit(solution)/shard_map/ppermute | solution.py:345
  53.3 13.6 %collective-permute-start.14 = (bf16[400,256]{1,0:T(8,128)(2,1)S(1)}, bf16[400,256]{1,0:T(8,128)(2,1)S(1)}, u32[]{:S(2)}, u32[]{:S(2)}) collective-permute-start(bf16[400,256]{1,0:T(8,128)(2,1)S(1)} %get-tuple-element.48), channel_id=1, source_target_pairs={{8,0},{12,4},{16,8},{20,12},{24,16},{28,20},{32,24},{36,28},{40,32... | collective-permute-start | bytes 614408 | tf_op jit(solution)/shard_map/ppermute | solution.py:345
  57.5 11.6 %collective-permute-start.15 = (bf16[400,256]{1,0:T(8,128)(2,1)S(1)}, bf16[400,256]{1,0:T(8,128)(2,1)S(1)}, u32[]{:S(2)}, u32[]{:S(2)}) collective-permute-start(bf16[400,256]{1,0:T(8,128)(2,1)S(1)} %get-tuple-element.49), channel_id=1, source_target_pairs={{16,0},{20,4},{24,8},{28,12},{32,16},{36,20},{40,24},{44,28},{48,3... | collective-permute-start | bytes 614408 | tf_op jit(solution)/shard_map/ppermute | solution.py:345
  69.3 3.1 %collective-permute-start.16 = (bf16[192,512]{1,0:T(8,128)(2,1)S(1)}, bf16[192,512]{1,0:T(8,128)(2,1)S(1)}, u32[]{:S(2)}, u32[]{:S(2)}) collective-permute-start(bf16[192,512]{1,0:T(8,128)(2,1)S(1)} %get-tuple-element.51), channel_id=1, source_target_pairs={{0,4},{4,0},{8,12},{12,8},{16,20},{20,16},{24,28},{28,24},{32,36},... | collective-permute-start | bytes 589832 | tf_op jit(solution)/shard_map/ppermute | solution.py:348

commit v3 on v2

v3 whole, which is shorter than its diff:
```python
from functools import partial

import jax
import jax.numpy as jnp
from jax import lax
from jax.experimental import pallas as pl
from jax.experimental.pallas import tpu as pltpu
from jax.sharding import PartitionSpec as P


HQ = 32
HK = 4
DH = 128
LOSS_SCALE = 65536
ROWS = 192
CHIP = 2 * ROWS
WIN = 3 * CHIP
GROUP = HQ // HK
SUB = 96
LANES = SUB * GROUP
SPANS = (256, 512, 640, 704, 784, 896)
CHUNKS = 2
TAIL = 16
PACK = CHIP + TAIL
MASKED = -1e30
SCALE = DH ** (-0.5)
LOG2E = 1.4426950408889634
HALVES = 1
PART = LANES // HALVES
SHARED = 384
F32 = jnp.float32
BF16 = jnp.bfloat16


def to_column(row, shift=0):
    n = row.shape[1]
    r = lax.broadcasted_iota(jnp.int32, (n, n), 0)
    c = lax.broadcasted_iota(jnp.int32, (n, n), 1)
    return jnp.sum(jnp.where(c == r + shift, row, 0), axis=1, keepdims=True)


def end_row(starts, seq_len):
    n = starts.shape[1]
    r = lax.broadcasted_iota(jnp.int32, (n, n), 0)
    c = lax.broadcasted_iota(jnp.int32, (n, n), 1)
    col = to_column(starts)
    row = jnp.sum(jnp.where(r == c + 1, col, 0), axis=0, keepdims=True)
    lane = lax.broadcasted_iota(jnp.int32, (1, n), 1)
    return jnp.where(lane == n - 1, seq_len, row)


def pack_kernel(seq_len, idx_ref, kv_ref, got_ref, lr_ref, got_lr_ref, st_ref, ct_ref, *own_refs):
    index = idx_ref[0]
    core = index % 2
    for half in range(2):

        @pl.when(core == half)
        def _():
            for j in range(CHUNKS):
                for k in range(2):
                    lo = k * HK * DH + (half * CHUNKS + j) * DH
                    own_refs[j][0:ROWS, k * DH : (k + 1) * DH] = kv_ref[:, lo : lo + DH]
                    own_refs[j][ROWS:CHIP, k * DH : (k + 1) * DH] = got_ref[:, lo : lo + DH]

    starts = st_ref[...]
    n = starts.shape[1]
    row_i = lax.broadcasted_iota(jnp.int32, (n, 1), 0)
    st = to_column(starts)
    en = jnp.where(row_i == n - 1, seq_len, to_column(starts, 1))
    first = jnp.maximum(st, en - to_column(ct_ref[...]))
    lane = lax.broadcasted_iota(jnp.int32, (n, ROWS), 1)
    part = jnp.zeros((n, 1), F32)
    for ref, where in ((lr_ref, index), (got_lr_ref, index + 1 - 2 * core)):
        pos = where * ROWS + lane
        part = part + jnp.sum(jnp.where((pos >= first) & (pos < en), ref[...], 0.0), axis=1, keepdims=True)
    r = lax.broadcasted_iota(jnp.int32, (n, n), 0)
    c = lax.broadcasted_iota(jnp.int32, (n, n), 1)
    part = jnp.sum(jnp.where(r == c, part, 0.0), axis=0, keepdims=True)
    high = part.astype(BF16).astype(F32)
    rest = part - high
    mid = rest.astype(BF16).astype(F32)
    low = rest - mid
    k = lax.broadcasted_iota(jnp.int32, (TAIL, n), 0)
    tail = jnp.where(k == 0, high, jnp.where(k == 1, mid, jnp.where(k == 2, low, 0.0))).astype(BF16)
    for ref in own_refs:
        ref[CHIP:PACK, :] = jnp.zeros((TAIL, 2 * DH), BF16)
    own_refs[0][CHIP:PACK, 0:n] = tail


def early_kernel(kv_hbm, lr_ref, st_ref, ct_ref, kv_ref, lr_out, st_out, ct_out, sem):
    copy = pltpu.make_async_copy(kv_hbm, kv_ref, sem)
    copy.start()
    lr_out[...] = lr_ref[...]
    st_out[...] = st_ref[...]
    ct_out[...] = ct_ref[...]
    copy.wait()


def join_kernel(seq_len, idx_ref, q_hbm, g_hbm, got_q_ref, got_g_ref, st_ref, ct_ref, sc_ref, cnt_ref, q_all, g_all, sems):
    core = idx_ref[0] % 2
    width = q_all.shape[1]
    cols = pl.ds(pl.multiple_of(core * width, width), width)
    mine = pl.ds(pl.multiple_of(core * ROWS, ROWS), ROWS)
    other = pl.ds(pl.multiple_of((1 - core) * ROWS, ROWS), ROWS)
    copies = [
        pltpu.make_async_copy(q_hbm.at[:, cols], q_all.at[mine], sems.at[0]),
        pltpu.make_async_copy(g_hbm.at[:, cols], g_all.at[mine], sems.at[1]),
    ]
    for copy in copies:
        copy.start()
    index = idx_ref[0]
    first = index // 2 * CHIP
    base = first - (WIN - CHIP)
    sc_ref[0] = index % 2
    sc_ref[1] = base
    starts = st_ref[...].astype(F32)
    for s in range(CHIP // SUB):
        at = (first + s * SUB).astype(F32)
        start = jnp.max(jnp.where(starts <= at, starts, 0.0)).astype(jnp.int32)
        low = jnp.maximum(start - base, 0) // 16 * 16
        need = (WIN - CHIP) + (s + 1) * SUB - low
        pick = jnp.int32(0)
        span = jnp.int32(SPANS[0])
        for v in range(1, len(SPANS)):
            more = need > SPANS[v - 1]
            pick = jnp.where(more, v, pick)
            span = jnp.where(more, SPANS[v], span)
        sc_ref[2 + 2 * s] = jnp.minimum(low, WIN - span)
        sc_ref[3 + 2 * s] = pick
    used = jnp.sum(jnp.where(ct_ref[...] > 0, 1.0, 0.0), axis=1, keepdims=True)
    cnt_ref[...] = jnp.broadcast_to(used, cnt_ref.shape)
    slots = st_ref[...]
    ends = end_row(slots, seq_len)
    first_answer = jnp.maximum(slots, ends - ct_ref[...])

    def answers(where):
        pos = where * ROWS + lax.broadcasted_iota(jnp.int32, (ROWS, slots.shape[1]), 0)
        hit = jnp.where((pos >= first_answer) & (pos < ends), 1.0, 0.0)
        return jnp.sum(hit, axis=1, keepdims=True) > 0.5

    q_all[other, :] = got_q_ref[:, cols]
    g_all[other, :] = jnp.where(answers(index + 1 - 2 * core), got_g_ref[:, cols], jnp.zeros((), BF16))
    kept = answers(index)
    for copy in copies:
        copy.wait()
    g_all[mine, :] = jnp.where(kept, g_all[mine, :], jnp.zeros((), BF16))


def nt(a, b):
    return lax.dot_general(a, b, (((1,), (1,)), ((), ())), preferred_element_type=F32)


def nn(a, b):
    return lax.dot_general(a, b, (((1,), (0,)), ((), ())), preferred_element_type=F32)


def tn(a, b):
    return lax.dot_general(a, b, (((0,), (0,)), ((), ())), preferred_element_type=F32)


def fold(x, op):
    out = x[0:8]
    for i in range(8, x.shape[0], 8):
        out = op(out, x[i : i + 8])
    return out


def attention_kernel(chunk, sc_ref, q_all, g_all, own_ref, a_ref, b_ref, st_ref, *refs):
    refs = refs[1:] if chunk else refs
    dq_own_ref, dq_other_ref, d_own_ref, d_a_ref, d_b_ref, *refs = refs
    k_all, v_all, q_now, g_now, s_buf, d_buf, k_acc, v_acc, dq_now, dq_all = refs
    core = sc_ref[0]
    base = sc_ref[1]
    mine = pl.multiple_of(core * ROWS, ROWS)
    other = pl.multiple_of((1 - core) * ROWS, ROWS)
    width = GROUP * DH
    for i, src in enumerate((b_ref, a_ref, own_ref)):
        for at, lo in ((mine, 0), (other, ROWS)):
            rows = pl.ds(i * CHIP + at, ROWS)
            k_all[rows, :] = src[lo : lo + ROWS, 0:DH]
            v_all[rows, :] = src[lo : lo + ROWS, DH : 2 * DH]
    k_acc[...] = jnp.zeros(k_acc.shape, F32)
    v_acc[...] = jnp.zeros(v_acc.shape, F32)
    starts = st_ref[...]
    st_col = to_column(starts)

    def flush(row_first):
        done = dq_now[...].T
        for h in range(GROUP):
            dq_all[pl.ds(row_first, SUB), h * DH : (h + 1) * DH] = done[h * SUB : (h + 1) * SUB].astype(BF16)

    def span_step(span, key_first, row_first, low, pos):
        pieces = [(o, min(256, span - o)) for o in range(0, span, 256)]
        flush(row_first)
        state = [{} for _ in range(HALVES)]

        def rows_of(o, size):
            return pl.ds(pl.multiple_of(key_first + o, 16), size)

        def score(i, o, size):
            part = slice(i * PART, (i + 1) * PART)
            scores = nt(k_all[rows_of(o, size), :], q_now[part, :])
            key_pos = base + key_first + o + lax.broadcasted_iota(jnp.int32, (size, SHARED), 0)
            seen = (key_pos >= low) & (key_pos <= pos)
            scores = jnp.where(jnp.concatenate([seen] * (PART // SHARED), axis=1), scores, MASKED)
            s_buf[o : o + size, part] = scores
            top = fold(scores, jnp.maximum)
            state[i]["top"] = top if o == 0 else jnp.maximum(state[i]["top"], top)

        def weigh(i, o, size):
            part = slice(i * PART, (i + 1) * PART)
            if o == 0:
                state[i]["peak"] = jnp.max(state[i]["top"], axis=0, keepdims=True) * (SCALE * LOG2E)
            d_probs = nt(v_all[rows_of(o, size), :], g_now[part, :])
            weight = jnp.exp2(s_buf[o : o + size, part] * (SCALE * LOG2E) - state[i]["peak"])
            s_buf[o : o + size, part] = weight
            d_buf[o : o + size, part] = d_probs
            total = fold(weight, jnp.add)
            delta = fold(weight * d_probs, jnp.add)
            state[i]["total"] = total if o == 0 else state[i]["total"] + total
            state[i]["delta"] = delta if o == 0 else state[i]["delta"] + delta

        def finish(i, o, size):
            part = slice(i * PART, (i + 1) * PART)
            if o == 0:
                inverse = 1.0 / jnp.sum(state[i]["total"], axis=0, keepdims=True)
                state[i]["inverse"] = inverse
                state[i]["delta"] = jnp.sum(state[i]["delta"], axis=0, keepdims=True) * inverse
            rows = rows_of(o, size)
            probs = s_buf[o : o + size, part] * state[i]["inverse"]
            d_scores = (probs * (d_buf[o : o + size, part] - state[i]["delta"])).astype(BF16)
            v_acc[rows, :] += nn(probs.astype(BF16), g_now[part, :])
            k_acc[rows, :] += nn(d_scores, q_now[part, :])
            dq = tn(k_all[rows, :], d_scores)
            state[i]["dq"] = dq if o == 0 else state[i]["dq"] + dq

        stages = (score, weigh, finish)
        for t in range(len(stages) + HALVES - 1):
            for o, size in pieces:
                for i in range(HALVES):
                    if 0 <= t - i < len(stages):
                        stages[t - i](i, o, size)
        for i in range(HALVES):
            dq_now[:, i * PART : (i + 1) * PART] = state[i]["dq"] * SCALE

    def step(s, carry):
        key_first = pl.multiple_of(sc_ref[2 + 2 * s], 16)
        pick = sc_ref[3 + 2 * s]
        row_first = pl.multiple_of(s * SUB, SUB)
        for h in range(GROUP):
            col = chunk * width + h * DH
            q_now[h * SUB : (h + 1) * SUB, :] = q_all[pl.ds(row_first, SUB), col : col + DH]
            g_now[h * SUB : (h + 1) * SUB, :] = g_all[pl.ds(row_first, SUB), col : col + DH]
        lane = lax.broadcasted_iota(jnp.int32, (1, SHARED), 1)
        pos = base + (WIN - CHIP) + row_first + lane % SUB
        low = jnp.max(jnp.where(st_col <= pos, st_col, 0), axis=0, keepdims=True)
        for v, span in enumerate(SPANS):
            pl.when(pick == v)(partial(span_step, span, key_first, row_first, low, pos))
        return carry

    lax.fori_loop(0, CHIP // SUB, step, 0)
    flush(CHIP)
    dq_own_ref[...] = dq_all[pl.ds(SUB + mine, ROWS), :]
    dq_other_ref[:, chunk * width : (chunk + 1) * width] = dq_all[pl.ds(SUB + other, ROWS), :]
    for i, dst in enumerate((d_b_ref, d_a_ref, d_own_ref)):
        for at, lo in ((mine, 0), (other, ROWS)):
            rows = pl.ds(i * CHIP + at, ROWS)
            dst[lo : lo + ROWS, 0:DH] = (k_acc[rows, :] * SCALE).astype(dst.dtype)
            dst[lo : lo + ROWS, DH : 2 * DH] = v_acc[rows, :].astype(dst.dtype)
    d_b_ref[CHIP:PACK, 0:DH] = own_ref[CHIP:PACK, 0:DH]
    d_b_ref[CHIP:PACK, DH : 2 * DH] = a_ref[CHIP:PACK, 0:DH]


def row_coefs(starts, ends, coef, first):
    n = starts.shape[1]
    pos = first + lax.broadcasted_iota(jnp.int32, (ROWS, n), 0)
    return jnp.sum(jnp.where((pos >= starts) & (pos < ends), coef, 0.0), axis=1, keepdims=True)


def query_kernel(seq_len, idx_ref, st_ref, ct_ref, docs_ref, more_ref, *refs):
    tail_refs, mine_refs, got_ref = refs[0:4], refs[4:6], refs[6]
    out_ref, scale_ref, other_ref = refs[7:10]
    index = idx_ref[0]
    step = pl.program_id(0)

    @pl.when(step == 0)
    def _():
        starts = st_ref[...]
        n = starts.shape[1]
        sums = jnp.zeros((1, n), F32)
        for ref in tail_refs:
            sums = sums + jnp.sum(ref[CHIP:PACK, 0:n].astype(F32), axis=0, keepdims=True)
        sums = sums + jnp.sum(tail_refs[-1][CHIP:PACK, DH : DH + n].astype(F32), axis=0, keepdims=True)
        size = jnp.maximum(ct_ref[...], 1).astype(F32)
        coef = LOSS_SCALE * 2.0 / (1.0 + jnp.exp(-sums / size)) / (size * (docs_ref[0:1, 0:n] + more_ref[0:1, 0:n]))
        ends = end_row(starts, seq_len)
        for dst, where in ((scale_ref, index), (other_ref, index // 2 * 2 + 1 - index % 2)):
            dst[...] = jnp.broadcast_to(row_coefs(starts, ends, coef, where * ROWS), dst.shape)

    scale = scale_ref[:, 0:1]
    width = GROUP * DH
    for k in range(2):
        for j in range(CHUNKS):

            @pl.when(step == (index % 2 + k) % 2 * CHUNKS + j)
            def _():
                src = got_ref[:, j * width : (j + 1) * width] if k else mine_refs[j][...]
                out_ref[...] = (src.astype(F32) * scale).astype(BF16)


def key_value_kernel(*refs):
    scale_refs, own_refs, a_refs, b_refs, outs = refs[0:2], refs[2:4], refs[4:6], refs[6:8], refs[8:10]
    for i in range(2):
        rows = slice(i * ROWS, (i + 1) * ROWS)
        scale = scale_refs[i][...]
        for j in range(CHUNKS):
            for k in range(2):
                cols = slice(k * DH, (k + 1) * DH)
                out = own_refs[j][rows, cols] + a_refs[j][rows, cols].astype(F32) + b_refs[j][rows, cols].astype(F32)
                at = (k * CHUNKS + j) * DH
                outs[i][:, at : at + DH] = (out * scale).astype(BF16)


def in_vmem(x):
    return pltpu.with_memory_space_constraint(x, pltpu.VMEM)


def in_hbm(x):
    return pltpu.with_memory_space_constraint(x, pltpu.HBM)


def local(query, key_value, upstream, log_ratio, doc_starts, answer_counts):
    count = lax.axis_size("ctx")
    seq_len = ROWS * count
    index = lax.axis_index("ctx").astype(jnp.int32)
    core = index % 2
    where = index.reshape(1)
    smem = pl.BlockSpec(memory_space=pltpu.SMEM)
    vmem = pl.BlockSpec(memory_space=pltpu.VMEM)

    def moved(value, steps):
        return lax.ppermute(value, "ctx", [(i, (i + steps) % count) for i in range(count)])

    def swapped(value):
        return lax.ppermute(value, "ctx", [(i, i ^ 1) for i in range(count)])

    def exchanged(value, bit):
        return lax.ppermute(value, "dp", [(i, i ^ bit) for i in range(lax.axis_size("dp"))])

    width = GROUP * DH
    got_lr = swapped(log_ratio)
    got_kv = swapped(key_value[0])
    hbm = pl.BlockSpec(memory_space=pl.ANY)
    slots = doc_starts.shape[1]
    own_kv, ratios, starts, counts = pl.pallas_call(
        early_kernel,
        out_shape=(
            pltpu.VMEM((ROWS, 2 * HK * DH), BF16),
            pltpu.VMEM((1, ROWS), F32),
            pltpu.VMEM((1, slots), jnp.int32),
            pltpu.VMEM((1, slots), jnp.int32),
        ),
        in_specs=[hbm] + [vmem] * 3,
        out_specs=(vmem,) * 4,
        scratch_shapes=[pltpu.SemaphoreType.DMA],
        compiler_params=pltpu.CompilerParams(vmem_limit_bytes=4 << 20),
        name="early",
    )(*[in_hbm(x) for x in (key_value[0], log_ratio, doc_starts, answer_counts)])
    packed = pltpu.VMEM((PACK, 2 * DH), BF16)
    own = pl.pallas_call(
        partial(pack_kernel, seq_len),
        out_shape=(packed,) * CHUNKS,
        in_specs=[smem] + [vmem] * 6,
        out_specs=(vmem,) * CHUNKS,
        compiler_params=pltpu.CompilerParams(vmem_limit_bytes=4 << 20),
        name="pack",
    )(where, *[in_vmem(x) for x in (own_kv, got_kv, ratios, got_lr, starts, counts)])
    back1, back2 = [], []
    for j in range(CHUNKS):
        back1.append(moved(own[j], 2))
        back2.append(moved(own[j], 4))
    got_q = swapped(query[0])
    got_g = swapped(upstream[0])
    joint = pltpu.VMEM((CHIP, CHUNKS * width), BF16)
    scalars, docs, q_all, g_all = pl.pallas_call(
        partial(join_kernel, seq_len),
        out_shape=(
            jax.ShapeDtypeStruct((2 + 2 * (CHIP // SUB),), jnp.int32),
            pltpu.VMEM((8, 128), F32),
            joint,
            joint,
        ),
        in_specs=[smem, hbm, hbm] + [vmem] * 4,
        out_specs=(smem,) + (vmem,) * 3,
        scratch_shapes=[pltpu.SemaphoreType.DMA((2,))],
        compiler_params=pltpu.CompilerParams(vmem_limit_bytes=8 << 20),
        name="join",
    )(where, in_hbm(query[0]), in_hbm(upstream[0]), *[in_vmem(x) for x in (got_q, got_g, starts, counts)])
    more_docs = exchanged(docs, 1)

    dq_mine, dq_other, d_own, d_a, d_b = [], [], [], [], []
    for j in range(CHUNKS):
        operands = (q_all, g_all, own[j], back1[j], back2[j], starts, *dq_other[-1:])
        outs = pl.pallas_call(
            partial(attention_kernel, j),
            in_specs=[smem] + [vmem] * len(operands),
            input_output_aliases={len(operands): 1} if j else {},
            out_specs=[vmem] * 5,
            scratch_shapes=[
                pltpu.VMEM((WIN, DH), BF16),
                pltpu.VMEM((WIN, DH), BF16),
                pltpu.VMEM((LANES, DH), BF16),
                pltpu.VMEM((LANES, DH), BF16),
                pltpu.VMEM((SPANS[-1], LANES), F32),
                pltpu.VMEM((SPANS[-1], LANES), F32),
                pltpu.VMEM((WIN, DH), F32),
                pltpu.VMEM((WIN, DH), F32),
                pltpu.VMEM((DH, LANES), F32),
                pltpu.VMEM((SUB + CHIP, width), BF16),
            ],
            out_shape=[
                pltpu.VMEM((ROWS, width), BF16),
                pltpu.VMEM((ROWS, CHUNKS * width), BF16),
                pltpu.VMEM((CHIP, 2 * DH), F32),
                pltpu.VMEM((CHIP, 2 * DH), BF16),
                pltpu.VMEM((PACK, 2 * DH), BF16),
            ],
            compiler_params=pltpu.CompilerParams(vmem_limit_bytes=24 << 20),
        )(scalars, *[in_vmem(x) for x in operands])
        for kept, out in zip((dq_mine, dq_other, d_own, d_a, d_b), outs):
            kept.append(out)

    got_a, got_b = [], []
    for j in range(CHUNKS):
        got_a.append(moved(d_a[j], -2))
        got_b.append(moved(d_b[j], -4))
    dq_got = swapped(dq_other[-1])
    docs = docs + more_docs
    more_docs = exchanged(docs, 2)
    tails = (own[0], back1[0], back2[0], got_b[0])
    d_query, scale_mine, scale_other = pl.pallas_call(
        partial(query_kernel, seq_len),
        grid=(2 * CHUNKS,),
        out_shape=(
            jax.ShapeDtypeStruct((ROWS, HQ * DH), BF16),
            pltpu.VMEM((ROWS, DH), F32),
            pltpu.VMEM((ROWS, DH), F32),
        ),
        in_specs=[smem] + [vmem] * 11,
        out_specs=(pl.BlockSpec((ROWS, width), lambda i: (0, i)), vmem, vmem),
        compiler_params=pltpu.CompilerParams(vmem_limit_bytes=8 << 20),
        name="q_out",
    )(where, *[in_vmem(x) for x in (starts, counts, docs, more_docs, *tails, *dq_mine, dq_got)])
    half = pltpu.VMEM((ROWS, 2 * CHUNKS * DH), BF16)
    kv_mine, kv_send = pl.pallas_call(
        key_value_kernel,
        out_shape=(half, half),
        in_specs=[vmem] * 8,
        out_specs=(vmem, vmem),
        compiler_params=pltpu.CompilerParams(vmem_limit_bytes=4 << 20),
        name="kv_out",
    )(*[in_vmem(x) for x in (scale_mine, scale_other, *d_own, *got_a, *got_b)])
    kv_got = swapped(kv_send)
    cut = CHUNKS * DH
    lower, upper = (jnp.where(core == 0, kv_mine, kv_got), jnp.where(core == 0, kv_got, kv_mine))
    d_key_value = jnp.concatenate([lower[:, :cut], upper[:, :cut], lower[:, cut:], upper[:, cut:]], axis=1)
    return (d_query[None], d_key_value[None])


def solution(mesh):
    return jax.shard_map(
        local,
        mesh=mesh,
        in_specs=(
            P("dp", "ctx", None),
            P("dp", "ctx", None),
            P("dp", "ctx", None),
            P("dp", "ctx"),
            P("dp", None),
            P("dp", None),
        ),
        out_specs=(P("dp", "ctx", None), P("dp", "ctx", None)),
        check_vma=False,
    )
```

time: 73.6 us -> 69.2 us (0.940)
  the two profiles are of different devices: /device:TPU:27 before, /device:TPU:1 now
where the time goes in v3:
time: 69.2 us; the launch traced here: 69 us
  starting transfers between devices  28.3 us (41%)
  waiting for transfers between devices  20.5 us (30%)
  Pallas kernels  18.6 us (27%)
  other arithmetic  0.83 us (1%)
  between operations  0.71 us (1%)
    ppermute x8, waiting for transfers between devices, moved(): lax.ppermute(value, 'ctx', [(i, (i + steps) % count) for i in range(count)])  14.7 us
    ppermute x8, starting transfers between devices, moved(): lax.ppermute(value, 'ctx', [(i, (i + steps) % count) for i in range(count)])  12.3 us
    pallas_call x2, Pallas kernels, local(): pl.pallas_call(partial(attention_kernel, j), in_specs=[smem] + [vmem] * l...  12.2 us
    ppermute x2, starting transfers between devices, exchanged(): lax.ppermute(value, 'dp', [(i, i ^ bit) for i in range(lax.axis_size('dp'...  10.5 us
    ppermute x6, starting transfers between devices, swapped(): return lax.ppermute(value, 'ctx', [(i, i ^ 1) for i in range(count)])  5.45 us
    ppermute x6, waiting for transfers between devices, swapped(): return lax.ppermute(value, 'ctx', [(i, i ^ 1) for i in range(count)])  4.83 us
    pallas_call x1, Pallas kernels, local(): pl.pallas_call(partial(query_kernel, seq_len), grid=(2 * CHUNKS,), out_sh...  2.22 us
    pallas_call x1, Pallas kernels, local(): pl.pallas_call(partial(join_kernel, seq_len), out_shape=(jax.ShapeDtypeSt...  1.99 us
  transfers between devices with their start and end apart: 16, of which 8 were waited for; matrix products, arithmetic and copies ran while one was open for 0% of the time, Pallas kernels for 18%

profile of v3, /device:TPU:1, one launch (start us, length us, event | category | flops | bytes accessed | tf_op | source)
XLA Modules:
  0.0 69.0 jit_solution(6310343188248641317)
XLA Ops:
  0.6 1.5 %collective-permute-start = (bf16[192,4096]{1,0:T(8,128)(2,1)}, bf16[192,4096]{1,0:T(8,128)(2,1)S(1)}, u32[]{:S(2)}, u32[]{:S(2)}) collective-permute-start(bf16[192,4096]{1,0:T(8,128)(2,1)} %bitcast.7), channel_id=1, source_target_pairs={{0,4},{4,0},{8,12},{12,8},{16,20},{20,16},{24,28},{28,24},{32,36},... | collective-permute-start | bytes 4718600 | tf_op jit(solution)/shard_map/ppermute | solution.py:345
  2.1 0.1 collective-permute-start.1
  2.2 0.4 collective-permute-start.4
  2.6 0.1 collective-permute-start.5
  2.7 1.7 %early.1 = (bf16[192,1024]{1,0:T(8,128)(2,1)S(1)}, f32[1,192]{1,0:T(1,128)S(1)}, s32[1,64]{1,0:T(1,128)S(1)}, s32[1,64]{1,0:T(1,128)S(1)}) custom-call(bf16[192,1024]{1,0:T(8,128)(2,1)} %bitcast.12, f32[1,192]{1,0:T(1,128)} %lr_ref.1, s32[1,64]{1,0:T(1,128)} %st_ref.1, s32[1,64]{1,0:T(1,128)} %ct_ref.1), custom_call_target="tpu_custom_call" | custom-call | tf_op jit(solution)/shard_map/early/pallas_call | solution.py:355
  4.4 3.7 %collective-permute-done.5.got_lr_ref = f32[1,192]{1,0:T(1,128)S(1)} collective-permute-done((f32[1,192]{1,0:T(1,128)}, f32[1,192]{1,0:T(1,128)S(1)}, u32[]{:S(2)}, u32[]{:S(2)}) %collective-permute-start.5) | collective-permute-done | bytes 800 | tf_op jit(solution)/shard_map/ppermute | solution.py:345
  8.2 0.3 pack.1
  8.5 1.4 %collective-permute-start.6 = (bf16[400,256]{1,0:T(8,128)(2,1)S(1)}, bf16[400,256]{1,0:T(8,128)(2,1)S(1)}, u32[]{:S(2)}, u32[]{:S(2)}) collective-permute-start(bf16[400,256]{1,0:T(8,128)(2,1)S(1)} %get-tuple-element.32.own_ref.refs_0_), channel_id=1, source_target_pairs={{0,8},{4,12},{8,16},{12,20},{16,24},{20,28},{24,32},{28,36},{32,40... | collective-permute-start | bytes 614408 | tf_op jit(solution)/shard_map/ppermute | solution.py:342
  9.8 2.5 %collective-permute-start.7 = (bf16[400,256]{1,0:T(8,128)(2,1)S(1)}, bf16[400,256]{1,0:T(8,128)(2,1)S(1)}, u32[]{:S(2)}, u32[]{:S(2)}) collective-permute-start(bf16[400,256]{1,0:T(8,128)(2,1)S(1)} %get-tuple-element.32.own_ref.refs_0_), channel_id=1, source_target_pairs={{0,16},{4,20},{8,24},{12,28},{16,32},{20,36},{24,40},{28,44},{32,4... | collective-permute-start | bytes 614408 | tf_op jit(solution)/shard_map/ppermute | solution.py:342
  12.3 1.5 %collective-permute-start.10 = (bf16[400,256]{1,0:T(8,128)(2,1)S(1)}, bf16[400,256]{1,0:T(8,128)(2,1)S(1)}, u32[]{:S(2)}, u32[]{:S(2)}) collective-permute-start(bf16[400,256]{1,0:T(8,128)(2,1)S(1)} %get-tuple-element.38.own_ref), channel_id=1, source_target_pairs={{0,16},{4,20},{8,24},{12,28},{16,32},{20,36},{24,40},{28,44},{32,4... | collective-permute-start | bytes 614408 | tf_op jit(solution)/shard_map/ppermute | solution.py:342
  13.8 0.0 collective-permute-done.got_q_ref
  13.8 1.2 %collective-permute-start.9 = (bf16[400,256]{1,0:T(8,128)(2,1)S(1)}, bf16[400,256]{1,0:T(8,128)(2,1)S(1)}, u32[]{:S(2)}, u32[]{:S(2)}) collective-permute-start(bf16[400,256]{1,0:T(8,128)(2,1)S(1)} %get-tuple-element.38.own_ref), channel_id=1, source_target_pairs={{0,8},{4,12},{8,16},{12,20},{16,24},{20,28},{24,32},{28,36},{32,40... | collective-permute-start | bytes 614408 | tf_op jit(solution)/shard_map/ppermute | solution.py:342
  15.1 2.0 %join.1 = (s32[10]{0:T(128)S(1)}, f32[8,128]{1,0:T(8,128)S(1)}, bf16[384,2048]{1,0:T(8,128)(2,1)S(1)}, bf16[384,2048]{1,0:T(8,128)(2,1)S(1)}) custom-call(s32[1]{0:T(128)} %bitcast.idx_ref, bf16[192,4096]{1,0:T(8,128)(2,1)} %bitcast.8, bf16[192,4096]{1,0:T(8,128)(2,1)} %bitcast.10, bf16[192,4096]{1,0:T(8,128)(2,1)S(1)} %collective-permute-done.got_q_ref, ...), custom_call_target="tpu_custom_call" | custom-call | tf_op jit(solution)/shard_map/join/pallas_call | solution.py:385
  17.1 1.6 %collective-permute-done.6.a_ref.refs_1_ = bf16[400,256]{1,0:T(8,128)(2,1)S(1)} collective-permute-done((bf16[400,256]{1,0:T(8,128)(2,1)S(1)}, bf16[400,256]{1,0:T(8,128)(2,1)S(1)}, u32[]{:S(2)}, u32[]{:S(2)}) %collective-permute-start.6) | collective-permute-done | bytes 204832 | tf_op jit(solution)/shard_map/ppermute | solution.py:342
  18.6 5.3 %collective-permute-done.7.b_ref.refs_2_ = bf16[400,256]{1,0:T(8,128)(2,1)S(1)} collective-permute-done((bf16[400,256]{1,0:T(8,128)(2,1)S(1)}, bf16[400,256]{1,0:T(8,128)(2,1)S(1)}, u32[]{:S(2)}, u32[]{:S(2)}) %collective-permute-start.7) | collective-permute-done | bytes 204832 | tf_op jit(solution)/shard_map/ppermute | solution.py:342
  24.0 6.0 %shard_map.77 = (bf16[192,1024]{1,0:T(8,128)(2,1)S(1)}, bf16[192,2048]{1,0:T(8,128)(2,1)S(1)}, f32[384,256]{1,0:T(8,128)S(1)}, bf16[384,256]{1,0:T(8,128)(2,1)S(1)}, bf16[400,256]{1,0:T(8,128)(2,1)S(1)}) custom-call(s32[10]{0:T(128)S(1)} %get-tuple-element.33.sc_ref, bf16[384,2048]{1,0:T(8,128)(2,1)S(1)} %get-tuple-element.34.q_all, ...), custom_call_target="tpu_custom_call" | custom-call | tf_op jit(solution)/shard_map/pallas_call | solution.py:404
  30.0 2.1 %collective-permute-done.9.a_ref = bf16[400,256]{1,0:T(8,128)(2,1)S(1)} collective-permute-done((bf16[400,256]{1,0:T(8,128)(2,1)S(1)}, bf16[400,256]{1,0:T(8,128)(2,1)S(1)}, u32[]{:S(2)}, u32[]{:S(2)}) %collective-permute-start.9) | collective-permute-done | bytes 204832 | tf_op jit(solution)/shard_map/ppermute | solution.py:342
  32.1 6.2 %shard_map.78 = (bf16[192,1024]{1,0:T(8,128)(2,1)S(1)}, bf16[192,2048]{1,0:T(8,128)(2,1)S(1)}, f32[384,256]{1,0:T(8,128)S(1)}, bf16[384,256]{1,0:T(8,128)(2,1)S(1)}, bf16[400,256]{1,0:T(8,128)(2,1)S(1)}) custom-call(s32[10]{0:T(128)S(1)} %get-tuple-element.33.sc_ref, bf16[384,2048]{1,0:T(8,128)(2,1)S(1)} %get-tuple-element.34.q_all, ...), custom_call_target="tpu_custom_call", output_to_operand_aliasing={{1}: (7, {})} | custom-call | tf_op jit(solution)/shard_map/pallas_call | solution.py:404
  38.3 1.2 %collective-permute-start.11 = (bf16[192,2048]{1,0:T(8,128)(2,1)S(1)}, bf16[192,2048]{1,0:T(8,128)(2,1)S(1)}, u32[]{:S(2)}, u32[]{:S(2)}) collective-permute-start(bf16[192,2048]{1,0:T(8,128)(2,1)S(1)} %get-tuple-element.41), channel_id=1, source_target_pairs={{0,4},{4,0},{8,12},{12,8},{16,20},{20,16},{24,28},{28,24},{32,36},... | collective-permute-start | bytes 2359304 | tf_op jit(solution)/shard_map/ppermute | solution.py:345
  39.6 3.7 %collective-permute-start.8 = (bf16[400,256]{1,0:T(8,128)(2,1)S(1)}, bf16[400,256]{1,0:T(8,128)(2,1)S(1)}, u32[]{:S(2)}, u32[]{:S(2)}) collective-permute-start(bf16[400,256]{1,0:T(8,128)(2,1)S(1)} %get-tuple-element.36), channel_id=1, source_target_pairs={{0,112},{4,116},{8,120},{12,124},{16,0},{20,4},{24,8},{28,12},{32,... | collective-permute-start | bytes 614408 | tf_op jit(solution)/shard_map/ppermute | solution.py:342
  43.3 1.6 %collective-permute-start.2 = (f32[8,128]{1,0:T(8,128)S(1)}, f32[8,128]{1,0:T(8,128)S(1)}, u32[]{:S(2)}, u32[]{:S(2)}) collective-permute-start(f32[8,128]{1,0:T(8,128)S(1)} %get-tuple-element.29), channel_id=1, source_target_pairs={{0,1},{1,0},{2,3},{3,2},{4,5},{5,4},{6,7},{7,6},{8,9},{9,8},{10,11... | collective-permute-start | bytes 12296 | tf_op jit(solution)/shard_map/ppermute | solution.py:348
  44.9 1.5 %collective-permute-start.14 = (bf16[400,256]{1,0:T(8,128)(2,1)S(1)}, bf16[400,256]{1,0:T(8,128)(2,1)S(1)}, u32[]{:S(2)}, u32[]{:S(2)}) collective-permute-start(bf16[400,256]{1,0:T(8,128)(2,1)S(1)} %get-tuple-element.49), channel_id=1, source_target_pairs={{0,112},{4,116},{8,120},{12,124},{16,0},{20,4},{24,8},{28,12},{32,... | collective-permute-start | bytes 614408 | tf_op jit(solution)/shard_map/ppermute | solution.py:342
  46.4 8.9 %collective-permute-start.3 = (f32[8,128]{1,0:T(8,128)S(1)}, f32[8,128]{1,0:T(8,128)S(1)}, u32[]{:S(2)}, u32[]{:S(2)}) collective-permute-start(f32[8,128]{1,0:T(8,128)S(1)} %add.7.docs_ref), channel_id=1, source_target_pairs={{0,2},{1,3},{2,0},{3,1},{4,6},{5,7},{6,4},{7,5},{8,10},{9,11},{10,... | collective-permute-start | bytes 12296 | tf_op jit(solution)/shard_map/ppermute | solution.py:348
  55.3 1.0 %collective-permute-done.3.more_ref = f32[8,128]{1,0:T(8,128)S(1)} collective-permute-done((f32[8,128]{1,0:T(8,128)S(1)}, f32[8,128]{1,0:T(8,128)S(1)}, u32[]{:S(2)}, u32[]{:S(2)}) %collective-permute-start.3) | collective-permute-done | bytes 4128 | tf_op jit(solution)/shard_map/ppermute | solution.py:348
  56.3 0.6 collective-permute-start.12
  56.9 2.2 %q_out.1 = (bf16[192,4096]{1,0:T(8,128)(2,1)}, f32[192,128]{1,0:T(8,128)S(1)}, f32[192,128]{1,0:T(8,128)S(1)}) custom-call(s32[1]{0:T(128)} %bitcast.idx_ref, s32[1,64]{1,0:T(1,128)S(1)} %get-tuple-element.27.st_ref, s32[1,64]{1,0:T(1,128)S(1)} %get-tuple-element.28.ct_ref, f32[8,128]{1,0:T(8,128)S(1)} %add.7.docs_ref, ...), custom_call_target="tpu_custom_call" | custom-call | tf_op jit(solution)/shard_map/q_out/pallas_call | solution.py:441
  59.1 1.5 %collective-permute-done.13.refs_5_ = bf16[384,256]{1,0:T(8,128)(2,1)S(1)} collective-permute-done((bf16[384,256]{1,0:T(8,128)(2,1)S(1)}, bf16[384,256]{1,0:T(8,128)(2,1)S(1)}, u32[]{:S(2)}, u32[]{:S(2)}) %collective-permute-start.13) | collective-permute-done | bytes 196640 | tf_op jit(solution)/shard_map/ppermute | solution.py:342
  60.5 4.2 %collective-permute-done.12.refs_4_ = bf16[384,256]{1,0:T(8,128)(2,1)S(1)} collective-permute-done((bf16[384,256]{1,0:T(8,128)(2,1)S(1)}, bf16[384,256]{1,0:T(8,128)(2,1)S(1)}, u32[]{:S(2)}, u32[]{:S(2)}) %collective-permute-start.12) | collective-permute-done | bytes 196640 | tf_op jit(solution)/shard_map/ppermute | solution.py:342
  64.8 0.2 kv_out.1
  65.0 2.1 %collective-permute-start.15 = (bf16[192,512]{1,0:T(8,128)(2,1)S(1)}, bf16[192,512]{1,0:T(8,128)(2,1)S(1)}, u32[]{:S(2)}, u32[]{:S(2)}) collective-permute-start(bf16[192,512]{1,0:T(8,128)(2,1)S(1)} %get-tuple-element.51), channel_id=1, source_target_pairs={{0,4},{4,0},{8,12},{12,8},{16,20},{20,16},{24,28},{28,24},{32,36},... | collective-permute-start | bytes 589832 | tf_op jit(solution)/shard_map/ppermute | solution.py:345
  67.1 1.1 %collective-permute-done.15 = bf16[192,512]{1,0:T(8,128)(2,1)S(1)} collective-permute-done((bf16[192,512]{1,0:T(8,128)(2,1)S(1)}, bf16[192,512]{1,0:T(8,128)(2,1)S(1)}, u32[]{:S(2)}, u32[]{:S(2)}) %collective-permute-start.15) | collective-permute-done | bytes 196640 | tf_op jit(solution)/shard_map/ppermute | solution.py:345
  68.2 0.8 %maximum_bitcast_fusion = bf16[1,192,1024]{2,1,0:T(8,128)(2,1)} fusion(bf16[192,256]{1,0:T(8,128)(2,1)S(1)} %get-tuple-element.58, bf16[192,256]{1,0:T(8,128)(2,1)S(1)} %get-tuple-element.55, bf16[192,256]{1,0:T(8,128)(2,1)S(1)} %get-tuple-element.59, bf16[192,256]{1,0:T(8,128)(2,1)S(1)} %get-tuple-element.54), kind=kLoop, calls=%fused_computation | loop fusion | flops 1572864 | bytes 786432 | tf_op jit(solution)/shard_map/broadcast_in_dim | solution.py:467
  (11 shorter events, 0.1 us)
Async XLA Ops:
  0.6 13.2 %collective-permute-start = (bf16[192,4096]{1,0:T(8,128)(2,1)}, bf16[192,4096]{1,0:T(8,128)(2,1)S(1)}, u32[]{:S(2)}, u32[]{:S(2)}) collective-permute-start(bf16[192,4096]{1,0:T(8,128)(2,1)} %bitcast.7), channel_id=1, source_target_pairs={{0,4},{4,0},{8,12},{12,8},{16,20},{20,16},{24,28},{28,24},{32,36},... | collective-permute-start | bytes 4718600 | tf_op jit(solution)/shard_map/ppermute | solution.py:345
  2.1 13.0 %collective-permute-start.1 = (bf16[192,4096]{1,0:T(8,128)(2,1)}, bf16[192,4096]{1,0:T(8,128)(2,1)S(1)}, u32[]{:S(2)}, u32[]{:S(2)}) collective-permute-start(bf16[192,4096]{1,0:T(8,128)(2,1)} %bitcast.9), channel_id=1, source_target_pairs={{0,4},{4,0},{8,12},{12,8},{16,20},{20,16},{24,28},{28,24},{32,36},... | collective-permute-start | bytes 4718600 | tf_op jit(solution)/shard_map/ppermute | solution.py:345
  2.2 6.0 %collective-permute-start.4 = (bf16[192,1024]{1,0:T(8,128)(2,1)}, bf16[192,1024]{1,0:T(8,128)(2,1)S(1)}, u32[]{:S(2)}, u32[]{:S(2)}) collective-permute-start(bf16[192,1024]{1,0:T(8,128)(2,1)} %bitcast.11), channel_id=1, source_target_pairs={{0,4},{4,0},{8,12},{12,8},{16,20},{20,16},{24,28},{28,24},{32,36},... | collective-permute-start | bytes 1179656 | tf_op jit(solution)/shard_map/ppermute | solution.py:345
  2.6 5.5 %collective-permute-start.5 = (f32[1,192]{1,0:T(1,128)}, f32[1,192]{1,0:T(1,128)S(1)}, u32[]{:S(2)}, u32[]{:S(2)}) collective-permute-start(f32[1,192]{1,0:T(1,128)} %lr_ref.1), channel_id=1, source_target_pairs={{0,4},{4,0},{8,12},{12,8},{16,20},{20,16},{24,28},{28,24},{32,36},... | collective-permute-start | bytes 2312 | tf_op jit(solution)/shard_map/ppermute | solution.py:345
  8.5 10.2 %collective-permute-start.6 = (bf16[400,256]{1,0:T(8,128)(2,1)S(1)}, bf16[400,256]{1,0:T(8,128)(2,1)S(1)}, u32[]{:S(2)}, u32[]{:S(2)}) collective-permute-start(bf16[400,256]{1,0:T(8,128)(2,1)S(1)} %get-tuple-element.32.own_ref.refs_0_), channel_id=1, source_target_pairs={{0,8},{4,12},{8,16},{12,20},{16,24},{20,28},{24,32},{28,36},{32,40... | collective-permute-start | bytes 614408 | tf_op jit(solution)/shard_map/ppermute | solution.py:342
  9.8 14.1 %collective-permute-start.7 = (bf16[400,256]{1,0:T(8,128)(2,1)S(1)}, bf16[400,256]{1,0:T(8,128)(2,1)S(1)}, u32[]{:S(2)}, u32[]{:S(2)}) collective-permute-start(bf16[400,256]{1,0:T(8,128)(2,1)S(1)} %get-tuple-element.32.own_ref.refs_0_), channel_id=1, source_target_pairs={{0,16},{4,20},{8,24},{12,28},{16,32},{20,36},{24,40},{28,44},{32,4... | collective-permute-start | bytes 614408 | tf_op jit(solution)/shard_map/ppermute | solution.py:342
  12.3 17.7 %collective-permute-start.10 = (bf16[400,256]{1,0:T(8,128)(2,1)S(1)}, bf16[400,256]{1,0:T(8,128)(2,1)S(1)}, u32[]{:S(2)}, u32[]{:S(2)}) collective-permute-start(bf16[400,256]{1,0:T(8,128)(2,1)S(1)} %get-tuple-element.38.own_ref), channel_id=1, source_target_pairs={{0,16},{4,20},{8,24},{12,28},{16,32},{20,36},{24,40},{28,44},{32,4... | collective-permute-start | bytes 614408 | tf_op jit(solution)/shard_map/ppermute | solution.py:342
  13.8 18.3 %collective-permute-start.9 = (bf16[400,256]{1,0:T(8,128)(2,1)S(1)}, bf16[400,256]{1,0:T(8,128)(2,1)S(1)}, u32[]{:S(2)}, u32[]{:S(2)}) collective-permute-start(bf16[400,256]{1,0:T(8,128)(2,1)S(1)} %get-tuple-element.38.own_ref), channel_id=1, source_target_pairs={{0,8},{4,12},{8,16},{12,20},{16,24},{20,28},{24,32},{28,36},{32,40... | collective-permute-start | bytes 614408 | tf_op jit(solution)/shard_map/ppermute | solution.py:342
  38.3 18.5 %collective-permute-start.11 = (bf16[192,2048]{1,0:T(8,128)(2,1)S(1)}, bf16[192,2048]{1,0:T(8,128)(2,1)S(1)}, u32[]{:S(2)}, u32[]{:S(2)}) collective-permute-start(bf16[192,2048]{1,0:T(8,128)(2,1)S(1)} %get-tuple-element.41), channel_id=1, source_target_pairs={{0,4},{4,0},{8,12},{12,8},{16,20},{20,16},{24,28},{28,24},{32,36},... | collective-permute-start | bytes 2359304 | tf_op jit(solution)/shard_map/ppermute | solution.py:345
  39.6 17.3 %collective-permute-start.8 = (bf16[400,256]{1,0:T(8,128)(2,1)S(1)}, bf16[400,256]{1,0:T(8,128)(2,1)S(1)}, u32[]{:S(2)}, u32[]{:S(2)}) collective-permute-start(bf16[400,256]{1,0:T(8,128)(2,1)S(1)} %get-tuple-element.36), channel_id=1, source_target_pairs={{0,112},{4,116},{8,120},{12,124},{16,0},{20,4},{24,8},{28,12},{32,... | collective-permute-start | bytes 614408 | tf_op jit(solution)/shard_map/ppermute | solution.py:342
  43.3 3.1 %collective-permute-start.2 = (f32[8,128]{1,0:T(8,128)S(1)}, f32[8,128]{1,0:T(8,128)S(1)}, u32[]{:S(2)}, u32[]{:S(2)}) collective-permute-start(f32[8,128]{1,0:T(8,128)S(1)} %get-tuple-element.29), channel_id=1, source_target_pairs={{0,1},{1,0},{2,3},{3,2},{4,5},{5,4},{6,7},{7,6},{8,9},{9,8},{10,11... | collective-permute-start | bytes 12296 | tf_op jit(solution)/shard_map/ppermute | solution.py:348
  44.9 19.9 %collective-permute-start.14 = (bf16[400,256]{1,0:T(8,128)(2,1)S(1)}, bf16[400,256]{1,0:T(8,128)(2,1)S(1)}, u32[]{:S(2)}, u32[]{:S(2)}) collective-permute-start(bf16[400,256]{1,0:T(8,128)(2,1)S(1)} %get-tuple-element.49), channel_id=1, source_target_pairs={{0,112},{4,116},{8,120},{12,124},{16,0},{20,4},{24,8},{28,12},{32,... | collective-permute-start | bytes 614408 | tf_op jit(solution)/shard_map/ppermute | solution.py:342
  46.4 9.9 %collective-permute-start.3 = (f32[8,128]{1,0:T(8,128)S(1)}, f32[8,128]{1,0:T(8,128)S(1)}, u32[]{:S(2)}, u32[]{:S(2)}) collective-permute-start(f32[8,128]{1,0:T(8,128)S(1)} %add.7.docs_ref), channel_id=1, source_target_pairs={{0,2},{1,3},{2,0},{3,1},{4,6},{5,7},{6,4},{7,5},{8,10},{9,11},{10,... | collective-permute-start | bytes 12296 | tf_op jit(solution)/shard_map/ppermute | solution.py:348
  55.3 5.3 %collective-permute-start.13 = (bf16[384,256]{1,0:T(8,128)(2,1)S(1)}, bf16[384,256]{1,0:T(8,128)(2,1)S(1)}, u32[]{:S(2)}, u32[]{:S(2)}) collective-permute-start(bf16[384,256]{1,0:T(8,128)(2,1)S(1)} %get-tuple-element.48), channel_id=1, source_target_pairs={{0,120},{4,124},{8,0},{12,4},{16,8},{20,12},{24,16},{28,20},{32,24... | collective-permute-start | bytes 589832 | tf_op jit(solution)/shard_map/ppermute | solution.py:342
  56.3 8.5 %collective-permute-start.12 = (bf16[384,256]{1,0:T(8,128)(2,1)S(1)}, bf16[384,256]{1,0:T(8,128)(2,1)S(1)}, u32[]{:S(2)}, u32[]{:S(2)}) collective-permute-start(bf16[384,256]{1,0:T(8,128)(2,1)S(1)} %get-tuple-element.47), channel_id=1, source_target_pairs={{0,120},{4,124},{8,0},{12,4},{16,8},{20,12},{24,16},{28,20},{32,24... | collective-permute-start | bytes 589832 | tf_op jit(solution)/shard_map/ppermute | solution.py:342
  65.0 3.2 %collective-permute-start.15 = (bf16[192,512]{1,0:T(8,128)(2,1)S(1)}, bf16[192,512]{1,0:T(8,128)(2,1)S(1)}, u32[]{:S(2)}, u32[]{:S(2)}) collective-permute-start(bf16[192,512]{1,0:T(8,128)(2,1)S(1)} %get-tuple-element.51), channel_id=1, source_target_pairs={{0,4},{4,0},{8,12},{12,8},{16,20},{20,16},{24,28},{28,24},{32,36},... | collective-permute-start | bytes 589832 | tf_op jit(solution)/shard_map/ppermute | solution.py:345

commit v4 on v3

--- a/solution.py
+++ b/solution.py
@@ -96,18 +96,28 @@
     copy.wait()
 
 
-def join_kernel(seq_len, idx_ref, q_hbm, g_hbm, got_q_ref, got_g_ref, st_ref, ct_ref, sc_ref, cnt_ref, q_all, g_all, sems):
+def halves_kernel(idx_ref, q_hbm, g_hbm, snd_ref, q_all, g_all, sems):
     core = idx_ref[0] % 2
     width = q_all.shape[1]
-    cols = pl.ds(pl.multiple_of(core * width, width), width)
-    mine = pl.ds(pl.multiple_of(core * ROWS, ROWS), ROWS)
-    other = pl.ds(pl.multiple_of((1 - core) * ROWS, ROWS), ROWS)
+    rows = pl.ds(pl.multiple_of(core * ROWS, ROWS), ROWS)
+    mine = pl.ds(pl.multiple_of(core * width, width), width)
+    theirs = pl.ds(pl.multiple_of((1 - core) * width, width), width)
     copies = [
-        pltpu.make_async_copy(q_hbm.at[:, cols], q_all.at[mine], sems.at[0]),
-        pltpu.make_async_copy(g_hbm.at[:, cols], g_all.at[mine], sems.at[1]),
+        pltpu.make_async_copy(q_hbm.at[:, theirs], snd_ref.at[0], sems.at[0]),
+        pltpu.make_async_copy(g_hbm.at[:, theirs], snd_ref.at[1], sems.at[1]),
+        pltpu.make_async_copy(q_hbm.at[:, mine], q_all.at[rows], sems.at[2]),
+        pltpu.make_async_copy(g_hbm.at[:, mine], g_all.at[rows], sems.at[3]),
     ]
     for copy in copies:
         copy.start()
+    for copy in copies:
+        copy.wait()
+
+
+def join_kernel(seq_len, idx_ref, got_ref, q_in, g_in, st_ref, ct_ref, sc_ref, cnt_ref, q_all, g_all):
+    core = idx_ref[0] % 2
+    mine = pl.ds(pl.multiple_of(core * ROWS, ROWS), ROWS)
+    other = pl.ds(pl.multiple_of((1 - core) * ROWS, ROWS), ROWS)
     index = idx_ref[0]
     first = index // 2 * CHIP
     base = first - (WIN - CHIP)
@@ -138,12 +148,9 @@
         hit = jnp.where((pos >= first_answer) & (pos < ends), 1.0, 0.0)
         return jnp.sum(hit, axis=1, keepdims=True) > 0.5
 
-    q_all[other, :] = got_q_ref[:, cols]
-    g_all[other, :] = jnp.where(answers(index + 1 - 2 * core), got_g_ref[:, cols], jnp.zeros((), BF16))
-    kept = answers(index)
-    for copy in copies:
-        copy.wait()
-    g_all[mine, :] = jnp.where(kept, g_all[mine, :], jnp.zeros((), BF16))
+    q_all[other, :] = got_ref[0]
+    g_all[other, :] = jnp.where(answers(index + 1 - 2 * core), got_ref[1], jnp.zeros((), BF16))
+    g_all[mine, :] = jnp.where(answers(index), g_in[mine, :], jnp.zeros((), BF16))
 
 
 def nt(a, b):
@@ -340,6 +347,12 @@
 
     def moved(value, steps):
         return lax.ppermute(value, "ctx", [(i, (i + steps) % count) for i in range(count)])
+
+    def moved_two_chips(value, steps):
+        pairs = [(i, i + steps) for i in range(count) if 0 <= i + steps < count]
+        senders, receivers = sorted(set(range(count)) - {i for i, _ in pairs}), sorted(set(range(count)) - {i for _, i in pairs})
+        half = len(senders) // 2
+        return lax.ppermute(value, "ctx", pairs + list(zip(senders, receivers[half:] + receivers[:half])))
 
     def swapped(value):
         return lax.ppermute(value, "ctx", [(i, i ^ 1) for i in range(count)])
@@ -378,10 +391,18 @@
     back1, back2 = [], []
     for j in range(CHUNKS):
         back1.append(moved(own[j], 2))
-        back2.append(moved(own[j], 4))
-    got_q = swapped(query[0])
-    got_g = swapped(upstream[0])
+        back2.append(moved_two_chips(own[j], 4))
     joint = pltpu.VMEM((CHIP, CHUNKS * width), BF16)
+    to_send, q_mine, g_mine = pl.pallas_call(
+        halves_kernel,
+        out_shape=(pltpu.VMEM((2, ROWS, CHUNKS * width), BF16), joint, joint),
+        in_specs=[smem, hbm, hbm],
+        out_specs=(vmem,) * 3,
+        scratch_shapes=[pltpu.SemaphoreType.DMA((4,))],
+        compiler_params=pltpu.CompilerParams(vmem_limit_bytes=8 << 20),
+        name="halves",
+    )(where, in_hbm(query[0]), in_hbm(upstream[0]))
+    got_rows = swapped(to_send)
     scalars, docs, q_all, g_all = pl.pallas_call(
         partial(join_kernel, seq_len),
         out_shape=(
@@ -390,12 +411,12 @@
             joint,
             joint,
         ),
-        in_specs=[smem, hbm, hbm] + [vmem] * 4,
+        in_specs=[smem] + [vmem] * 5,
         out_specs=(smem,) + (vmem,) * 3,
-        scratch_shapes=[pltpu.SemaphoreType.DMA((2,))],
+        input_output_aliases={2: 2, 3: 3},
         compiler_params=pltpu.CompilerParams(vmem_limit_bytes=8 << 20),
         name="join",
-    )(where, in_hbm(query[0]), in_hbm(upstream[0]), *[in_vmem(x) for x in (got_q, got_g, starts, counts)])
+    )(where, *[in_vmem(x) for x in (got_rows, q_mine, g_mine, starts, counts)])
     more_docs = exchanged(docs, 1)
 
     dq_mine, dq_other, d_own, d_a, d_b = [], [], [], [], []
@@ -433,7 +454,7 @@
     got_a, got_b = [], []
     for j in range(CHUNKS):
         got_a.append(moved(d_a[j], -2))
-        got_b.append(moved(d_b[j], -4))
+        got_b.append((moved_two_chips if j else moved)(d_b[j], -4))
     dq_got = swapped(dq_other[-1])
     docs = docs + more_docs
     more_docs = exchanged(docs, 2)

time: 69.2 us -> 63.7 us (0.921)
  waiting for transfers between devices: 20.5 us -> 17.3 us
  starting transfers between devices: 28.3 us -> 25.3 us
  Pallas kernels: 18.6 us -> 19.4 us
    ppermute x8 -> x5, waiting for transfers between devices: 14.7 us -> 6.33 us  [moved(): lax.ppermute(value, 'ctx', [(i, (i + steps) % count) for i in range(count)])]
    ppermute x0 -> x3, waiting for transfers between devices: none -> 7.16 us  [moved_two_chips(): lax.ppermute(value, 'ctx', pairs + list(zip(senders, receivers[half:] + r...]
    ppermute x2, starting transfers between devices: 10.5 us -> 5.08 us  [exchanged(): lax.ppermute(value, 'dp', [(i, i ^ bit) for i in range(lax.axis_size('dp'...]
    ppermute x0 -> x3, starting transfers between devices: none -> 5.2 us  [moved_two_chips(): lax.ppermute(value, 'ctx', pairs + list(zip(senders, receivers[half:] + r...]
    ppermute x6 -> x5, waiting for transfers between devices: 4.83 us -> 2.45 us  [swapped(): return lax.ppermute(value, 'ctx', [(i, i ^ 1) for i in range(count)])]
    ppermute x8 -> x5, starting transfers between devices: 12.3 us -> 10.1 us  [moved(): lax.ppermute(value, 'ctx', [(i, (i + steps) % count) for i in range(count)])]
    pallas_call x0 -> x1, Pallas kernels: none -> 1.93 us  [local(): pl.pallas_call(halves_kernel, out_shape=(pltpu.VMEM((2, ROWS, CHUNKS * wi...]
    pallas_call x1, Pallas kernels: 1.99 us -> 0.81 us  [local(): pl.pallas_call(partial(join_kernel, seq_len), out_shape=(jax.ShapeDtypeSt...]
  transfers between devices with their start and end apart: 16 -> 15, of which waited for: 8 -> 8; matrix products, arithmetic and copies ran while one was open for 0% -> 0% of each run, Pallas kernels for 18% -> 17%
where the time goes in v4:
time: 63.7 us; the launch traced here: 63.5 us
  starting transfers between devices  25.3 us (40%)
  Pallas kernels  19.4 us (30%)
  waiting for transfers between devices  17.3 us (27%)
  other arithmetic  0.83 us (1%)
  between operations  0.73 us (1%)
    pallas_call x2, Pallas kernels, local(): pl.pallas_call(partial(attention_kernel, j), in_specs=[smem] + [vmem] * l...  12.2 us
    ppermute x5, starting transfers between devices, moved(): lax.ppermute(value, 'ctx', [(i, (i + steps) % count) for i in range(count)])  10.1 us
    ppermute x3, waiting for transfers between devices, moved_two_chips(): lax.ppermute(value, 'ctx', pairs + list(zip(senders, receivers[half:] + r...  7.16 us
    ppermute x5, waiting for transfers between devices, moved(): lax.ppermute(value, 'ctx', [(i, (i + steps) % count) for i in range(count)])  6.33 us
    ppermute x3, starting transfers between devices, moved_two_chips(): lax.ppermute(value, 'ctx', pairs + list(zip(senders, receivers[half:] + r...  5.2 us
    ppermute x2, starting transfers between devices, exchanged(): lax.ppermute(value, 'dp', [(i, i ^ bit) for i in range(lax.axis_size('dp'...  5.08 us
    ppermute x5, starting transfers between devices, swapped(): return lax.ppermute(value, 'ctx', [(i, i ^ 1) for i in range(count)])  4.88 us
    ppermute x5, waiting for transfers between devices, swapped(): return lax.ppermute(value, 'ctx', [(i, i ^ 1) for i in range(count)])  2.45 us
  transfers between devices with their start and end apart: 15, of which 8 were waited for; matrix products, arithmetic and copies ran while one was open for 0% of the time, Pallas kernels for 17%

profile of v4, /device:TPU:1, one launch (start us, length us, event | category | flops | bytes accessed | tf_op | source)
XLA Modules:
  0.0 63.5 jit_solution(7116538624045973755)
XLA Ops:
  0.6 0.0 copy-start.1
  0.7 1.9 %halves.1 = (bf16[2,192,2048]{2,1,0:T(8,128)(2,1)S(1)}, bf16[384,2048]{1,0:T(8,128)(2,1)S(1)}, bf16[384,2048]{1,0:T(8,128)(2,1)S(1)}) custom-call(s32[1]{0:T(128)} %bitcast.idx_ref, bf16[192,4096]{1,0:T(8,128)(2,1)} %bitcast.7, bf16[192,4096]{1,0:T(8,128)(2,1)} %bitcast.8), custom_call_target="tpu_custom_call" | custom-call | tf_op jit(solution)/shard_map/halves/pallas_call | solution.py:396
  2.6 1.5 %collective-permute-start = (bf16[2,192,2048]{2,1,0:T(8,128)(2,1)S(1)}, bf16[2,192,2048]{2,1,0:T(8,128)(2,1)S(1)}, u32[]{:S(2)}, u32[]{:S(2)}) collective-permute-start(bf16[2,192,2048]{2,1,0:T(8,128)(2,1)S(1)} %get-tuple-element.32), channel_id=1, source_target_pairs={{0,4},{4,0},{8,12},{12,8},{16,20},{20,16},{24,28},{28,24},{32,36},... | collective-permute-start | bytes 4718600 | tf_op jit(solution)/shard_map/ppermute | solution.py:358
  4.1 0.1 collective-permute-start.3
  4.2 0.4 collective-permute-start.4
  4.6 1.7 %early.1 = (bf16[192,1024]{1,0:T(8,128)(2,1)S(1)}, f32[1,192]{1,0:T(1,128)S(1)}, s32[1,64]{1,0:T(1,128)S(1)}, s32[1,64]{1,0:T(1,128)S(1)}) custom-call(bf16[192,1024]{1,0:T(8,128)(2,1)} %bitcast.9, f32[1,192]{1,0:T(1,128)} %lr_ref.1, s32[1,64]{1,0:T(1,128)} %st_ref.1, s32[1,64]{1,0:T(1,128)} %ct_ref.1), custom_call_target="tpu_custom_call" | custom-call | tf_op jit(solution)/shard_map/early/pallas_call | solution.py:368
  6.3 1.4 %collective-permute-done.4.got_lr_ref = f32[1,192]{1,0:T(1,128)S(1)} collective-permute-done((f32[1,192]{1,0:T(1,128)S(1)}, f32[1,192]{1,0:T(1,128)S(1)}, u32[]{:S(2)}, u32[]{:S(2)}) %collective-permute-start.4) | collective-permute-done | bytes 800 | tf_op jit(solution)/shard_map/ppermute | solution.py:358
  7.7 0.3 pack.1
  8.0 1.4 %collective-permute-start.5 = (bf16[400,256]{1,0:T(8,128)(2,1)S(1)}, bf16[400,256]{1,0:T(8,128)(2,1)S(1)}, u32[]{:S(2)}, u32[]{:S(2)}) collective-permute-start(bf16[400,256]{1,0:T(8,128)(2,1)S(1)} %get-tuple-element.38.own_ref.refs_0_), channel_id=1, source_target_pairs={{0,8},{4,12},{8,16},{12,20},{16,24},{20,28},{24,32},{28,36},{32,40... | collective-permute-start | bytes 614408 | tf_op jit(solution)/shard_map/ppermute | solution.py:349
  9.4 2.5 %collective-permute-start.6 = (bf16[400,256]{1,0:T(8,128)(2,1)S(1)}, bf16[400,256]{1,0:T(8,128)(2,1)S(1)}, u32[]{:S(2)}, u32[]{:S(2)}) collective-permute-start(bf16[400,256]{1,0:T(8,128)(2,1)S(1)} %get-tuple-element.38.own_ref.refs_0_), channel_id=1, source_target_pairs={{0,16},{4,20},{8,24},{12,28},{16,32},{20,36},{24,40},{28,44},{32,4... | collective-permute-start | bytes 614408 | tf_op jit(solution)/shard_map/ppermute | solution.py:355
  11.8 0.6 collective-permute-start.8
  12.4 2.7 %collective-permute-start.9 = (bf16[400,256]{1,0:T(8,128)(2,1)S(1)}, bf16[400,256]{1,0:T(8,128)(2,1)S(1)}, u32[]{:S(2)}, u32[]{:S(2)}) collective-permute-start(bf16[400,256]{1,0:T(8,128)(2,1)S(1)} %get-tuple-element.44.own_ref), channel_id=1, source_target_pairs={{0,16},{4,20},{8,24},{12,28},{16,32},{20,36},{24,40},{28,44},{32,4... | collective-permute-start | bytes 614408 | tf_op jit(solution)/shard_map/ppermute | solution.py:355
  15.2 0.8 %join.1 = (s32[10]{0:T(128)S(1)}, f32[8,128]{1,0:T(8,128)S(1)}, bf16[384,2048]{1,0:T(8,128)(2,1)S(1)}, bf16[384,2048]{1,0:T(8,128)(2,1)S(1)}) custom-call(s32[1]{0:T(128)} %bitcast.idx_ref, bf16[2,192,2048]{2,1,0:T(8,128)(2,1)S(1)} %collective-permute-done.got_ref, ...), custom_call_target="tpu_custom_call", output_to_operand_aliasing={{2}: (2, {}), {3}: (3, {})} | custom-call | tf_op jit(solution)/shard_map/join/pallas_call | solution.py:406
  16.0 2.2 %collective-permute-done.5.a_ref.refs_1_ = bf16[400,256]{1,0:T(8,128)(2,1)S(1)} collective-permute-done((bf16[400,256]{1,0:T(8,128)(2,1)S(1)}, bf16[400,256]{1,0:T(8,128)(2,1)S(1)}, u32[]{:S(2)}, u32[]{:S(2)}) %collective-permute-start.5) | collective-permute-done | bytes 204832 | tf_op jit(solution)/shard_map/ppermute | solution.py:349
  18.1 4.4 %collective-permute-done.6.b_ref.refs_2_ = bf16[400,256]{1,0:T(8,128)(2,1)S(1)} collective-permute-done((bf16[400,256]{1,0:T(8,128)(2,1)S(1)}, bf16[400,256]{1,0:T(8,128)(2,1)S(1)}, u32[]{:S(2)}, u32[]{:S(2)}) %collective-permute-start.6) | collective-permute-done | bytes 204832 | tf_op jit(solution)/shard_map/ppermute | solution.py:355
  22.5 6.0 %shard_map.77 = (bf16[192,1024]{1,0:T(8,128)(2,1)S(1)}, bf16[192,2048]{1,0:T(8,128)(2,1)S(1)}, f32[384,256]{1,0:T(8,128)S(1)}, bf16[384,256]{1,0:T(8,128)(2,1)S(1)}, bf16[400,256]{1,0:T(8,128)(2,1)S(1)}) custom-call(s32[10]{0:T(128)S(1)} %get-tuple-element.39.sc_ref, bf16[384,2048]{1,0:T(8,128)(2,1)S(1)} %get-tuple-element.40.q_all, ...), custom_call_target="tpu_custom_call" | custom-call | tf_op jit(solution)/shard_map/pallas_call | solution.py:425
  28.5 2.8 %collective-permute-done.9.b_ref = bf16[400,256]{1,0:T(8,128)(2,1)S(1)} collective-permute-done((bf16[400,256]{1,0:T(8,128)(2,1)S(1)}, bf16[400,256]{1,0:T(8,128)(2,1)S(1)}, u32[]{:S(2)}, u32[]{:S(2)}) %collective-permute-start.9) | collective-permute-done | bytes 204832 | tf_op jit(solution)/shard_map/ppermute | solution.py:355
  31.3 6.2 %shard_map.78 = (bf16[192,1024]{1,0:T(8,128)(2,1)S(1)}, bf16[192,2048]{1,0:T(8,128)(2,1)S(1)}, f32[384,256]{1,0:T(8,128)S(1)}, bf16[384,256]{1,0:T(8,128)(2,1)S(1)}, bf16[400,256]{1,0:T(8,128)(2,1)S(1)}) custom-call(s32[10]{0:T(128)S(1)} %get-tuple-element.39.sc_ref, bf16[384,2048]{1,0:T(8,128)(2,1)S(1)} %get-tuple-element.40.q_all, ...), custom_call_target="tpu_custom_call", output_to_operand_aliasing={{1}: (7, {})} | custom-call | tf_op jit(solution)/shard_map/pallas_call | solution.py:425
  37.5 1.0 %collective-permute-start.10 = (bf16[192,2048]{1,0:T(8,128)(2,1)S(1)}, bf16[192,2048]{1,0:T(8,128)(2,1)S(1)}, u32[]{:S(2)}, u32[]{:S(2)}) collective-permute-start(bf16[192,2048]{1,0:T(8,128)(2,1)S(1)} %get-tuple-element.47), channel_id=1, source_target_pairs={{0,4},{4,0},{8,12},{12,8},{16,20},{20,16},{24,28},{28,24},{32,36},... | collective-permute-start | bytes 2359304 | tf_op jit(solution)/shard_map/ppermute | solution.py:358
  38.6 1.8 %collective-permute-start.7 = (bf16[400,256]{1,0:T(8,128)(2,1)S(1)}, bf16[400,256]{1,0:T(8,128)(2,1)S(1)}, u32[]{:S(2)}, u32[]{:S(2)}) collective-permute-start(bf16[400,256]{1,0:T(8,128)(2,1)S(1)} %get-tuple-element.42), channel_id=1, source_target_pairs={{0,112},{4,116},{8,120},{12,124},{16,0},{20,4},{24,8},{28,12},{32,... | collective-permute-start | bytes 614408 | tf_op jit(solution)/shard_map/ppermute | solution.py:349
  40.3 1.6 %collective-permute-start.1 = (f32[8,128]{1,0:T(8,128)S(1)}, f32[8,128]{1,0:T(8,128)S(1)}, u32[]{:S(2)}, u32[]{:S(2)}) collective-permute-start(f32[8,128]{1,0:T(8,128)S(1)} %get-tuple-element.35), channel_id=1, source_target_pairs={{0,1},{1,0},{2,3},{3,2},{4,5},{5,4},{6,7},{7,6},{8,9},{9,8},{10,11... | collective-permute-start | bytes 12296 | tf_op jit(solution)/shard_map/ppermute | solution.py:361
  42.0 1.0 %collective-permute-done.1 = f32[8,128]{1,0:T(8,128)S(1)} collective-permute-done((f32[8,128]{1,0:T(8,128)S(1)}, f32[8,128]{1,0:T(8,128)S(1)}, u32[]{:S(2)}, u32[]{:S(2)}) %collective-permute-start.1) | collective-permute-done | bytes 4128 | tf_op jit(solution)/shard_map/ppermute | solution.py:361
  43.0 3.5 %collective-permute-start.2 = (f32[8,128]{1,0:T(8,128)S(1)}, f32[8,128]{1,0:T(8,128)S(1)}, u32[]{:S(2)}, u32[]{:S(2)}) collective-permute-start(f32[8,128]{1,0:T(8,128)S(1)} %add.7.docs_ref), channel_id=1, source_target_pairs={{0,2},{1,3},{2,0},{3,1},{4,6},{5,7},{6,4},{7,5},{8,10},{9,11},{10,... | collective-permute-start | bytes 12296 | tf_op jit(solution)/shard_map/ppermute | solution.py:361
  46.4 0.9 %collective-permute-start.12 = (bf16[384,256]{1,0:T(8,128)(2,1)S(1)}, bf16[384,256]{1,0:T(8,128)(2,1)S(1)}, u32[]{:S(2)}, u32[]{:S(2)}) collective-permute-start(bf16[384,256]{1,0:T(8,128)(2,1)S(1)} %get-tuple-element.54), channel_id=1, source_target_pairs={{0,120},{4,124},{8,0},{12,4},{16,8},{20,12},{24,16},{28,20},{32,24... | collective-permute-start | bytes 589832 | tf_op jit(solution)/shard_map/ppermute | solution.py:349
  47.3 0.4 collective-permute-done.2.more_ref
  47.7 5.5 %collective-permute-start.11 = (bf16[384,256]{1,0:T(8,128)(2,1)S(1)}, bf16[384,256]{1,0:T(8,128)(2,1)S(1)}, u32[]{:S(2)}, u32[]{:S(2)}) collective-permute-start(bf16[384,256]{1,0:T(8,128)(2,1)S(1)} %get-tuple-element.53), channel_id=1, source_target_pairs={{0,120},{4,124},{8,0},{12,4},{16,8},{20,12},{24,16},{28,20},{32,24... | collective-permute-start | bytes 589832 | tf_op jit(solution)/shard_map/ppermute | solution.py:349
  53.2 2.2 %q_out.1 = (bf16[192,4096]{1,0:T(8,128)(2,1)}, f32[192,128]{1,0:T(8,128)S(1)}, f32[192,128]{1,0:T(8,128)S(1)}) custom-call(s32[1]{0:T(128)} %bitcast.idx_ref, s32[1,64]{1,0:T(1,128)S(1)} %get-tuple-element.30.st_ref, s32[1,64]{1,0:T(1,128)S(1)} %get-tuple-element.31.ct_ref, f32[8,128]{1,0:T(8,128)S(1)} %add.7.docs_ref, ...), custom_call_target="tpu_custom_call" | custom-call | tf_op jit(solution)/shard_map/q_out/pallas_call | solution.py:462
  55.4 4.2 %collective-permute-done.11.refs_4_ = bf16[384,256]{1,0:T(8,128)(2,1)S(1)} collective-permute-done((bf16[384,256]{1,0:T(8,128)(2,1)S(1)}, bf16[384,256]{1,0:T(8,128)(2,1)S(1)}, u32[]{:S(2)}, u32[]{:S(2)}) %collective-permute-start.11) | collective-permute-done | bytes 196640 | tf_op jit(solution)/shard_map/ppermute | solution.py:349
  59.6 0.2 kv_out.1
  59.8 1.9 %collective-permute-start.14 = (bf16[192,512]{1,0:T(8,128)(2,1)S(1)}, bf16[192,512]{1,0:T(8,128)(2,1)S(1)}, u32[]{:S(2)}, u32[]{:S(2)}) collective-permute-start(bf16[192,512]{1,0:T(8,128)(2,1)S(1)} %get-tuple-element.57), channel_id=1, source_target_pairs={{0,4},{4,0},{8,12},{12,8},{16,20},{20,16},{24,28},{28,24},{32,36},... | collective-permute-start | bytes 589832 | tf_op jit(solution)/shard_map/ppermute | solution.py:358
  61.6 1.1 %collective-permute-done.14 = bf16[192,512]{1,0:T(8,128)(2,1)S(1)} collective-permute-done((bf16[192,512]{1,0:T(8,128)(2,1)S(1)}, bf16[192,512]{1,0:T(8,128)(2,1)S(1)}, u32[]{:S(2)}, u32[]{:S(2)}) %collective-permute-start.14) | collective-permute-done | bytes 196640 | tf_op jit(solution)/shard_map/ppermute | solution.py:358
  62.8 0.8 %maximum_bitcast_fusion = bf16[1,192,1024]{2,1,0:T(8,128)(2,1)} fusion(bf16[192,256]{1,0:T(8,128)(2,1)S(1)} %get-tuple-element.64, bf16[192,256]{1,0:T(8,128)(2,1)S(1)} %get-tuple-element.61, bf16[192,256]{1,0:T(8,128)(2,1)S(1)} %get-tuple-element.65, bf16[192,256]{1,0:T(8,128)(2,1)S(1)} %get-tuple-element.60), kind=kLoop, calls=%fused_computation | loop fusion | flops 1572864 | bytes 786432 | tf_op jit(solution)/shard_map/broadcast_in_dim | solution.py:488
  (14 shorter events, 0.1 us)
Async XLA Ops:
  0.6 3.4 %copy-start = (bf16[1,192,1024]{2,1,0:T(8,128)(2,1)S(1)}, bf16[1,192,1024]{2,1,0:T(8,128)(2,1)}, u32[]{:S(2)}) copy-start(bf16[1,192,1024]{2,1,0:T(8,128)(2,1)} %param.7) | copy-start | bytes 1179652
  0.6 3.5 %copy-start.1 = (f32[1,192]{1,0:T(1,128)S(1)}, f32[1,192]{1,0:T(1,128)}, u32[]{:S(2)}) copy-start(f32[1,192]{1,0:T(1,128)} %lr_ref.1) | copy-start | bytes 2308
  2.6 12.6 %collective-permute-start = (bf16[2,192,2048]{2,1,0:T(8,128)(2,1)S(1)}, bf16[2,192,2048]{2,1,0:T(8,128)(2,1)S(1)}, u32[]{:S(2)}, u32[]{:S(2)}) collective-permute-start(bf16[2,192,2048]{2,1,0:T(8,128)(2,1)S(1)} %get-tuple-element.32), channel_id=1, source_target_pairs={{0,4},{4,0},{8,12},{12,8},{16,20},{20,16},{24,28},{28,24},{32,36},... | collective-permute-start | bytes 4718600 | tf_op jit(solution)/shard_map/ppermute | solution.py:358
  4.1 3.6 %collective-permute-start.3 = (bf16[192,1024]{1,0:T(8,128)(2,1)S(1)}, bf16[192,1024]{1,0:T(8,128)(2,1)S(1)}, u32[]{:S(2)}, u32[]{:S(2)}) collective-permute-start(bf16[192,1024]{1,0:T(8,128)(2,1)S(1)} %bitcast.10), channel_id=1, source_target_pairs={{0,4},{4,0},{8,12},{12,8},{16,20},{20,16},{24,28},{28,24},{32,36},... | collective-permute-start | bytes 1179656 | tf_op jit(solution)/shard_map/ppermute | solution.py:358
  4.2 3.5 %collective-permute-start.4 = (f32[1,192]{1,0:T(1,128)S(1)}, f32[1,192]{1,0:T(1,128)S(1)}, u32[]{:S(2)}, u32[]{:S(2)}) collective-permute-start(f32[1,192]{1,0:T(1,128)S(1)} %copy-done.1), channel_id=1, source_target_pairs={{0,4},{4,0},{8,12},{12,8},{16,20},{20,16},{24,28},{28,24},{32,36},... | collective-permute-start | bytes 2312 | tf_op jit(solution)/shard_map/ppermute | solution.py:358
  8.0 10.2 %collective-permute-start.5 = (bf16[400,256]{1,0:T(8,128)(2,1)S(1)}, bf16[400,256]{1,0:T(8,128)(2,1)S(1)}, u32[]{:S(2)}, u32[]{:S(2)}) collective-permute-start(bf16[400,256]{1,0:T(8,128)(2,1)S(1)} %get-tuple-element.38.own_ref.refs_0_), channel_id=1, source_target_pairs={{0,8},{4,12},{8,16},{12,20},{16,24},{20,28},{24,32},{28,36},{32,40... | collective-permute-start | bytes 614408 | tf_op jit(solution)/shard_map/ppermute | solution.py:349
  9.4 13.2 %collective-permute-start.6 = (bf16[400,256]{1,0:T(8,128)(2,1)S(1)}, bf16[400,256]{1,0:T(8,128)(2,1)S(1)}, u32[]{:S(2)}, u32[]{:S(2)}) collective-permute-start(bf16[400,256]{1,0:T(8,128)(2,1)S(1)} %get-tuple-element.38.own_ref.refs_0_), channel_id=1, source_target_pairs={{0,16},{4,20},{8,24},{12,28},{16,32},{20,36},{24,40},{28,44},{32,4... | collective-permute-start | bytes 614408 | tf_op jit(solution)/shard_map/ppermute | solution.py:355
  11.8 16.7 %collective-permute-start.8 = (bf16[400,256]{1,0:T(8,128)(2,1)S(1)}, bf16[400,256]{1,0:T(8,128)(2,1)S(1)}, u32[]{:S(2)}, u32[]{:S(2)}) collective-permute-start(bf16[400,256]{1,0:T(8,128)(2,1)S(1)} %get-tuple-element.44.own_ref), channel_id=1, source_target_pairs={{0,8},{4,12},{8,16},{12,20},{16,24},{20,28},{24,32},{28,36},{32,40... | collective-permute-start | bytes 614408 | tf_op jit(solution)/shard_map/ppermute | solution.py:349
  12.4 18.9 %collective-permute-start.9 = (bf16[400,256]{1,0:T(8,128)(2,1)S(1)}, bf16[400,256]{1,0:T(8,128)(2,1)S(1)}, u32[]{:S(2)}, u32[]{:S(2)}) collective-permute-start(bf16[400,256]{1,0:T(8,128)(2,1)S(1)} %get-tuple-element.44.own_ref), channel_id=1, source_target_pairs={{0,16},{4,20},{8,24},{12,28},{16,32},{20,36},{24,40},{28,44},{32,4... | collective-permute-start | bytes 614408 | tf_op jit(solution)/shard_map/ppermute | solution.py:355
  37.5 15.6 %collective-permute-start.10 = (bf16[192,2048]{1,0:T(8,128)(2,1)S(1)}, bf16[192,2048]{1,0:T(8,128)(2,1)S(1)}, u32[]{:S(2)}, u32[]{:S(2)}) collective-permute-start(bf16[192,2048]{1,0:T(8,128)(2,1)S(1)} %get-tuple-element.47), channel_id=1, source_target_pairs={{0,4},{4,0},{8,12},{12,8},{16,20},{20,16},{24,28},{28,24},{32,36},... | collective-permute-start | bytes 2359304 | tf_op jit(solution)/shard_map/ppermute | solution.py:358
  38.6 14.6 %collective-permute-start.7 = (bf16[400,256]{1,0:T(8,128)(2,1)S(1)}, bf16[400,256]{1,0:T(8,128)(2,1)S(1)}, u32[]{:S(2)}, u32[]{:S(2)}) collective-permute-start(bf16[400,256]{1,0:T(8,128)(2,1)S(1)} %get-tuple-element.42), channel_id=1, source_target_pairs={{0,112},{4,116},{8,120},{12,124},{16,0},{20,4},{24,8},{28,12},{32,... | collective-permute-start | bytes 614408 | tf_op jit(solution)/shard_map/ppermute | solution.py:349
  40.3 2.6 %collective-permute-start.1 = (f32[8,128]{1,0:T(8,128)S(1)}, f32[8,128]{1,0:T(8,128)S(1)}, u32[]{:S(2)}, u32[]{:S(2)}) collective-permute-start(f32[8,128]{1,0:T(8,128)S(1)} %get-tuple-element.35), channel_id=1, source_target_pairs={{0,1},{1,0},{2,3},{3,2},{4,5},{5,4},{6,7},{7,6},{8,9},{9,8},{10,11... | collective-permute-start | bytes 12296 | tf_op jit(solution)/shard_map/ppermute | solution.py:361
  42.0 17.6 %collective-permute-start.13 = (bf16[400,256]{1,0:T(8,128)(2,1)S(1)}, bf16[400,256]{1,0:T(8,128)(2,1)S(1)}, u32[]{:S(2)}, u32[]{:S(2)}) collective-permute-start(bf16[400,256]{1,0:T(8,128)(2,1)S(1)} %get-tuple-element.55), channel_id=1, source_target_pairs={{16,0},{20,4},{24,8},{28,12},{32,16},{36,20},{40,24},{44,28},{48,3... | collective-permute-start | bytes 614408 | tf_op jit(solution)/shard_map/ppermute | solution.py:355
  43.0 4.7 %collective-permute-start.2 = (f32[8,128]{1,0:T(8,128)S(1)}, f32[8,128]{1,0:T(8,128)S(1)}, u32[]{:S(2)}, u32[]{:S(2)}) collective-permute-start(f32[8,128]{1,0:T(8,128)S(1)} %add.7.docs_ref), channel_id=1, source_target_pairs={{0,2},{1,3},{2,0},{3,1},{4,6},{5,7},{6,4},{7,5},{8,10},{9,11},{10,... | collective-permute-start | bytes 12296 | tf_op jit(solution)/shard_map/ppermute | solution.py:361
  46.4 9.0 %collective-permute-start.12 = (bf16[384,256]{1,0:T(8,128)(2,1)S(1)}, bf16[384,256]{1,0:T(8,128)(2,1)S(1)}, u32[]{:S(2)}, u32[]{:S(2)}) collective-permute-start(bf16[384,256]{1,0:T(8,128)(2,1)S(1)} %get-tuple-element.54), channel_id=1, source_target_pairs={{0,120},{4,124},{8,0},{12,4},{16,8},{20,12},{24,16},{28,20},{32,24... | collective-permute-start | bytes 589832 | tf_op jit(solution)/shard_map/ppermute | solution.py:349
  47.7 11.9 %collective-permute-start.11 = (bf16[384,256]{1,0:T(8,128)(2,1)S(1)}, bf16[384,256]{1,0:T(8,128)(2,1)S(1)}, u32[]{:S(2)}, u32[]{:S(2)}) collective-permute-start(bf16[384,256]{1,0:T(8,128)(2,1)S(1)} %get-tuple-element.53), channel_id=1, source_target_pairs={{0,120},{4,124},{8,0},{12,4},{16,8},{20,12},{24,16},{28,20},{32,24... | collective-permute-start | bytes 589832 | tf_op jit(solution)/shard_map/ppermute | solution.py:349
  59.8 2.9 %collective-permute-start.14 = (bf16[192,512]{1,0:T(8,128)(2,1)S(1)}, bf16[192,512]{1,0:T(8,128)(2,1)S(1)}, u32[]{:S(2)}, u32[]{:S(2)}) collective-permute-start(bf16[192,512]{1,0:T(8,128)(2,1)S(1)} %get-tuple-element.57), channel_id=1, source_target_pairs={{0,4},{4,0},{8,12},{12,8},{16,20},{20,16},{24,28},{28,24},{32,36},... | collective-permute-start | bytes 589832 | tf_op jit(solution)/shard_map/ppermute | solution.py:358

commit v5 on v4

--- a/solution.py
+++ b/solution.py
@@ -284,42 +284,58 @@
     return jnp.sum(jnp.where((pos >= starts) & (pos < ends), coef, 0.0), axis=1, keepdims=True)
 
 
-def query_kernel(seq_len, idx_ref, st_ref, ct_ref, docs_ref, more_ref, *refs):
-    tail_refs, mine_refs, got_ref = refs[0:4], refs[4:6], refs[6]
-    out_ref, scale_ref, other_ref = refs[7:10]
-    index = idx_ref[0]
-    step = pl.program_id(0)
-
-    @pl.when(step == 0)
-    def _():
-        starts = st_ref[...]
-        n = starts.shape[1]
-        sums = jnp.zeros((1, n), F32)
-        for ref in tail_refs:
-            sums = sums + jnp.sum(ref[CHIP:PACK, 0:n].astype(F32), axis=0, keepdims=True)
-        sums = sums + jnp.sum(tail_refs[-1][CHIP:PACK, DH : DH + n].astype(F32), axis=0, keepdims=True)
-        size = jnp.maximum(ct_ref[...], 1).astype(F32)
-        coef = LOSS_SCALE * 2.0 / (1.0 + jnp.exp(-sums / size)) / (size * (docs_ref[0:1, 0:n] + more_ref[0:1, 0:n]))
-        ends = end_row(starts, seq_len)
-        for dst, where in ((scale_ref, index), (other_ref, index // 2 * 2 + 1 - index % 2)):
-            dst[...] = jnp.broadcast_to(row_coefs(starts, ends, coef, where * ROWS), dst.shape)
-
+def query_kernel(idx_ref, scale_ref, *refs):
+    mine_refs, got_ref, out_hbm, done, sems = refs[0:2], *refs[2:6]
     scale = scale_ref[:, 0:1]
     width = GROUP * DH
+    copies = []
     for k in range(2):
         for j in range(CHUNKS):
-
-            @pl.when(step == (index % 2 + k) % 2 * CHUNKS + j)
-            def _():
-                src = got_ref[:, j * width : (j + 1) * width] if k else mine_refs[j][...]
-                out_ref[...] = (src.astype(F32) * scale).astype(BF16)
-
-
-def key_value_kernel(*refs):
-    scale_refs, own_refs, a_refs, b_refs, outs = refs[0:2], refs[2:4], refs[4:6], refs[6:8], refs[8:10]
-    for i in range(2):
+            src = got_ref[:, j * width : (j + 1) * width] if k else mine_refs[j][...]
+            slot = k * CHUNKS + j
+            done[slot] = (src.astype(F32) * scale).astype(BF16)
+            at = pl.multiple_of(((idx_ref[0] + k) % 2 * CHUNKS + j) * width, width)
+            copies.append(pltpu.make_async_copy(done.at[slot], out_hbm.at[:, pl.ds(at, width)], sems.at[slot]))
+            copies[-1].start()
+    for copy in copies:
+        copy.wait()
+
+
+def place_kernel(idx_ref, mine_ref, got_ref, out_hbm, sems):
+    cut = CHUNKS * DH
+    copies = []
+    for k, src in enumerate((mine_ref, got_ref)):
+        for j in range(2):
+            at = pl.multiple_of(j * HK * DH + (idx_ref[0] + k) % 2 * cut, cut)
+            copies.append(
+                pltpu.make_async_copy(
+                    src.at[:, j * cut : (j + 1) * cut], out_hbm.at[:, pl.ds(at, cut)], sems.at[2 * k + j]
+                )
+            )
+            copies[-1].start()
+    for copy in copies:
+        copy.wait()
+
+
+def key_value_kernel(seq_len, idx_ref, st_ref, ct_ref, docs_ref, more_ref, *refs):
+    tail_refs, own_refs, a_refs, b_refs = refs[0:3], refs[3:5], refs[5:7], refs[7:9]
+    outs, scale_ref = refs[9:11], refs[11]
+    index = idx_ref[0]
+    starts = st_ref[...]
+    n = starts.shape[1]
+    sums = jnp.zeros((1, n), F32)
+    for ref in (*tail_refs, b_refs[0]):
+        sums = sums + jnp.sum(ref[CHIP:PACK, 0:n].astype(F32), axis=0, keepdims=True)
+    sums = sums + jnp.sum(b_refs[0][CHIP:PACK, DH : DH + n].astype(F32), axis=0, keepdims=True)
+    size = jnp.maximum(ct_ref[...], 1).astype(F32)
+    docs = docs_ref[0:1, 0:n] + more_ref[0:1, 0:n]
+    coef = LOSS_SCALE * 2.0 / (1.0 + jnp.exp(-sums / size)) / (size * docs)
+    ends = end_row(starts, seq_len)
+    for i, where in enumerate((index, index // 2 * 2 + 1 - index % 2)):
         rows = slice(i * ROWS, (i + 1) * ROWS)
-        scale = scale_refs[i][...]
+        scale = jnp.broadcast_to(row_coefs(starts, ends, coef, where * ROWS), (ROWS, DH))
+        if i == 0:
+            scale_ref[...] = scale
         for j in range(CHUNKS):
             for k in range(2):
                 cols = slice(k * DH, (k + 1) * DH)
@@ -340,7 +356,6 @@
     count = lax.axis_size("ctx")
     seq_len = ROWS * count
     index = lax.axis_index("ctx").astype(jnp.int32)
-    core = index % 2
     where = index.reshape(1)
     smem = pl.BlockSpec(memory_space=pltpu.SMEM)
     vmem = pl.BlockSpec(memory_space=pltpu.VMEM)
@@ -458,33 +473,34 @@
     dq_got = swapped(dq_other[-1])
     docs = docs + more_docs
     more_docs = exchanged(docs, 2)
-    tails = (own[0], back1[0], back2[0], got_b[0])
-    d_query, scale_mine, scale_other = pl.pallas_call(
-        partial(query_kernel, seq_len),
-        grid=(2 * CHUNKS,),
-        out_shape=(
-            jax.ShapeDtypeStruct((ROWS, HQ * DH), BF16),
-            pltpu.VMEM((ROWS, DH), F32),
-            pltpu.VMEM((ROWS, DH), F32),
-        ),
-        in_specs=[smem] + [vmem] * 11,
-        out_specs=(pl.BlockSpec((ROWS, width), lambda i: (0, i)), vmem, vmem),
+    half = pltpu.VMEM((ROWS, 2 * CHUNKS * DH), BF16)
+    operands = (starts, counts, docs, more_docs, own[0], back1[0], back2[0], *d_own, *got_a, *got_b)
+    kv_mine, kv_send, scale = pl.pallas_call(
+        partial(key_value_kernel, seq_len),
+        out_shape=(half, half, pltpu.VMEM((ROWS, DH), F32)),
+        in_specs=[smem] + [vmem] * len(operands),
+        out_specs=(vmem,) * 3,
+        compiler_params=pltpu.CompilerParams(vmem_limit_bytes=8 << 20),
+        name="kv_out",
+    )(where, *[in_vmem(x) for x in operands])
+    kv_got = swapped(kv_send)
+    d_query = pl.pallas_call(
+        query_kernel,
+        out_shape=jax.ShapeDtypeStruct((ROWS, HQ * DH), BF16),
+        in_specs=[smem] + [vmem] * 4,
+        out_specs=hbm,
+        scratch_shapes=[pltpu.VMEM((2 * CHUNKS, ROWS, width), BF16), pltpu.SemaphoreType.DMA((2 * CHUNKS,))],
         compiler_params=pltpu.CompilerParams(vmem_limit_bytes=8 << 20),
         name="q_out",
-    )(where, *[in_vmem(x) for x in (starts, counts, docs, more_docs, *tails, *dq_mine, dq_got)])
-    half = pltpu.VMEM((ROWS, 2 * CHUNKS * DH), BF16)
-    kv_mine, kv_send = pl.pallas_call(
-        key_value_kernel,
-        out_shape=(half, half),
-        in_specs=[vmem] * 8,
-        out_specs=(vmem, vmem),
-        compiler_params=pltpu.CompilerParams(vmem_limit_bytes=4 << 20),
-        name="kv_out",
-    )(*[in_vmem(x) for x in (scale_mine, scale_other, *d_own, *got_a, *got_b)])
-    kv_got = swapped(kv_send)
-    cut = CHUNKS * DH
-    lower, upper = (jnp.where(core == 0, kv_mine, kv_got), jnp.where(core == 0, kv_got, kv_mine))
-    d_key_value = jnp.concatenate([lower[:, :cut], upper[:, :cut], lower[:, cut:], upper[:, cut:]], axis=1)
+    )(where, *[in_vmem(x) for x in (scale, *dq_mine, dq_got)])
+    d_key_value = pl.pallas_call(
+        place_kernel,
+        out_shape=jax.ShapeDtypeStruct((ROWS, 2 * HK * DH), BF16),
+        in_specs=[smem, vmem, vmem],
+        out_specs=hbm,
+        scratch_shapes=[pltpu.SemaphoreType.DMA((4,))],
+        name="place",
+    )(where, in_vmem(kv_mine), in_vmem(kv_got))
     return (d_query[None], d_key_value[None])
 
 

time: 63.7 us -> 67.2 us (1.055)
  waiting for transfers between devices: 17.3 us -> 21.2 us
  other arithmetic: 0.83 us -> 0.01 us
    ppermute x5, waiting for transfers between devices: 6.33 us -> 10.6 us  [moved(): lax.ppermute(value, 'ctx', [(i, (i + steps) % count) for i in range(count)])]
    ppermute x5, starting transfers between devices: 10.1 us -> 7.08 us  [moved(): lax.ppermute(value, 'ctx', [(i, (i + steps) % count) for i in range(count)])]
    ppermute x2, starting transfers between devices: 5.08 us -> 7.46 us  [exchanged(): lax.ppermute(value, 'dp', [(i, i ^ bit) for i in range(lax.axis_size('dp'...]
    broadcast_in_dim x1 -> x0, other arithmetic: 0.79 us -> none  [local(): return (d_query[None], d_key_value[None])]
    pallas_call x2 -> x3, Pallas kernels: 2.41 us -> 2.54 us  [the longest x1 1.46 us: local(): pl.pallas_call(query_kernel, out_shape=jax.ShapeDtypeStruct((ROWS, HQ * D...]
  transfers between devices with their start and end apart: 15 -> 15, of which waited for: 8 -> 8; matrix products, arithmetic and copies ran while one was open for 0% -> 0% of each run, Pallas kernels for 17% -> 15%
where the time goes in v5:
time: 67.2 us; the launch traced here: 67 us
  starting transfers between devices  25.4 us (38%)
  waiting for transfers between devices  21.2 us (32%)
  Pallas kernels  19.5 us (29%)
  between operations  0.92 us (1%)
    pallas_call x2, Pallas kernels, local(): pl.pallas_call(partial(attention_kernel, j), in_specs=[smem] + [vmem] * l...  12.2 us
    ppermute x5, waiting for transfers between devices, moved(): lax.ppermute(value, 'ctx', [(i, (i + steps) % count) for i in range(count)])  10.6 us
    ppermute x2, starting transfers between devices, exchanged(): lax.ppermute(value, 'dp', [(i, i ^ bit) for i in range(lax.axis_size('dp'...  7.46 us
    ppermute x3, waiting for transfers between devices, moved_two_chips(): lax.ppermute(value, 'ctx', pairs + list(zip(senders, receivers[half:] + r...  7.16 us
    ppermute x5, starting transfers between devices, moved(): lax.ppermute(value, 'ctx', [(i, (i + steps) % count) for i in range(count)])  7.08 us
    ppermute x3, starting transfers between devices, moved_two_chips(): lax.ppermute(value, 'ctx', pairs + list(zip(senders, receivers[half:] + r...  5.67 us
    ppermute x5, starting transfers between devices, swapped(): return lax.ppermute(value, 'ctx', [(i, i ^ 1) for i in range(count)])  5.17 us
    ppermute x5, waiting for transfers between devices, swapped(): return lax.ppermute(value, 'ctx', [(i, i ^ 1) for i in range(count)])  2.45 us
  transfers between devices with their start and end apart: 15, of which 8 were waited for; matrix products, arithmetic and copies ran while one was open for 0% of the time, Pallas kernels for 15%

profile of v5, /device:TPU:1, one launch (start us, length us, event | category | flops | bytes accessed | tf_op | source)
XLA Modules:
  0.0 67.0 jit_solution(16176088983110206491)
XLA Ops:
  0.6 0.0 copy-start
  0.6 0.0 copy-start.1
  0.7 1.9 %halves.1 = (bf16[2,192,2048]{2,1,0:T(8,128)(2,1)S(1)}, bf16[384,2048]{1,0:T(8,128)(2,1)S(1)}, bf16[384,2048]{1,0:T(8,128)(2,1)S(1)}) custom-call(s32[1]{0:T(128)} %bitcast.idx_ref, bf16[192,4096]{1,0:T(8,128)(2,1)} %bitcast.6, bf16[192,4096]{1,0:T(8,128)(2,1)} %bitcast.7), custom_call_target="tpu_custom_call" | custom-call | tf_op jit(solution)/shard_map/halves/pallas_call | solution.py:411
  2.6 1.5 %collective-permute-start = (bf16[2,192,2048]{2,1,0:T(8,128)(2,1)S(1)}, bf16[2,192,2048]{2,1,0:T(8,128)(2,1)S(1)}, u32[]{:S(2)}, u32[]{:S(2)}) collective-permute-start(bf16[2,192,2048]{2,1,0:T(8,128)(2,1)S(1)} %get-tuple-element.30), channel_id=1, source_target_pairs={{0,4},{4,0},{8,12},{12,8},{16,20},{20,16},{24,28},{28,24},{32,36},... | collective-permute-start | bytes 4718600 | tf_op jit(solution)/shard_map/ppermute | solution.py:373
  4.1 0.1 collective-permute-start.3
  4.2 0.4 collective-permute-start.4
  4.6 1.7 %early.1 = (bf16[192,1024]{1,0:T(8,128)(2,1)S(1)}, f32[1,192]{1,0:T(1,128)S(1)}, s32[1,64]{1,0:T(1,128)S(1)}, s32[1,64]{1,0:T(1,128)S(1)}) custom-call(bf16[192,1024]{1,0:T(8,128)(2,1)} %bitcast.9, f32[1,192]{1,0:T(1,128)} %lr_ref.1, s32[1,64]{1,0:T(1,128)} %st_ref.1, s32[1,64]{1,0:T(1,128)} %ct_ref.1), custom_call_target="tpu_custom_call" | custom-call | tf_op jit(solution)/shard_map/early/pallas_call | solution.py:383
  6.3 1.4 %collective-permute-done.4.got_lr_ref = f32[1,192]{1,0:T(1,128)S(1)} collective-permute-done((f32[1,192]{1,0:T(1,128)S(1)}, f32[1,192]{1,0:T(1,128)S(1)}, u32[]{:S(2)}, u32[]{:S(2)}) %collective-permute-start.4) | collective-permute-done | bytes 800 | tf_op jit(solution)/shard_map/ppermute | solution.py:373
  7.7 0.3 pack.1
  8.0 1.4 %collective-permute-start.5 = (bf16[400,256]{1,0:T(8,128)(2,1)S(1)}, bf16[400,256]{1,0:T(8,128)(2,1)S(1)}, u32[]{:S(2)}, u32[]{:S(2)}) collective-permute-start(bf16[400,256]{1,0:T(8,128)(2,1)S(1)} %get-tuple-element.36.own_ref.refs_0_), channel_id=1, source_target_pairs={{0,8},{4,12},{8,16},{12,20},{16,24},{20,28},{24,32},{28,36},{32,40... | collective-permute-start | bytes 614408 | tf_op jit(solution)/shard_map/ppermute | solution.py:364
  9.4 2.5 %collective-permute-start.6 = (bf16[400,256]{1,0:T(8,128)(2,1)S(1)}, bf16[400,256]{1,0:T(8,128)(2,1)S(1)}, u32[]{:S(2)}, u32[]{:S(2)}) collective-permute-start(bf16[400,256]{1,0:T(8,128)(2,1)S(1)} %get-tuple-element.36.own_ref.refs_0_), channel_id=1, source_target_pairs={{0,16},{4,20},{8,24},{12,28},{16,32},{20,36},{24,40},{28,44},{32,4... | collective-permute-start | bytes 614408 | tf_op jit(solution)/shard_map/ppermute | solution.py:370
  11.8 0.6 collective-permute-start.7
  12.4 2.7 %collective-permute-start.8 = (bf16[400,256]{1,0:T(8,128)(2,1)S(1)}, bf16[400,256]{1,0:T(8,128)(2,1)S(1)}, u32[]{:S(2)}, u32[]{:S(2)}) collective-permute-start(bf16[400,256]{1,0:T(8,128)(2,1)S(1)} %get-tuple-element.41.own_ref), channel_id=1, source_target_pairs={{0,16},{4,20},{8,24},{12,28},{16,32},{20,36},{24,40},{28,44},{32,4... | collective-permute-start | bytes 614408 | tf_op jit(solution)/shard_map/ppermute | solution.py:370
  15.2 0.8 %join.1 = (s32[10]{0:T(128)S(1)}, f32[8,128]{1,0:T(8,128)S(1)}, bf16[384,2048]{1,0:T(8,128)(2,1)S(1)}, bf16[384,2048]{1,0:T(8,128)(2,1)S(1)}) custom-call(s32[1]{0:T(128)} %bitcast.idx_ref, bf16[2,192,2048]{2,1,0:T(8,128)(2,1)S(1)} %collective-permute-done.got_ref, ...), custom_call_target="tpu_custom_call", output_to_operand_aliasing={{2}: (2, {}), {3}: (3, {})} | custom-call | tf_op jit(solution)/shard_map/join/pallas_call | solution.py:421
  16.0 2.2 %collective-permute-done.5.a_ref.refs_1_ = bf16[400,256]{1,0:T(8,128)(2,1)S(1)} collective-permute-done((bf16[400,256]{1,0:T(8,128)(2,1)S(1)}, bf16[400,256]{1,0:T(8,128)(2,1)S(1)}, u32[]{:S(2)}, u32[]{:S(2)}) %collective-permute-start.5) | collective-permute-done | bytes 204832 | tf_op jit(solution)/shard_map/ppermute | solution.py:364
  18.1 4.4 %collective-permute-done.6.b_ref.refs_2_ = bf16[400,256]{1,0:T(8,128)(2,1)S(1)} collective-permute-done((bf16[400,256]{1,0:T(8,128)(2,1)S(1)}, bf16[400,256]{1,0:T(8,128)(2,1)S(1)}, u32[]{:S(2)}, u32[]{:S(2)}) %collective-permute-start.6) | collective-permute-done | bytes 204832 | tf_op jit(solution)/shard_map/ppermute | solution.py:370
  22.5 6.0 %shard_map.77 = (bf16[192,1024]{1,0:T(8,128)(2,1)S(1)}, bf16[192,2048]{1,0:T(8,128)(2,1)S(1)}, f32[384,256]{1,0:T(8,128)S(1)}, bf16[384,256]{1,0:T(8,128)(2,1)S(1)}, bf16[400,256]{1,0:T(8,128)(2,1)S(1)}) custom-call(s32[10]{0:T(128)S(1)} %get-tuple-element.37.sc_ref, bf16[384,2048]{1,0:T(8,128)(2,1)S(1)} %get-tuple-element.38.q_all, ...), custom_call_target="tpu_custom_call" | custom-call | tf_op jit(solution)/shard_map/pallas_call | solution.py:440
  28.5 2.8 %collective-permute-done.8.b_ref = bf16[400,256]{1,0:T(8,128)(2,1)S(1)} collective-permute-done((bf16[400,256]{1,0:T(8,128)(2,1)S(1)}, bf16[400,256]{1,0:T(8,128)(2,1)S(1)}, u32[]{:S(2)}, u32[]{:S(2)}) %collective-permute-start.8) | collective-permute-done | bytes 204832 | tf_op jit(solution)/shard_map/ppermute | solution.py:370
  31.3 6.2 %shard_map.78 = (bf16[192,1024]{1,0:T(8,128)(2,1)S(1)}, bf16[192,2048]{1,0:T(8,128)(2,1)S(1)}, f32[384,256]{1,0:T(8,128)S(1)}, bf16[384,256]{1,0:T(8,128)(2,1)S(1)}, bf16[400,256]{1,0:T(8,128)(2,1)S(1)}) custom-call(s32[10]{0:T(128)S(1)} %get-tuple-element.37.sc_ref, bf16[384,2048]{1,0:T(8,128)(2,1)S(1)} %get-tuple-element.38.q_all, ...), custom_call_target="tpu_custom_call", output_to_operand_aliasing={{1}: (7, {})} | custom-call | tf_op jit(solution)/shard_map/pallas_call | solution.py:440
  37.5 1.0 %collective-permute-start.13 = (bf16[192,2048]{1,0:T(8,128)(2,1)S(1)}, bf16[192,2048]{1,0:T(8,128)(2,1)S(1)}, u32[]{:S(2)}, u32[]{:S(2)}) collective-permute-start(bf16[192,2048]{1,0:T(8,128)(2,1)S(1)} %get-tuple-element.51), channel_id=1, source_target_pairs={{0,4},{4,0},{8,12},{12,8},{16,20},{20,16},{24,28},{28,24},{32,36},... | collective-permute-start | bytes 2359304 | tf_op jit(solution)/shard_map/ppermute | solution.py:373
  38.6 0.5 collective-permute-start.1
  39.0 0.5 collective-permute-start.12
  39.5 5.1 %collective-permute-start.11 = (bf16[400,256]{1,0:T(8,128)(2,1)S(1)}, bf16[400,256]{1,0:T(8,128)(2,1)S(1)}, u32[]{:S(2)}, u32[]{:S(2)}) collective-permute-start(bf16[400,256]{1,0:T(8,128)(2,1)S(1)} %get-tuple-element.46), channel_id=1, source_target_pairs={{0,112},{4,116},{8,120},{12,124},{16,0},{20,4},{24,8},{28,12},{32,... | collective-permute-start | bytes 614408 | tf_op jit(solution)/shard_map/ppermute | solution.py:364
  44.6 7.0 %collective-permute-start.2 = (f32[8,128]{1,0:T(8,128)S(1)}, f32[8,128]{1,0:T(8,128)S(1)}, u32[]{:S(2)}, u32[]{:S(2)}) collective-permute-start(f32[8,128]{1,0:T(8,128)S(1)} %add.3.docs_ref), channel_id=1, source_target_pairs={{0,2},{1,3},{2,0},{3,1},{4,6},{5,7},{6,4},{7,5},{8,10},{9,11},{10,... | collective-permute-start | bytes 12296 | tf_op jit(solution)/shard_map/ppermute | solution.py:376
  51.6 1.0 %collective-permute-done.2.more_ref = f32[8,128]{1,0:T(8,128)S(1)} collective-permute-done((f32[8,128]{1,0:T(8,128)S(1)}, f32[8,128]{1,0:T(8,128)S(1)}, u32[]{:S(2)}, u32[]{:S(2)}) %collective-permute-start.2) | collective-permute-done | bytes 4128 | tf_op jit(solution)/shard_map/ppermute | solution.py:376
  52.6 4.3 %collective-permute-done.10.refs_6_ = bf16[384,256]{1,0:T(8,128)(2,1)S(1)} collective-permute-done((bf16[384,256]{1,0:T(8,128)(2,1)S(1)}, bf16[384,256]{1,0:T(8,128)(2,1)S(1)}, u32[]{:S(2)}, u32[]{:S(2)}) %collective-permute-start.10) | collective-permute-done | bytes 196640 | tf_op jit(solution)/shard_map/ppermute | solution.py:364
  56.8 4.2 %collective-permute-done.9.refs_5_ = bf16[384,256]{1,0:T(8,128)(2,1)S(1)} collective-permute-done((bf16[384,256]{1,0:T(8,128)(2,1)S(1)}, bf16[384,256]{1,0:T(8,128)(2,1)S(1)}, u32[]{:S(2)}, u32[]{:S(2)}) %collective-permute-start.9) | collective-permute-done | bytes 196640 | tf_op jit(solution)/shard_map/ppermute | solution.py:364
  61.1 0.3 kv_out.1
  61.4 2.1 %collective-permute-start.14 = (bf16[192,512]{1,0:T(8,128)(2,1)S(1)}, bf16[192,512]{1,0:T(8,128)(2,1)S(1)}, u32[]{:S(2)}, u32[]{:S(2)}) collective-permute-start(bf16[192,512]{1,0:T(8,128)(2,1)S(1)} %get-tuple-element.53), channel_id=1, source_target_pairs={{0,4},{4,0},{8,12},{12,8},{16,20},{20,16},{24,28},{28,24},{32,36},... | collective-permute-start | bytes 589832 | tf_op jit(solution)/shard_map/ppermute | solution.py:373
  63.5 1.1 %collective-permute-done.14.got_ref = bf16[192,512]{1,0:T(8,128)(2,1)S(1)} collective-permute-done((bf16[192,512]{1,0:T(8,128)(2,1)S(1)}, bf16[192,512]{1,0:T(8,128)(2,1)S(1)}, u32[]{:S(2)}, u32[]{:S(2)}) %collective-permute-start.14) | collective-permute-done | bytes 196640 | tf_op jit(solution)/shard_map/ppermute | solution.py:373
  64.6 0.8 %place.1 = bf16[192,1024]{1,0:T(8,128)(2,1)} custom-call(s32[1]{0:T(128)} %bitcast.idx_ref, bf16[192,512]{1,0:T(8,128)(2,1)S(1)} %get-tuple-element.52.mine_ref, bf16[192,512]{1,0:T(8,128)(2,1)S(1)} %collective-permute-done.14.got_ref), custom_call_target="tpu_custom_call" | custom-call | tf_op jit(solution)/shard_map/place/pallas_call | solution.py:496
  65.4 1.5 %q_out.1 = bf16[192,4096]{1,0:T(8,128)(2,1)} custom-call(s32[1]{0:T(128)} %bitcast.idx_ref, f32[192,128]{1,0:T(8,128)S(1)} %get-tuple-element.48.scale_ref, bf16[192,1024]{1,0:T(8,128)(2,1)S(1)} %get-tuple-element.49.refs_0_, bf16[192,1024]{1,0:T(8,128)(2,1)S(1)} %get-tuple-element.50.refs_1_, bf16[192,2048]{1,0:T(8,128)(2,1)S(1)} %collective-permute-done.13.refs_2_), custom_call_target="tpu_custom_call" | custom-call | tf_op jit(solution)/shard_map/q_out/pallas_call | solution.py:487
  (12 shorter events, 0.0 us)
Async XLA Ops:
  0.6 3.4 %copy-start = (bf16[1,192,1024]{2,1,0:T(8,128)(2,1)S(1)}, bf16[1,192,1024]{2,1,0:T(8,128)(2,1)}, u32[]{:S(2)}) copy-start(bf16[1,192,1024]{2,1,0:T(8,128)(2,1)} %param.7) | copy-start | bytes 1179652
  0.6 3.5 %copy-start.1 = (f32[1,192]{1,0:T(1,128)S(1)}, f32[1,192]{1,0:T(1,128)}, u32[]{:S(2)}) copy-start(f32[1,192]{1,0:T(1,128)} %lr_ref.1) | copy-start | bytes 2308
  2.6 12.6 %collective-permute-start = (bf16[2,192,2048]{2,1,0:T(8,128)(2,1)S(1)}, bf16[2,192,2048]{2,1,0:T(8,128)(2,1)S(1)}, u32[]{:S(2)}, u32[]{:S(2)}) collective-permute-start(bf16[2,192,2048]{2,1,0:T(8,128)(2,1)S(1)} %get-tuple-element.30), channel_id=1, source_target_pairs={{0,4},{4,0},{8,12},{12,8},{16,20},{20,16},{24,28},{28,24},{32,36},... | collective-permute-start | bytes 4718600 | tf_op jit(solution)/shard_map/ppermute | solution.py:373
  4.1 3.6 %collective-permute-start.3 = (bf16[192,1024]{1,0:T(8,128)(2,1)S(1)}, bf16[192,1024]{1,0:T(8,128)(2,1)S(1)}, u32[]{:S(2)}, u32[]{:S(2)}) collective-permute-start(bf16[192,1024]{1,0:T(8,128)(2,1)S(1)} %bitcast.10), channel_id=1, source_target_pairs={{0,4},{4,0},{8,12},{12,8},{16,20},{20,16},{24,28},{28,24},{32,36},... | collective-permute-start | bytes 1179656 | tf_op jit(solution)/shard_map/ppermute | solution.py:373
  4.2 3.5 %collective-permute-start.4 = (f32[1,192]{1,0:T(1,128)S(1)}, f32[1,192]{1,0:T(1,128)S(1)}, u32[]{:S(2)}, u32[]{:S(2)}) collective-permute-start(f32[1,192]{1,0:T(1,128)S(1)} %copy-done.1), channel_id=1, source_target_pairs={{0,4},{4,0},{8,12},{12,8},{16,20},{20,16},{24,28},{28,24},{32,36},... | collective-permute-start | bytes 2312 | tf_op jit(solution)/shard_map/ppermute | solution.py:373
  8.0 10.2 %collective-permute-start.5 = (bf16[400,256]{1,0:T(8,128)(2,1)S(1)}, bf16[400,256]{1,0:T(8,128)(2,1)S(1)}, u32[]{:S(2)}, u32[]{:S(2)}) collective-permute-start(bf16[400,256]{1,0:T(8,128)(2,1)S(1)} %get-tuple-element.36.own_ref.refs_0_), channel_id=1, source_target_pairs={{0,8},{4,12},{8,16},{12,20},{16,24},{20,28},{24,32},{28,36},{32,40... | collective-permute-start | bytes 614408 | tf_op jit(solution)/shard_map/ppermute | solution.py:364
  9.4 13.2 %collective-permute-start.6 = (bf16[400,256]{1,0:T(8,128)(2,1)S(1)}, bf16[400,256]{1,0:T(8,128)(2,1)S(1)}, u32[]{:S(2)}, u32[]{:S(2)}) collective-permute-start(bf16[400,256]{1,0:T(8,128)(2,1)S(1)} %get-tuple-element.36.own_ref.refs_0_), channel_id=1, source_target_pairs={{0,16},{4,20},{8,24},{12,28},{16,32},{20,36},{24,40},{28,44},{32,4... | collective-permute-start | bytes 614408 | tf_op jit(solution)/shard_map/ppermute | solution.py:370
  11.8 16.7 %collective-permute-start.7 = (bf16[400,256]{1,0:T(8,128)(2,1)S(1)}, bf16[400,256]{1,0:T(8,128)(2,1)S(1)}, u32[]{:S(2)}, u32[]{:S(2)}) collective-permute-start(bf16[400,256]{1,0:T(8,128)(2,1)S(1)} %get-tuple-element.41.own_ref), channel_id=1, source_target_pairs={{0,8},{4,12},{8,16},{12,20},{16,24},{20,28},{24,32},{28,36},{32,40... | collective-permute-start | bytes 614408 | tf_op jit(solution)/shard_map/ppermute | solution.py:364
  12.4 18.9 %collective-permute-start.8 = (bf16[400,256]{1,0:T(8,128)(2,1)S(1)}, bf16[400,256]{1,0:T(8,128)(2,1)S(1)}, u32[]{:S(2)}, u32[]{:S(2)}) collective-permute-start(bf16[400,256]{1,0:T(8,128)(2,1)S(1)} %get-tuple-element.41.own_ref), channel_id=1, source_target_pairs={{0,16},{4,20},{8,24},{12,28},{16,32},{20,36},{24,40},{28,44},{32,4... | collective-permute-start | bytes 614408 | tf_op jit(solution)/shard_map/ppermute | solution.py:370
  37.5 27.9 %collective-permute-start.13 = (bf16[192,2048]{1,0:T(8,128)(2,1)S(1)}, bf16[192,2048]{1,0:T(8,128)(2,1)S(1)}, u32[]{:S(2)}, u32[]{:S(2)}) collective-permute-start(bf16[192,2048]{1,0:T(8,128)(2,1)S(1)} %get-tuple-element.51), channel_id=1, source_target_pairs={{0,4},{4,0},{8,12},{12,8},{16,20},{20,16},{24,28},{28,24},{32,36},... | collective-permute-start | bytes 2359304 | tf_op jit(solution)/shard_map/ppermute | solution.py:373
  38.6 6.0 %collective-permute-start.1 = (f32[8,128]{1,0:T(8,128)S(1)}, f32[8,128]{1,0:T(8,128)S(1)}, u32[]{:S(2)}, u32[]{:S(2)}) collective-permute-start(f32[8,128]{1,0:T(8,128)S(1)} %get-tuple-element.33), channel_id=1, source_target_pairs={{0,1},{1,0},{2,3},{3,2},{4,5},{5,4},{6,7},{7,6},{8,9},{9,8},{10,11... | collective-permute-start | bytes 12296 | tf_op jit(solution)/shard_map/ppermute | solution.py:376
  39.0 22.0 %collective-permute-start.12 = (bf16[400,256]{1,0:T(8,128)(2,1)S(1)}, bf16[400,256]{1,0:T(8,128)(2,1)S(1)}, u32[]{:S(2)}, u32[]{:S(2)}) collective-permute-start(bf16[400,256]{1,0:T(8,128)(2,1)S(1)} %get-tuple-element.47), channel_id=1, source_target_pairs={{16,0},{20,4},{24,8},{28,12},{32,16},{36,20},{40,24},{44,28},{48,3... | collective-permute-start | bytes 614408 | tf_op jit(solution)/shard_map/ppermute | solution.py:370
  39.5 21.5 %collective-permute-start.11 = (bf16[400,256]{1,0:T(8,128)(2,1)S(1)}, bf16[400,256]{1,0:T(8,128)(2,1)S(1)}, u32[]{:S(2)}, u32[]{:S(2)}) collective-permute-start(bf16[400,256]{1,0:T(8,128)(2,1)S(1)} %get-tuple-element.46), channel_id=1, source_target_pairs={{0,112},{4,116},{8,120},{12,124},{16,0},{20,4},{24,8},{28,12},{32,... | collective-permute-start | bytes 614408 | tf_op jit(solution)/shard_map/ppermute | solution.py:364
  44.6 8.0 %collective-permute-start.2 = (f32[8,128]{1,0:T(8,128)S(1)}, f32[8,128]{1,0:T(8,128)S(1)}, u32[]{:S(2)}, u32[]{:S(2)}) collective-permute-start(f32[8,128]{1,0:T(8,128)S(1)} %add.3.docs_ref), channel_id=1, source_target_pairs={{0,2},{1,3},{2,0},{3,1},{4,6},{5,7},{6,4},{7,5},{8,10},{9,11},{10,... | collective-permute-start | bytes 12296 | tf_op jit(solution)/shard_map/ppermute | solution.py:376
  51.6 5.2 %collective-permute-start.10 = (bf16[384,256]{1,0:T(8,128)(2,1)S(1)}, bf16[384,256]{1,0:T(8,128)(2,1)S(1)}, u32[]{:S(2)}, u32[]{:S(2)}) collective-permute-start(bf16[384,256]{1,0:T(8,128)(2,1)S(1)} %get-tuple-element.45), channel_id=1, source_target_pairs={{0,120},{4,124},{8,0},{12,4},{16,8},{20,12},{24,16},{28,20},{32,24... | collective-permute-start | bytes 589832 | tf_op jit(solution)/shard_map/ppermute | solution.py:364
  52.6 8.5 %collective-permute-start.9 = (bf16[384,256]{1,0:T(8,128)(2,1)S(1)}, bf16[384,256]{1,0:T(8,128)(2,1)S(1)}, u32[]{:S(2)}, u32[]{:S(2)}) collective-permute-start(bf16[384,256]{1,0:T(8,128)(2,1)S(1)} %get-tuple-element.44), channel_id=1, source_target_pairs={{0,120},{4,124},{8,0},{12,4},{16,8},{20,12},{24,16},{28,20},{32,24... | collective-permute-start | bytes 589832 | tf_op jit(solution)/shard_map/ppermute | solution.py:364
  61.4 3.2 %collective-permute-start.14 = (bf16[192,512]{1,0:T(8,128)(2,1)S(1)}, bf16[192,512]{1,0:T(8,128)(2,1)S(1)}, u32[]{:S(2)}, u32[]{:S(2)}) collective-permute-start(bf16[192,512]{1,0:T(8,128)(2,1)S(1)} %get-tuple-element.53), channel_id=1, source_target_pairs={{0,4},{4,0},{8,12},{12,8},{16,20},{20,16},{24,28},{28,24},{32,36},... | collective-permute-start | bytes 589832 | tf_op jit(solution)/shard_map/ppermute | solution.py:373

commit v6 on v5

--- a/solution.py
+++ b/solution.py
@@ -82,8 +82,7 @@
     low = rest - mid
     k = lax.broadcasted_iota(jnp.int32, (TAIL, n), 0)
     tail = jnp.where(k == 0, high, jnp.where(k == 1, mid, jnp.where(k == 2, low, 0.0))).astype(BF16)
-    for ref in own_refs:
-        ref[CHIP:PACK, :] = jnp.zeros((TAIL, 2 * DH), BF16)
+    own_refs[0][CHIP:PACK, :] = jnp.zeros((TAIL, 2 * DH), BF16)
     own_refs[0][CHIP:PACK, 0:n] = tail
 
 
@@ -274,8 +273,9 @@
             rows = pl.ds(i * CHIP + at, ROWS)
             dst[lo : lo + ROWS, 0:DH] = (k_acc[rows, :] * SCALE).astype(dst.dtype)
             dst[lo : lo + ROWS, DH : 2 * DH] = v_acc[rows, :].astype(dst.dtype)
-    d_b_ref[CHIP:PACK, 0:DH] = own_ref[CHIP:PACK, 0:DH]
-    d_b_ref[CHIP:PACK, DH : 2 * DH] = a_ref[CHIP:PACK, 0:DH]
+    if chunk == 0:
+        d_b_ref[CHIP:PACK, 0:DH] = own_ref[CHIP:PACK, 0:DH]
+        d_b_ref[CHIP:PACK, DH : 2 * DH] = a_ref[CHIP:PACK, 0:DH]
 
 
 def row_coefs(starts, ends, coef, first):
@@ -394,10 +394,10 @@
         compiler_params=pltpu.CompilerParams(vmem_limit_bytes=4 << 20),
         name="early",
     )(*[in_hbm(x) for x in (key_value[0], log_ratio, doc_starts, answer_counts)])
-    packed = pltpu.VMEM((PACK, 2 * DH), BF16)
+    packed = [pltpu.VMEM((CHIP if j else PACK, 2 * DH), BF16) for j in range(CHUNKS)]
     own = pl.pallas_call(
         partial(pack_kernel, seq_len),
-        out_shape=(packed,) * CHUNKS,
+        out_shape=tuple(packed),
         in_specs=[smem] + [vmem] * 6,
         out_specs=(vmem,) * CHUNKS,
         compiler_params=pltpu.CompilerParams(vmem_limit_bytes=4 << 20),
@@ -459,7 +459,7 @@
                 pltpu.VMEM((ROWS, CHUNKS * width), BF16),
                 pltpu.VMEM((CHIP, 2 * DH), F32),
                 pltpu.VMEM((CHIP, 2 * DH), BF16),
-                pltpu.VMEM((PACK, 2 * DH), BF16),
+                packed[j],
             ],
             compiler_params=pltpu.CompilerParams(vmem_limit_bytes=24 << 20),
         )(scalars, *[in_vmem(x) for x in operands])

time: 67.2 us -> 66.2 us (0.985)
  the two profiles are of different devices: /device:TPU:1 before, /device:TPU:25 now
where the time goes in v6:
time: 66.2 us; the launch traced here: 66 us
  waiting for transfers between devices  27.2 us (41%)
  starting transfers between devices  20.7 us (31%)
  Pallas kernels  17.1 us (26%)
  between operations  0.92 us (1%)
    ppermute x5, waiting for transfers between devices, moved(): lax.ppermute(value, 'ctx', [(i, (i + steps) % count) for i in range(count)])  14 us
    pallas_call x2, Pallas kernels, local(): pl.pallas_call(partial(attention_kernel, j), in_specs=[smem] + [vmem] * l...  9.85 us
    ppermute x3, waiting for transfers between devices, moved_two_chips(): lax.ppermute(value, 'ctx', pairs + list(zip(senders, receivers[half:] + r...  9.8 us
    ppermute x2, starting transfers between devices, exchanged(): lax.ppermute(value, 'dp', [(i, i ^ bit) for i in range(lax.axis_size('dp'...  9.33 us
    ppermute x5, starting transfers between devices, swapped(): return lax.ppermute(value, 'ctx', [(i, i ^ 1) for i in range(count)])  4.75 us
    ppermute x3, starting transfers between devices, moved_two_chips(): lax.ppermute(value, 'ctx', pairs + list(zip(senders, receivers[half:] + r...  3.52 us
    ppermute x5, starting transfers between devices, moved(): lax.ppermute(value, 'ctx', [(i, (i + steps) % count) for i in range(count)])  3.12 us
    ppermute x5, waiting for transfers between devices, swapped(): return lax.ppermute(value, 'ctx', [(i, i ^ 1) for i in range(count)])  2.45 us
  transfers between devices with their start and end apart: 15, of which 9 were waited for; matrix products, arithmetic and copies ran while one was open for 0% of the time, Pallas kernels for 13%

profile of v6, /device:TPU:25, one launch (start us, length us, event | category | flops | bytes accessed | tf_op | source)
XLA Modules:
  0.0 66.0 jit_solution(15853004182363535815)
XLA Ops:
  0.6 0.0 copy-start
  0.6 0.0 copy-start.1
  0.7 1.9 %halves.1 = (bf16[2,192,2048]{2,1,0:T(8,128)(2,1)S(1)}, bf16[384,2048]{1,0:T(8,128)(2,1)S(1)}, bf16[384,2048]{1,0:T(8,128)(2,1)S(1)}) custom-call(s32[1]{0:T(128)} %bitcast.idx_ref, bf16[192,4096]{1,0:T(8,128)(2,1)} %bitcast.6, bf16[192,4096]{1,0:T(8,128)(2,1)} %bitcast.7), custom_call_target="tpu_custom_call" | custom-call | tf_op jit(solution)/shard_map/halves/pallas_call | solution.py:411
  2.6 0.8 %collective-permute-start = (bf16[2,192,2048]{2,1,0:T(8,128)(2,1)S(1)}, bf16[2,192,2048]{2,1,0:T(8,128)(2,1)S(1)}, u32[]{:S(2)}, u32[]{:S(2)}) collective-permute-start(bf16[2,192,2048]{2,1,0:T(8,128)(2,1)S(1)} %get-tuple-element.30), channel_id=1, source_target_pairs={{0,4},{4,0},{8,12},{12,8},{16,20},{20,16},{24,28},{28,24},{32,36},... | collective-permute-start | bytes 4718600 | tf_op jit(solution)/shard_map/ppermute | solution.py:373
  3.4 0.1 collective-permute-start.3
  3.5 0.4 collective-permute-start.4
  3.9 1.7 %early.1 = (bf16[192,1024]{1,0:T(8,128)(2,1)S(1)}, f32[1,192]{1,0:T(1,128)S(1)}, s32[1,64]{1,0:T(1,128)S(1)}, s32[1,64]{1,0:T(1,128)S(1)}) custom-call(bf16[192,1024]{1,0:T(8,128)(2,1)} %bitcast.9, f32[1,192]{1,0:T(1,128)} %lr_ref.1, s32[1,64]{1,0:T(1,128)} %st_ref.1, s32[1,64]{1,0:T(1,128)} %ct_ref.1), custom_call_target="tpu_custom_call" | custom-call | tf_op jit(solution)/shard_map/early/pallas_call | solution.py:383
  5.6 1.4 %collective-permute-done.4.got_lr_ref = f32[1,192]{1,0:T(1,128)S(1)} collective-permute-done((f32[1,192]{1,0:T(1,128)S(1)}, f32[1,192]{1,0:T(1,128)S(1)}, u32[]{:S(2)}, u32[]{:S(2)}) %collective-permute-start.4) | collective-permute-done | bytes 800 | tf_op jit(solution)/shard_map/ppermute | solution.py:373
  7.0 0.3 pack.1
  7.3 1.3 %collective-permute-start.5 = (bf16[400,256]{1,0:T(8,128)(2,1)S(1)}, bf16[400,256]{1,0:T(8,128)(2,1)S(1)}, u32[]{:S(2)}, u32[]{:S(2)}) collective-permute-start(bf16[400,256]{1,0:T(8,128)(2,1)S(1)} %get-tuple-element.36.own_ref.refs_0_), channel_id=1, source_target_pairs={{0,8},{4,12},{8,16},{12,20},{16,24},{20,28},{24,32},{28,36},{32,40... | collective-permute-start | bytes 614408 | tf_op jit(solution)/shard_map/ppermute | solution.py:364
  8.5 2.5 %collective-permute-start.6 = (bf16[400,256]{1,0:T(8,128)(2,1)S(1)}, bf16[400,256]{1,0:T(8,128)(2,1)S(1)}, u32[]{:S(2)}, u32[]{:S(2)}) collective-permute-start(bf16[400,256]{1,0:T(8,128)(2,1)S(1)} %get-tuple-element.36.own_ref.refs_0_), channel_id=1, source_target_pairs={{0,16},{4,20},{8,24},{12,28},{16,32},{20,36},{24,40},{28,44},{32,4... | collective-permute-start | bytes 614408 | tf_op jit(solution)/shard_map/ppermute | solution.py:370
  11.0 1.1 %collective-permute-start.8 = (bf16[384,256]{1,0:T(8,128)(2,1)S(1)}, bf16[384,256]{1,0:T(8,128)(2,1)S(1)}, u32[]{:S(2)}, u32[]{:S(2)}) collective-permute-start(bf16[384,256]{1,0:T(8,128)(2,1)S(1)} %get-tuple-element.41.own_ref), channel_id=1, source_target_pairs={{0,16},{4,20},{8,24},{12,28},{16,32},{20,36},{24,40},{28,44},{32,4... | collective-permute-start | bytes 589832 | tf_op jit(solution)/shard_map/ppermute | solution.py:370
  12.1 0.8 %join.1 = (s32[10]{0:T(128)S(1)}, f32[8,128]{1,0:T(8,128)S(1)}, bf16[384,2048]{1,0:T(8,128)(2,1)S(1)}, bf16[384,2048]{1,0:T(8,128)(2,1)S(1)}) custom-call(s32[1]{0:T(128)} %bitcast.idx_ref, bf16[2,192,2048]{2,1,0:T(8,128)(2,1)S(1)} %collective-permute-done.got_ref, ...), custom_call_target="tpu_custom_call", output_to_operand_aliasing={{2}: (2, {}), {3}: (3, {})} | custom-call | tf_op jit(solution)/shard_map/join/pallas_call | solution.py:421
  12.9 2.8 %collective-permute-done.5.a_ref.refs_1_ = bf16[400,256]{1,0:T(8,128)(2,1)S(1)} collective-permute-done((bf16[400,256]{1,0:T(8,128)(2,1)S(1)}, bf16[400,256]{1,0:T(8,128)(2,1)S(1)}, u32[]{:S(2)}, u32[]{:S(2)}) %collective-permute-start.5) | collective-permute-done | bytes 204832 | tf_op jit(solution)/shard_map/ppermute | solution.py:364
  15.7 4.7 %collective-permute-done.6.b_ref.refs_2_ = bf16[400,256]{1,0:T(8,128)(2,1)S(1)} collective-permute-done((bf16[400,256]{1,0:T(8,128)(2,1)S(1)}, bf16[400,256]{1,0:T(8,128)(2,1)S(1)}, u32[]{:S(2)}, u32[]{:S(2)}) %collective-permute-start.6) | collective-permute-done | bytes 204832 | tf_op jit(solution)/shard_map/ppermute | solution.py:370
  20.4 4.8 %shard_map.77 = (bf16[192,1024]{1,0:T(8,128)(2,1)S(1)}, bf16[192,2048]{1,0:T(8,128)(2,1)S(1)}, f32[384,256]{1,0:T(8,128)S(1)}, bf16[384,256]{1,0:T(8,128)(2,1)S(1)}, bf16[400,256]{1,0:T(8,128)(2,1)S(1)}) custom-call(s32[10]{0:T(128)S(1)} %get-tuple-element.37.sc_ref, bf16[384,2048]{1,0:T(8,128)(2,1)S(1)} %get-tuple-element.38.q_all, ...), custom_call_target="tpu_custom_call" | custom-call | tf_op jit(solution)/shard_map/pallas_call | solution.py:440
  25.2 0.0 collective-permute-done.7.a_ref
  25.2 3.6 %collective-permute-done.8.b_ref = bf16[384,256]{1,0:T(8,128)(2,1)S(1)} collective-permute-done((bf16[384,256]{1,0:T(8,128)(2,1)S(1)}, bf16[384,256]{1,0:T(8,128)(2,1)S(1)}, u32[]{:S(2)}, u32[]{:S(2)}) %collective-permute-start.8) | collective-permute-done | bytes 196640 | tf_op jit(solution)/shard_map/ppermute | solution.py:370
  28.8 5.0 %shard_map.78 = (bf16[192,1024]{1,0:T(8,128)(2,1)S(1)}, bf16[192,2048]{1,0:T(8,128)(2,1)S(1)}, f32[384,256]{1,0:T(8,128)S(1)}, bf16[384,256]{1,0:T(8,128)(2,1)S(1)}, bf16[384,256]{1,0:T(8,128)(2,1)S(1)}) custom-call(s32[10]{0:T(128)S(1)} %get-tuple-element.37.sc_ref, bf16[384,2048]{1,0:T(8,128)(2,1)S(1)} %get-tuple-element.38.q_all, ...), custom_call_target="tpu_custom_call", output_to_operand_aliasing={{1}: (7, {})} | custom-call | tf_op jit(solution)/shard_map/pallas_call | solution.py:440
  33.9 1.3 %collective-permute-start.13 = (bf16[192,2048]{1,0:T(8,128)(2,1)S(1)}, bf16[192,2048]{1,0:T(8,128)(2,1)S(1)}, u32[]{:S(2)}, u32[]{:S(2)}) collective-permute-start(bf16[192,2048]{1,0:T(8,128)(2,1)S(1)} %get-tuple-element.51), channel_id=1, source_target_pairs={{0,4},{4,0},{8,12},{12,8},{16,20},{20,16},{24,28},{28,24},{32,36},... | collective-permute-start | bytes 2359304 | tf_op jit(solution)/shard_map/ppermute | solution.py:373
  35.2 2.8 %collective-permute-start.1 = (f32[8,128]{1,0:T(8,128)S(1)}, f32[8,128]{1,0:T(8,128)S(1)}, u32[]{:S(2)}, u32[]{:S(2)}) collective-permute-start(f32[8,128]{1,0:T(8,128)S(1)} %get-tuple-element.33), channel_id=1, source_target_pairs={{0,1},{1,0},{2,3},{3,2},{4,5},{5,4},{6,7},{7,6},{8,9},{9,8},{10,11... | collective-permute-start | bytes 12296 | tf_op jit(solution)/shard_map/ppermute | solution.py:376
  38.0 1.8 %collective-permute-start.11 = (bf16[400,256]{1,0:T(8,128)(2,1)S(1)}, bf16[400,256]{1,0:T(8,128)(2,1)S(1)}, u32[]{:S(2)}, u32[]{:S(2)}) collective-permute-start(bf16[400,256]{1,0:T(8,128)(2,1)S(1)} %get-tuple-element.46), channel_id=1, source_target_pairs={{0,112},{4,116},{8,120},{12,124},{16,0},{20,4},{24,8},{28,12},{32,... | collective-permute-start | bytes 614408 | tf_op jit(solution)/shard_map/ppermute | solution.py:364
  39.8 6.5 %collective-permute-start.2 = (f32[8,128]{1,0:T(8,128)S(1)}, f32[8,128]{1,0:T(8,128)S(1)}, u32[]{:S(2)}, u32[]{:S(2)}) collective-permute-start(f32[8,128]{1,0:T(8,128)S(1)} %add.3.docs_ref), channel_id=1, source_target_pairs={{0,2},{1,3},{2,0},{3,1},{4,6},{5,7},{6,4},{7,5},{8,10},{9,11},{10,... | collective-permute-start | bytes 12296 | tf_op jit(solution)/shard_map/ppermute | solution.py:376
  46.3 1.0 %collective-permute-done.2.more_ref = f32[8,128]{1,0:T(8,128)S(1)} collective-permute-done((f32[8,128]{1,0:T(8,128)S(1)}, f32[8,128]{1,0:T(8,128)S(1)}, u32[]{:S(2)}, u32[]{:S(2)}) %collective-permute-start.2) | collective-permute-done | bytes 4128 | tf_op jit(solution)/shard_map/ppermute | solution.py:376
  47.3 4.2 %collective-permute-done.10.refs_6_ = bf16[384,256]{1,0:T(8,128)(2,1)S(1)} collective-permute-done((bf16[384,256]{1,0:T(8,128)(2,1)S(1)}, bf16[384,256]{1,0:T(8,128)(2,1)S(1)}, u32[]{:S(2)}, u32[]{:S(2)}) %collective-permute-start.10) | collective-permute-done | bytes 196640 | tf_op jit(solution)/shard_map/ppermute | solution.py:364
  51.6 1.5 %collective-permute-done.12.refs_8_ = bf16[384,256]{1,0:T(8,128)(2,1)S(1)} collective-permute-done((bf16[384,256]{1,0:T(8,128)(2,1)S(1)}, bf16[384,256]{1,0:T(8,128)(2,1)S(1)}, u32[]{:S(2)}, u32[]{:S(2)}) %collective-permute-start.12) | collective-permute-done | bytes 196640 | tf_op jit(solution)/shard_map/ppermute | solution.py:370
  53.1 6.9 %collective-permute-done.9.refs_5_ = bf16[384,256]{1,0:T(8,128)(2,1)S(1)} collective-permute-done((bf16[384,256]{1,0:T(8,128)(2,1)S(1)}, bf16[384,256]{1,0:T(8,128)(2,1)S(1)}, u32[]{:S(2)}, u32[]{:S(2)}) %collective-permute-start.9) | collective-permute-done | bytes 196640 | tf_op jit(solution)/shard_map/ppermute | solution.py:364
  60.0 0.3 kv_out.1
  60.3 2.2 %collective-permute-start.14 = (bf16[192,512]{1,0:T(8,128)(2,1)S(1)}, bf16[192,512]{1,0:T(8,128)(2,1)S(1)}, u32[]{:S(2)}, u32[]{:S(2)}) collective-permute-start(bf16[192,512]{1,0:T(8,128)(2,1)S(1)} %get-tuple-element.53), channel_id=1, source_target_pairs={{0,4},{4,0},{8,12},{12,8},{16,20},{20,16},{24,28},{28,24},{32,36},... | collective-permute-start | bytes 589832 | tf_op jit(solution)/shard_map/ppermute | solution.py:373
  62.5 1.1 %collective-permute-done.14.got_ref = bf16[192,512]{1,0:T(8,128)(2,1)S(1)} collective-permute-done((bf16[192,512]{1,0:T(8,128)(2,1)S(1)}, bf16[192,512]{1,0:T(8,128)(2,1)S(1)}, u32[]{:S(2)}, u32[]{:S(2)}) %collective-permute-start.14) | collective-permute-done | bytes 196640 | tf_op jit(solution)/shard_map/ppermute | solution.py:373
  63.6 0.8 %place.1 = bf16[192,1024]{1,0:T(8,128)(2,1)} custom-call(s32[1]{0:T(128)} %bitcast.idx_ref, bf16[192,512]{1,0:T(8,128)(2,1)S(1)} %get-tuple-element.52.mine_ref, bf16[192,512]{1,0:T(8,128)(2,1)S(1)} %collective-permute-done.14.got_ref), custom_call_target="tpu_custom_call" | custom-call | tf_op jit(solution)/shard_map/place/pallas_call | solution.py:496
  64.3 1.5 %q_out.1 = bf16[192,4096]{1,0:T(8,128)(2,1)} custom-call(s32[1]{0:T(128)} %bitcast.idx_ref, f32[192,128]{1,0:T(8,128)S(1)} %get-tuple-element.48.scale_ref, bf16[192,1024]{1,0:T(8,128)(2,1)S(1)} %get-tuple-element.49.refs_0_, bf16[192,1024]{1,0:T(8,128)(2,1)S(1)} %get-tuple-element.50.refs_1_, bf16[192,2048]{1,0:T(8,128)(2,1)S(1)} %collective-permute-done.13.refs_2_), custom_call_target="tpu_custom_call" | custom-call | tf_op jit(solution)/shard_map/q_out/pallas_call | solution.py:487
  (12 shorter events, 0.0 us)
Async XLA Ops:
  0.6 2.7 %copy-start = (bf16[1,192,1024]{2,1,0:T(8,128)(2,1)S(1)}, bf16[1,192,1024]{2,1,0:T(8,128)(2,1)}, u32[]{:S(2)}) copy-start(bf16[1,192,1024]{2,1,0:T(8,128)(2,1)} %param.7) | copy-start | bytes 1179652
  0.6 2.8 %copy-start.1 = (f32[1,192]{1,0:T(1,128)S(1)}, f32[1,192]{1,0:T(1,128)}, u32[]{:S(2)}) copy-start(f32[1,192]{1,0:T(1,128)} %lr_ref.1) | copy-start | bytes 2308
  2.6 9.5 %collective-permute-start = (bf16[2,192,2048]{2,1,0:T(8,128)(2,1)S(1)}, bf16[2,192,2048]{2,1,0:T(8,128)(2,1)S(1)}, u32[]{:S(2)}, u32[]{:S(2)}) collective-permute-start(bf16[2,192,2048]{2,1,0:T(8,128)(2,1)S(1)} %get-tuple-element.30), channel_id=1, source_target_pairs={{0,4},{4,0},{8,12},{12,8},{16,20},{20,16},{24,28},{28,24},{32,36},... | collective-permute-start | bytes 4718600 | tf_op jit(solution)/shard_map/ppermute | solution.py:373
  3.4 3.6 %collective-permute-start.3 = (bf16[192,1024]{1,0:T(8,128)(2,1)S(1)}, bf16[192,1024]{1,0:T(8,128)(2,1)S(1)}, u32[]{:S(2)}, u32[]{:S(2)}) collective-permute-start(bf16[192,1024]{1,0:T(8,128)(2,1)S(1)} %bitcast.10), channel_id=1, source_target_pairs={{0,4},{4,0},{8,12},{12,8},{16,20},{20,16},{24,28},{28,24},{32,36},... | collective-permute-start | bytes 1179656 | tf_op jit(solution)/shard_map/ppermute | solution.py:373
  3.5 3.5 %collective-permute-start.4 = (f32[1,192]{1,0:T(1,128)S(1)}, f32[1,192]{1,0:T(1,128)S(1)}, u32[]{:S(2)}, u32[]{:S(2)}) collective-permute-start(f32[1,192]{1,0:T(1,128)S(1)} %copy-done.1), channel_id=1, source_target_pairs={{0,4},{4,0},{8,12},{12,8},{16,20},{20,16},{24,28},{28,24},{32,36},... | collective-permute-start | bytes 2312 | tf_op jit(solution)/shard_map/ppermute | solution.py:373
  7.3 8.4 %collective-permute-start.5 = (bf16[400,256]{1,0:T(8,128)(2,1)S(1)}, bf16[400,256]{1,0:T(8,128)(2,1)S(1)}, u32[]{:S(2)}, u32[]{:S(2)}) collective-permute-start(bf16[400,256]{1,0:T(8,128)(2,1)S(1)} %get-tuple-element.36.own_ref.refs_0_), channel_id=1, source_target_pairs={{0,8},{4,12},{8,16},{12,20},{16,24},{20,28},{24,32},{28,36},{32,40... | collective-permute-start | bytes 614408 | tf_op jit(solution)/shard_map/ppermute | solution.py:364
  8.5 11.9 %collective-permute-start.6 = (bf16[400,256]{1,0:T(8,128)(2,1)S(1)}, bf16[400,256]{1,0:T(8,128)(2,1)S(1)}, u32[]{:S(2)}, u32[]{:S(2)}) collective-permute-start(bf16[400,256]{1,0:T(8,128)(2,1)S(1)} %get-tuple-element.36.own_ref.refs_0_), channel_id=1, source_target_pairs={{0,16},{4,20},{8,24},{12,28},{16,32},{20,36},{24,40},{28,44},{32,4... | collective-permute-start | bytes 614408 | tf_op jit(solution)/shard_map/ppermute | solution.py:370
  11.0 14.2 %collective-permute-start.7 = (bf16[384,256]{1,0:T(8,128)(2,1)S(1)}, bf16[384,256]{1,0:T(8,128)(2,1)S(1)}, u32[]{:S(2)}, u32[]{:S(2)}) collective-permute-start(bf16[384,256]{1,0:T(8,128)(2,1)S(1)} %get-tuple-element.41.own_ref), channel_id=1, source_target_pairs={{0,8},{4,12},{8,16},{12,20},{16,24},{20,28},{24,32},{28,36},{32,40... | collective-permute-start | bytes 589832 | tf_op jit(solution)/shard_map/ppermute | solution.py:364
  11.0 17.8 %collective-permute-start.8 = (bf16[384,256]{1,0:T(8,128)(2,1)S(1)}, bf16[384,256]{1,0:T(8,128)(2,1)S(1)}, u32[]{:S(2)}, u32[]{:S(2)}) collective-permute-start(bf16[384,256]{1,0:T(8,128)(2,1)S(1)} %get-tuple-element.41.own_ref), channel_id=1, source_target_pairs={{0,16},{4,20},{8,24},{12,28},{16,32},{20,36},{24,40},{28,44},{32,4... | collective-permute-start | bytes 589832 | tf_op jit(solution)/shard_map/ppermute | solution.py:370
  33.9 30.5 %collective-permute-start.13 = (bf16[192,2048]{1,0:T(8,128)(2,1)S(1)}, bf16[192,2048]{1,0:T(8,128)(2,1)S(1)}, u32[]{:S(2)}, u32[]{:S(2)}) collective-permute-start(bf16[192,2048]{1,0:T(8,128)(2,1)S(1)} %get-tuple-element.51), channel_id=1, source_target_pairs={{0,4},{4,0},{8,12},{12,8},{16,20},{20,16},{24,28},{28,24},{32,36},... | collective-permute-start | bytes 2359304 | tf_op jit(solution)/shard_map/ppermute | solution.py:373
  35.2 4.6 %collective-permute-start.1 = (f32[8,128]{1,0:T(8,128)S(1)}, f32[8,128]{1,0:T(8,128)S(1)}, u32[]{:S(2)}, u32[]{:S(2)}) collective-permute-start(f32[8,128]{1,0:T(8,128)S(1)} %get-tuple-element.33), channel_id=1, source_target_pairs={{0,1},{1,0},{2,3},{3,2},{4,5},{5,4},{6,7},{7,6},{8,9},{9,8},{10,11... | collective-permute-start | bytes 12296 | tf_op jit(solution)/shard_map/ppermute | solution.py:376
  38.0 22.0 %collective-permute-start.11 = (bf16[400,256]{1,0:T(8,128)(2,1)S(1)}, bf16[400,256]{1,0:T(8,128)(2,1)S(1)}, u32[]{:S(2)}, u32[]{:S(2)}) collective-permute-start(bf16[400,256]{1,0:T(8,128)(2,1)S(1)} %get-tuple-element.46), channel_id=1, source_target_pairs={{0,112},{4,116},{8,120},{12,124},{16,0},{20,4},{24,8},{28,12},{32,... | collective-permute-start | bytes 614408 | tf_op jit(solution)/shard_map/ppermute | solution.py:364
  39.8 7.5 %collective-permute-start.2 = (f32[8,128]{1,0:T(8,128)S(1)}, f32[8,128]{1,0:T(8,128)S(1)}, u32[]{:S(2)}, u32[]{:S(2)}) collective-permute-start(f32[8,128]{1,0:T(8,128)S(1)} %add.3.docs_ref), channel_id=1, source_target_pairs={{0,2},{1,3},{2,0},{3,1},{4,6},{5,7},{6,4},{7,5},{8,10},{9,11},{10,... | collective-permute-start | bytes 12296 | tf_op jit(solution)/shard_map/ppermute | solution.py:376
  46.3 5.2 %collective-permute-start.10 = (bf16[384,256]{1,0:T(8,128)(2,1)S(1)}, bf16[384,256]{1,0:T(8,128)(2,1)S(1)}, u32[]{:S(2)}, u32[]{:S(2)}) collective-permute-start(bf16[384,256]{1,0:T(8,128)(2,1)S(1)} %get-tuple-element.45), channel_id=1, source_target_pairs={{0,120},{4,124},{8,0},{12,4},{16,8},{20,12},{24,16},{28,20},{32,24... | collective-permute-start | bytes 589832 | tf_op jit(solution)/shard_map/ppermute | solution.py:364
  46.3 6.7 %collective-permute-start.12 = (bf16[384,256]{1,0:T(8,128)(2,1)S(1)}, bf16[384,256]{1,0:T(8,128)(2,1)S(1)}, u32[]{:S(2)}, u32[]{:S(2)}) collective-permute-start(bf16[384,256]{1,0:T(8,128)(2,1)S(1)} %get-tuple-element.47), channel_id=1, source_target_pairs={{16,0},{20,4},{24,8},{28,12},{32,16},{36,20},{40,24},{44,28},{48,3... | collective-permute-start | bytes 589832 | tf_op jit(solution)/shard_map/ppermute | solution.py:370
  47.3 12.6 %collective-permute-start.9 = (bf16[384,256]{1,0:T(8,128)(2,1)S(1)}, bf16[384,256]{1,0:T(8,128)(2,1)S(1)}, u32[]{:S(2)}, u32[]{:S(2)}) collective-permute-start(bf16[384,256]{1,0:T(8,128)(2,1)S(1)} %get-tuple-element.44), channel_id=1, source_target_pairs={{0,120},{4,124},{8,0},{12,4},{16,8},{20,12},{24,16},{28,20},{32,24... | collective-permute-start | bytes 589832 | tf_op jit(solution)/shard_map/ppermute | solution.py:364
  60.3 3.3 %collective-permute-start.14 = (bf16[192,512]{1,0:T(8,128)(2,1)S(1)}, bf16[192,512]{1,0:T(8,128)(2,1)S(1)}, u32[]{:S(2)}, u32[]{:S(2)}) collective-permute-start(bf16[192,512]{1,0:T(8,128)(2,1)S(1)} %get-tuple-element.53), channel_id=1, source_target_pairs={{0,4},{4,0},{8,12},{12,8},{16,20},{20,16},{24,28},{28,24},{32,36},... | collective-permute-start | bytes 589832 | tf_op jit(solution)/shard_map/ppermute | solution.py:373
